TPU v7x, 128 devices: a whole 4x4x4 slice. The times are simulated.
128 devices in a mesh: gx: 16 (over z, y_lo, core), gy: 8 (over y_hi, x).
Axes of the slice: x: 4, y: 4 (y_hi: 2, y_lo: 2; y = y_hi * 2 + y_lo), z: 4, core: 2. Of those that a mesh axis runs over, the one named last changes fastest.
Arguments:
- water_state: float32 [3, 2048, 4096], P(None, 'gy', 'gx'), may hold values from -0.1 to 1, as said below
- ground: float32 [2048, 4096], P('gy', 'gx'), may hold values from 0 to 0.3
- log_rough: float32 [2048, 4096], P('gy', 'gx'), may hold values from -3.5 to -1.6
- moment: float32 [2048, 4096], P('gy', 'gx'), may hold values from -3 to 3
- second: float32 [2048, 4096], P('gy', 'gx'), may hold values from 0.001 to 1
- wet_tiles: int32 [16, 32], P('gy', 'gx'), may hold values from 0 to 1, as said below
- cotangent: float32 [3, 2048, 4096], P(None, 'gy', 'gx'), may hold values from -2400 to 2400
Outputs:
- new_rough: float32 [2048, 4096], P('gy', 'gx')
- new_moment: float32 [2048, 4096], P('gy', 'gx')
- new_second: float32 [2048, 4096], P('gy', 'gx')
Inputs may be any that keep to these rules, and one draw needn't show every extreme that they name: `water_state`: depths (first field) lie in 0.2 to 1.0, discharges in -0.1 to 0.1. `wet_tiles`: two devices of one gy index whose gx indices differ by half of the gx axis form a pair; a pair holds at most 6 wet tiles together, and in every draw some pair holds exactly 6, one of its devices with all its tiles wet.
All inputs are finite; a program needn't handle non-finite values.
Results may differ from a plain program's by a relative error of at most 0.0003.
Values sent between devices are 32-bit elements; how exact they have to be, the bound alone decides.
No kernel may reach another device: no remote copies, remote signals or barrier semaphores. Data moves between devices by JAX's collectives and lax.ppermute only.
A program may use at most 64 MiB of HBM per device.

v0:
```python
import jax
import jax.numpy as jnp
import numpy as np
from jax import lax
from jax.sharding import PartitionSpec as P

LOAD = 3
STEPS = 2
UPDATES = 20


GRAVITY = 9.81
COURANT = 0.1
GRAVITY_DT = 9.81
SPEED_EPS = 0.0001
BETA_ONE = 0.9
BETA_TWO = 0.999
LEARN_RATE = 0.05
ATAN_SCALE = 1.27


def extended_2(array, sides, width):
    for axis, dim in sides:
        peers, length = (lax.axis_size(axis), array.shape[dim])
        up = [(i, (i + 1) % peers) for i in range(peers - 1)]
        down = [(j, i) for i, j in up]
        last = lax.slice_in_dim(array, length - width, length, axis=dim)
        first = lax.slice_in_dim(array, 0, width, axis=dim)
        before = lax.ppermute(last, axis, up)
        after = lax.ppermute(first, axis, down)
        array = jnp.concatenate([before, array, after], axis=dim)
    return array


def swapped(value, axis, distance):
    mask = 2**distance
    pairs = [(source, source ^ mask) for source in range(lax.axis_size(axis))]
    return lax.ppermute(value, axis, pairs)


def mean_four(field):
    return 0.25 * (field[1:-1, 2:] + field[1:-1, :-2] + field[2:, 1:-1] + field[:-2, 1:-1])


def diff_cols(field):
    return field[:, 2:] - field[:, :-2]


def diff_rows(field):
    return field[2:, :] - field[:-2, :]


def flux_step(padded):
    depth_now, east_flow, south_flow, ground = (padded[0], padded[1], padded[2], padded[3])
    half_step = 0.5 * COURANT
    row_depth, row_east, row_south = (depth_now[1:-1, :], east_flow[1:-1, :], south_flow[1:-1, :])
    col_depth, col_east, col_south = (depth_now[:, 1:-1], east_flow[:, 1:-1], south_flow[:, 1:-1])
    inner_depth = depth_now[1:-1, 1:-1]
    new_depth = mean_four(depth_now) - half_step * (diff_cols(row_east) + diff_rows(col_south))
    new_east = (
        mean_four(east_flow)
        - half_step
        * (
            diff_cols(row_east * row_east / row_depth + 0.5 * GRAVITY * row_depth * row_depth)
            + diff_rows(col_east * col_south / col_depth)
        )
        - half_step * GRAVITY * inner_depth * diff_cols(ground[1:-1, :])
    )
    new_south = (
        mean_four(south_flow)
        - half_step
        * (
            diff_cols(row_east * row_south / row_depth)
            + diff_rows(col_south * col_south / col_depth + 0.5 * GRAVITY * col_depth * col_depth)
        )
        - half_step * GRAVITY * inner_depth * diff_rows(ground[:, 1:-1])
    )
    return jnp.stack([new_depth, new_east, new_south])


def friction(pre_state, log_rough):
    depth_now, east_flow, south_flow = (pre_state[0], pre_state[1], pre_state[2])
    speed = jnp.sqrt(east_flow * east_flow + south_flow * south_flow + SPEED_EPS)
    drag = 1.0 + GRAVITY_DT * jnp.exp(2.0 * log_rough) * speed * jnp.power(depth_now, -7.0 / 3.0)
    return jnp.stack([depth_now, east_flow / drag, south_flow / drag])


def mirror_walls(raw_tile, wall_flag):
    fields, height, width = raw_tile.shape
    col_pos = lax.broadcasted_iota(jnp.int32, (1, 1, width), 2)
    row_pos = lax.broadcasted_iota(jnp.int32, (1, height, 1), 1)
    sign_cols = jnp.array([1.0, -1.0, 1.0, 1.0], raw_tile.dtype)[:, None, None]
    sign_rows = jnp.array([1.0, 1.0, -1.0, 1.0], raw_tile.dtype)[:, None, None]
    west_side = (col_pos == 0) & (wall_flag[0] > 0)
    raw_tile = jnp.where(west_side, sign_cols * raw_tile[:, :, 1:2], raw_tile)
    east_side = (col_pos == width - 1) & (wall_flag[1] > 0)
    raw_tile = jnp.where(east_side, sign_cols * raw_tile[:, :, width - 2 : width - 1], raw_tile)
    north_side = (row_pos == 0) & (wall_flag[2] > 0)
    raw_tile = jnp.where(north_side, sign_rows * raw_tile[:, 1:2, :], raw_tile)
    south_side = (row_pos == height - 1) & (wall_flag[3] > 0)
    raw_tile = jnp.where(south_side, sign_rows * raw_tile[:, height - 2 : height - 1, :], raw_tile)
    return raw_tile


def tile_forward(raw_tile, wall_flag):
    return flux_step(mirror_walls(raw_tile, wall_flag))


def tile_adjoint(raw_tile, wall_flag, cot_tile):
    fields, height, width = raw_tile.shape
    field_pos = lax.broadcasted_iota(jnp.int32, (fields, height, width), 0)
    row_pos = lax.broadcasted_iota(jnp.int32, (fields, height, width), 1)
    col_pos = lax.broadcasted_iota(jnp.int32, (fields, height, width), 2)
    row_edge = (row_pos == 0) | (row_pos == height - 1)
    col_edge = (col_pos == 0) | (col_pos == width - 1)
    inner_mask = (field_pos < 3) & jnp.logical_not(row_edge) & jnp.logical_not(col_edge)
    corner_mask = (field_pos == 0) & row_edge & col_edge

    def extended(inner):
        spread = jnp.pad(inner, ((0, 1), (1, 1), (1, 1)))
        whole = jnp.where(inner_mask, spread, raw_tile)
        fixed = mirror_walls(whole, wall_flag)
        fixed = jnp.where(corner_mask, 1.0, fixed)
        return flux_step(jnp.pad(fixed, ((0, 0), (1, 1), (1, 1)), mode="edge"))

    _, pullback = jax.vjp(extended, raw_tile[:3, 1:-1, 1:-1])
    return pullback(cot_tile)[0]


def with_rims(fields):
    return extended_2(fields, (("gx", 2), ("gy", 1)), 1)


def cut_tiles(padded, tile_rows, tile_cols, tile_side):
    pieces = []
    for row_tile in range(tile_rows):
        for col_tile in range(tile_cols):
            pieces.append(
                padded[
                    :,
                    row_tile * tile_side : (row_tile + 1) * tile_side + 2,
                    col_tile * tile_side : (col_tile + 1) * tile_side + 2,
                ]
            )
    return jnp.stack(pieces)


def join_tiles(tiles, tile_rows, tile_cols):
    fields, tile_side = (tiles.shape[1], tiles.shape[2])
    blocks = tiles.reshape(tile_rows, tile_cols, fields, tile_side, tile_side).transpose(
        2, 0, 3, 1, 4
    )
    return blocks.reshape(fields, tile_rows * tile_side, tile_cols * tile_side)


def wall_flags(tile_rows, tile_cols):
    col_index = lax.axis_index("gx")
    row_index = lax.axis_index("gy")
    col_last = lax.axis_size("gx") - 1
    row_last = lax.axis_size("gy") - 1
    tile_row_of = np.arange(tile_rows * tile_cols) // tile_cols
    tile_col_of = np.arange(tile_rows * tile_cols) % tile_cols
    west_wall = jnp.asarray(tile_col_of == 0) & (col_index == 0)
    east_wall = jnp.asarray(tile_col_of == tile_cols - 1) & (col_index == col_last)
    north_wall = jnp.asarray(tile_row_of == 0) & (row_index == 0)
    south_wall = jnp.asarray(tile_row_of == tile_rows - 1) & (row_index == row_last)
    return jnp.stack([west_wall, east_wall, north_wall, south_wall], 1).astype(jnp.int32)


def share_work(payload, flag_rows, work, order, own_wet, slot_count, partner_bit):
    tile_count = payload.shape[0]
    spare_slots = tile_count - slot_count
    kept_payload = payload[order[:slot_count]]
    kept_flags = flag_rows[order[:slot_count]]
    sent_payload = payload[order[slot_count:]]
    sent_flags = flag_rows[order[slot_count:]]
    came_payload, came_flags = swapped((sent_payload, sent_flags), "gx", partner_bit)
    slot_ids = jnp.arange(slot_count)
    borrow_index = jnp.clip(slot_ids - own_wet, 0, spare_slots - 1)
    owned_slot = slot_ids < own_wet
    work_payload = jnp.where(
        owned_slot[:, None, None, None], kept_payload, came_payload[borrow_index]
    )
    work_flags = jnp.where(owned_slot[:, None], kept_flags, came_flags[borrow_index])
    results = work(work_payload, work_flags)
    results_back = results[jnp.clip(own_wet + jnp.arange(spare_slots), 0, slot_count - 1)]
    returned = swapped(results_back, "gx", partner_bit)
    sent_valid = (jnp.arange(spare_slots) < own_wet - slot_count)[:, None, None, None]
    in_order = jnp.concatenate(
        [
            jnp.where(owned_slot[:, None, None, None], results, 0.0),
            jnp.where(sent_valid, returned, 0.0),
        ],
        0,
    )
    inverse_order = jnp.argsort(order)
    merged = in_order[inverse_order]
    return (merged, work_payload, work_flags)


def on_device(water_state, ground, log_rough, moment, second, wet_tiles, cotangent):
    tile_rows, tile_cols = wet_tiles.shape
    tile_count = tile_rows * tile_cols
    tile_side = water_state.shape[1] // tile_rows
    slot_count = LOAD
    wet_flat = wet_tiles.reshape(tile_count)
    wet_cells = jnp.repeat(jnp.repeat(wet_tiles, tile_side, 0), tile_side, 1) > 0
    order = jnp.argsort(1 - wet_flat, stable=True)
    own_wet = jnp.sum(wet_flat)
    partner_bit = lax.axis_size("gx").bit_length() - 2
    flag_rows = wall_flags(tile_rows, tile_cols)
    ground_padded = with_rims(ground[None])
    forward_many = jax.vmap(tile_forward)
    adjoint_many = jax.vmap(tile_adjoint)
    pre_list = []
    raw_list = []
    kept_list = []
    current = water_state
    for step_index in range(STEPS):
        padded = jnp.concatenate([with_rims(current), ground_padded], 0)
        raw_tiles = cut_tiles(padded, tile_rows, tile_cols, tile_side)
        results, slot_raws, slot_flags = share_work(
            raw_tiles, flag_rows, forward_many, order, own_wet, slot_count, partner_bit
        )
        pre_state = jnp.where(wet_cells[None], join_tiles(results, tile_rows, tile_cols), current)
        pre_list.append(pre_state)
        raw_list.append(raw_tiles)
        kept_list.append(slot_raws)
        current = jnp.where(wet_cells[None], friction(pre_state, log_rough), current)
    cot_now = cotangent
    gradient = jnp.zeros_like(log_rough)
    for step_index in reversed(range(STEPS)):
        masked = jnp.where(wet_cells[None], cot_now, 0.0)
        _, pullback = jax.vjp(friction, pre_list[step_index], log_rough)
        cot_pre, grad_step = pullback(masked)
        gradient = gradient + grad_step
        if step_index > 0:
            cot_tiles = cut_tiles(with_rims(cot_pre), tile_rows, tile_cols, tile_side)
            raw_tiles = raw_list[step_index]
            combined = jnp.concatenate([raw_tiles, cot_tiles], 1)

            def adjoint_work(payload, flags_here):
                return adjoint_many(payload[:, :4], flags_here, payload[:, 4:])

            results, _, _ = share_work(
                combined, flag_rows, adjoint_work, order, own_wet, slot_count, partner_bit
            )
            cot_now = join_tiles(results, tile_rows, tile_cols)
    new_moment = BETA_ONE * moment + (1.0 - BETA_ONE) * gradient
    new_second = BETA_TWO * second + (1.0 - BETA_TWO) * gradient * gradient
    direction = jnp.arctan2(
        new_moment / (1.0 - BETA_ONE**UPDATES), jnp.sqrt(new_second / (1.0 - BETA_TWO**UPDATES))
    )
    new_rough = log_rough - LEARN_RATE * ATAN_SCALE * direction
    return (new_rough, new_moment, new_second)


def solution(mesh):
    in_specs = (
        P(None, "gy", "gx"),
        P("gy", "gx"),
        P("gy", "gx"),
        P("gy", "gx"),
        P("gy", "gx"),
        P("gy", "gx"),
        P(None, "gy", "gx"),
    )
    out_specs = (P("gy", "gx"), P("gy", "gx"), P("gy", "gx"))
    return jax.shard_map(
        on_device, mesh=mesh, in_specs=in_specs, out_specs=out_specs, check_vma=False
    )
```

profile of v0, /device:TPU:46, one launch (start us, length us, event | category | flops | bytes accessed | tf_op | source)
XLA Modules:
  0.0 311.7 jit_solution(17571290110678858355)
XLA Ops:
  2.2 1.9 collective-permute-start.5
  4.1 3.6 %collective-permute-start.6 = (f32[1,256,1]{2,0,1:T(1,128)S(1)}, f32[1,256,1]{2,0,1:T(1,128)S(1)}, u32[]{:S(2)}, u32[]{:S(2)}) collective-permute-start(f32[1,256,1]{2,0,1:T(1,128)S(1)} %get-tuple-element.191), channel_id=1, source_target_pairs={{8,0},{16,8},{24,16},{32,24},{40,32},{48,40},{56,48},{64,56},{72,6... | collective-permute-start | bytes 3080 | tf_op jit(solution)/shard_map/ppermute | solution.py:30
  7.8 1.7 copy.348
  10.6 2.1 collective-permute-start.1
  12.7 3.5 %collective-permute-start.2 = (f32[3,256,1]{2,0,1:T(4,128)S(1)}, f32[3,256,1]{2,0,1:T(4,128)S(1)}, u32[]{:S(2)}, u32[]{:S(2)}) collective-permute-start(f32[3,256,1]{2,0,1:T(4,128)S(1)} %get-tuple-element.181), channel_id=1, source_target_pairs={{8,0},{16,8},{24,16},{32,24},{40,32},{48,40},{56,48},{64,56},{72,6... | collective-permute-start | bytes 9224 | tf_op jit(solution)/shard_map/ppermute | solution.py:30
  20.7 3.0 collective-permute-start
  27.9 4.1 %collective-permute-start.7 = (f32[1,1,258]{2,0,1:T(1,128)S(1)}, f32[1,1,258]{2,0,1:T(1,128)S(1)}, u32[]{:S(2)}, u32[]{:S(2)}) collective-permute-start(f32[1,1,258]{2,0,1:T(1,128)S(1)} %get-tuple-element.188), channel_id=1, source_target_pairs={{0,1},{1,2},{2,3},{3,4},{4,5},{5,6},{6,7},{8,9},{9,10},{10,11},{11... | collective-permute-start | bytes 3104 | tf_op jit(solution)/shard_map/ppermute | solution.py:29
  32.1 1.9 collective-permute-start.8
  34.1 7.5 %collective-permute-start.3 = (f32[3,1,258]{2,0,1:T(4,128)S(1)}, f32[3,1,258]{2,0,1:T(4,128)S(1)}, u32[]{:S(2)}, u32[]{:S(2)}) collective-permute-start(f32[3,1,258]{2,0,1:T(4,128)S(1)} %get-tuple-element.154), channel_id=1, source_target_pairs={{0,1},{1,2},{2,3},{3,4},{4,5},{5,6},{6,7},{8,9},{9,10},{10,11},{11... | collective-permute-start | bytes 9296 | tf_op jit(solution)/shard_map/ppermute | solution.py:29
  41.6 1.9 collective-permute-start.4
  43.8 6.9 %collective-permute-done.4 = f32[3,1,258]{2,0,1:T(4,128)S(1)} collective-permute-done((f32[3,1,258]{2,0,1:T(4,128)S(1)}, f32[3,1,258]{2,0,1:T(4,128)S(1)}, u32[]{:S(2)}, u32[]{:S(2)}) %collective-permute-start.4) | collective-permute-done | bytes 3128 | tf_op jit(solution)/shard_map/ppermute | solution.py:30
  50.8 3.6 %maximum_maximum_fusion.1 = f32[4,258,258]{2,0,1:T(4,128)S(1)} fusion(f32[1,1,258]{2,0,1:T(1,128)S(1)} %collective-permute-done.8, f32[1,256,1]{2,0,1:T(1,128)S(1)} %collective-permute-done.6, f32[1,256,256]{2,0,1:T(1,128)S(1)} %broadcast_in_dim.425, f32[1,256,1]{2,0,1:T(1,128)S(1)} %collective-permute-done.5, f32[1,1,258]{2,0,1:T(1,128)S(1)} %collective-permute-done.7, ...), kind=kLoop, calls=%fused_computation.36 | loop fusion | flops 2396304 | bytes 2130048 | tf_op jit(solution)/shard_map/concatenate | solution.py:220
  58.6 3.1 gather_fusion.1
  61.8 7.4 %collective-permute-done.9 = f32[1,4,130,130]{3,1,2,0:T(4,128)S(1)} collective-permute-done((f32[1,4,130,130]{3,1,2,0:T(4,128)S(1)}, f32[1,4,130,130]{3,1,2,0:T(4,128)S(1)}, u32[]{:S(2)}, u32[]{:S(2)}) %collective-permute-start.9) | collective-permute-done | bytes 270432 | tf_op jit(solution)/shard_map/ppermute | solution.py:38
  70.5 1.6 slice_multiply_fusion.5
  72.1 1.7 copy.354
  76.3 1.7 copy.357
  78.2 2.1 broadcast_select_fusion.9
  80.4 1.9 broadcast_select_fusion.8
  82.4 2.5 broadcast_select_fusion.7
  89.3 3.8 %collective-permute-start.10 = (f32[1,3,128,128]{3,1,2,0:T(4,128)S(1)}, f32[1,3,128,128]{3,1,2,0:T(4,128)S(1)}, u32[]{:S(2)}, u32[]{:S(2)}) collective-permute-start(f32[1,3,128,128]{3,1,2,0:T(4,128)S(1)} %bitcast.282), channel_id=1, source_target_pairs={{0,64},{8,72},{16,80},{24,88},{32,96},{40,104},{48,112},{56,120},{... | collective-permute-start | bytes 589832 | tf_op jit(solution)/shard_map/ppermute | solution.py:38
  94.0 3.8 %collective-permute-done.10 = f32[1,3,128,128]{3,1,2,0:T(4,128)S(1)} collective-permute-done((f32[1,3,128,128]{3,1,2,0:T(4,128)S(1)}, f32[1,3,128,128]{3,1,2,0:T(4,128)S(1)}, u32[]{:S(2)}, u32[]{:S(2)}) %collective-permute-start.10) | collective-permute-done | bytes 196640 | tf_op jit(solution)/shard_map/ppermute | solution.py:38
  101.9 1.9 collective-permute-start.11
  103.8 3.6 %collective-permute-start.12 = (f32[3,256,1]{2,1,0:T(8,128)S(1)}, f32[3,256,1]{2,1,0:T(8,128)S(1)}, u32[]{:S(2)}, u32[]{:S(2)}) collective-permute-start(f32[3,256,1]{2,1,0:T(8,128)S(1)} %get-tuple-element.185), channel_id=1, source_target_pairs={{8,0},{16,8},{24,16},{32,24},{40,32},{48,40},{56,48},{64,56},{72,6... | collective-permute-start | bytes 9224 | tf_op jit(solution)/shard_map/ppermute | solution.py:30
  107.5 3.5 %collective-permute-done.11 = f32[3,256,1]{2,1,0:T(8,128)S(1)} collective-permute-done((f32[3,256,1]{2,1,0:T(8,128)S(1)}, f32[3,256,1]{2,1,0:T(8,128)S(1)}, u32[]{:S(2)}, u32[]{:S(2)}) %collective-permute-start.11) | collective-permute-done | bytes 3104 | tf_op jit(solution)/shard_map/ppermute | solution.py:29
  111.0 3.1 collective-permute-done.12
  114.2 1.9 collective-permute-start.13
  116.1 3.9 %collective-permute-start.14 = (f32[3,1,258]{2,1,0:T(1,128)S(1)}, f32[3,1,258]{2,1,0:T(1,128)S(1)}, u32[]{:S(2)}, u32[]{:S(2)}) collective-permute-start(f32[3,1,258]{2,1,0:T(1,128)S(1)} %get-tuple-element.165), channel_id=1, source_target_pairs={{1,0},{2,1},{3,2},{4,3},{5,4},{6,5},{7,6},{9,8},{10,9},{11,10},{12... | collective-permute-start | bytes 9296 | tf_op jit(solution)/shard_map/ppermute | solution.py:30
  121.3 4.0 %collective-permute-done.14 = f32[3,1,258]{2,1,0:T(1,128)S(1)} collective-permute-done((f32[3,1,258]{2,1,0:T(1,128)S(1)}, f32[3,1,258]{2,1,0:T(1,128)S(1)}, u32[]{:S(2)}, u32[]{:S(2)}) %collective-permute-start.14) | collective-permute-done | bytes 3128 | tf_op jit(solution)/shard_map/ppermute | solution.py:30
  128.3 2.3 collective-permute-start.15
  130.6 3.1 gather_fusion.3
  133.7 11.0 %collective-permute-done.15 = f32[1,4,130,130]{3,1,2,0:T(4,128)S(1)} collective-permute-done((f32[1,4,130,130]{3,1,2,0:T(4,128)S(1)}, f32[1,4,130,130]{3,1,2,0:T(4,128)S(1)}, u32[]{:S(2)}, u32[]{:S(2)}) %collective-permute-start.15) | collective-permute-done | bytes 270432 | tf_op jit(solution)/shard_map/ppermute | solution.py:38
  147.6 1.7 copy.377
  151.8 2.3 copy.380
  155.0 2.1 broadcast_select_fusion.5
  157.2 1.9 broadcast_select_fusion.4
  159.2 2.5 broadcast_select_fusion.3
  166.7 9.3 %collective-permute-done.16 = f32[1,3,128,128]{3,1,2,0:T(4,128)S(1)} collective-permute-done((f32[1,3,128,128]{3,1,2,0:T(4,128)S(1)}, f32[1,3,128,128]{3,1,2,0:T(4,128)S(1)}, u32[]{:S(2)}, u32[]{:S(2)}) %collective-permute-start.16) | collective-permute-done | bytes 196640 | tf_op jit(solution)/shard_map/ppermute | solution.py:38
  182.9 1.9 collective-permute-start.17
  184.8 3.6 %collective-permute-start.18 = (f32[3,256,1]{2,0,1:T(4,128)S(1)}, f32[3,256,1]{2,0,1:T(4,128)S(1)}, u32[]{:S(2)}, u32[]{:S(2)}) collective-permute-start(f32[3,256,1]{2,0,1:T(4,128)S(1)} %get-tuple-element.179), channel_id=1, source_target_pairs={{8,0},{16,8},{24,16},{32,24},{40,32},{48,40},{56,48},{64,56},{72,6... | collective-permute-start | bytes 9224 | tf_op jit(solution)/shard_map/ppermute | solution.py:30
  188.5 8.5 %collective-permute-done.17 = f32[3,256,1]{2,0,1:T(4,128)S(1)} collective-permute-done((f32[3,256,1]{2,0,1:T(4,128)S(1)}, f32[3,256,1]{2,0,1:T(4,128)S(1)}, u32[]{:S(2)}, u32[]{:S(2)}) %collective-permute-start.17) | collective-permute-done | bytes 3104 | tf_op jit(solution)/shard_map/ppermute | solution.py:29
  197.6 2.2 collective-permute-start.19
  199.9 3.7 %collective-permute-start.20 = (f32[3,1,258]{2,0,1:T(4,128)S(1)}, f32[3,1,258]{2,0,1:T(4,128)S(1)}, u32[]{:S(2)}, u32[]{:S(2)}) collective-permute-start(f32[3,1,258]{2,0,1:T(4,128)S(1)} %get-tuple-element.153), channel_id=1, source_target_pairs={{1,0},{2,1},{3,2},{4,3},{5,4},{6,5},{7,6},{9,8},{10,9},{11,10},{12... | collective-permute-start | bytes 9296 | tf_op jit(solution)/shard_map/ppermute | solution.py:30
  203.6 5.4 %collective-permute-done.20 = f32[3,1,258]{2,0,1:T(4,128)S(1)} collective-permute-done((f32[3,1,258]{2,0,1:T(4,128)S(1)}, f32[3,1,258]{2,0,1:T(4,128)S(1)}, u32[]{:S(2)}, u32[]{:S(2)}) %collective-permute-start.20) | collective-permute-done | bytes 3128 | tf_op jit(solution)/shard_map/ppermute | solution.py:30
  211.6 1.9 copy.394
  215.7 3.1 copy.393
  218.8 3.0 gather_fusion.5
  221.7 17.4 %collective-permute-done.21 = f32[1,7,130,130]{3,0,2,1:T(1,128)} collective-permute-done((f32[1,7,130,130]{3,0,2,1:T(1,128)}, f32[1,7,130,130]{3,0,2,1:T(1,128)}, u32[]{:S(2)}, u32[]{:S(2)}) %collective-permute-start.21) | collective-permute-done | bytes 473232 | tf_op jit(solution)/shard_map/ppermute | solution.py:38
  240.4 2.1 copy_select_fusion
  243.0 1.9 multiply_bitcast_fusion.3
  245.9 1.7 slice_multiply_fusion.1
  247.6 1.7 copy.397
  251.6 2.3 copy.400
  256.3 1.6 broadcast_select_fusion
  258.0 1.9 select_select_fusion
  261.2 2.9 pad_maximum_fusion.1
  264.5 2.7 fusion.98
  276.5 1.9 fusion
  278.5 3.0 select_reduce_fusion.2
  281.6 1.7 fusion.6
  284.5 1.7 copy.428
  289.1 1.7 copy.434
  295.3 9.8 %collective-permute-done.22 = f32[1,3,128,128]{3,1,2,0:T(4,128)S(1)} collective-permute-done((f32[1,3,128,128]{3,1,2,0:T(4,128)S(1)}, f32[1,3,128,128]{3,1,2,0:T(4,128)S(1)}, u32[]{:S(2)}, u32[]{:S(2)}) %collective-permute-start.22) | collective-permute-done | bytes 196640 | tf_op jit(solution)/shard_map/ppermute | solution.py:38
  308.5 3.0 multiply_subtract_fusion
  (304 shorter events, 83.8 us)
Async XLA Ops:
  1.8 14.4 %copy-start.51 = (s32[2,2]{1,0:T(2,128)S(1)}, s32[2,2]{1,0:T(2,128)}, u32[]{:S(2)}) copy-start(s32[2,2]{1,0:T(2,128)} %param.22) | copy-start | bytes 52
  1.8 17.7 %copy-start.56 = (pred[4]{0:T(512)(128)(4,1)S(1)}, pred[4]{0:T(512)(128)(4,1)}, u32[]{:S(2)}) copy-start(pred[4]{0:T(512)(128)(4,1)} %constant.139.clone) | copy-start | bytes 16
  1.8 17.9 %copy-start.55 = (pred[4]{0:T(512)(128)(4,1)S(1)}, pred[4]{0:T(512)(128)(4,1)}, u32[]{:S(2)}) copy-start(pred[4]{0:T(512)(128)(4,1)} %constant.140.clone) | copy-start | bytes 16
  1.8 18.0 %copy-start.54 = (pred[4]{0:T(512)(128)(4,1)S(1)}, pred[4]{0:T(512)(128)(4,1)}, u32[]{:S(2)}) copy-start(pred[4]{0:T(512)(128)(4,1)} %constant.141.clone) | copy-start | bytes 16
  1.8 18.1 %copy-start.53 = (pred[4]{0:T(512)(128)(4,1)S(1)}, pred[4]{0:T(512)(128)(4,1)}, u32[]{:S(2)}) copy-start(pred[4]{0:T(512)(128)(4,1)} %constant.142.clone) | copy-start | bytes 16
  2.2 25.7 %collective-permute-start.5 = (f32[1,256,1]{2,0,1:T(1,128)S(1)}, f32[1,256,1]{2,0,1:T(1,128)S(1)}, u32[]{:S(2)}, u32[]{:S(2)}) collective-permute-start(f32[1,256,1]{2,0,1:T(1,128)S(1)} %get-tuple-element.190), channel_id=1, source_target_pairs={{0,8},{8,16},{16,24},{24,32},{32,40},{40,48},{48,56},{56,64},{64,7... | collective-permute-start | bytes 3080 | tf_op jit(solution)/shard_map/ppermute | solution.py:29
  4.1 23.7 %collective-permute-start.6 = (f32[1,256,1]{2,0,1:T(1,128)S(1)}, f32[1,256,1]{2,0,1:T(1,128)S(1)}, u32[]{:S(2)}, u32[]{:S(2)}) collective-permute-start(f32[1,256,1]{2,0,1:T(1,128)S(1)} %get-tuple-element.191), channel_id=1, source_target_pairs={{8,0},{16,8},{24,16},{32,24},{40,32},{48,40},{56,48},{64,56},{72,6... | collective-permute-start | bytes 3080 | tf_op jit(solution)/shard_map/ppermute | solution.py:30
  10.6 23.4 %collective-permute-start.1 = (f32[3,256,1]{2,0,1:T(4,128)}, f32[3,256,1]{2,0,1:T(4,128)S(1)}, u32[]{:S(2)}, u32[]{:S(2)}) collective-permute-start(f32[3,256,1]{2,0,1:T(4,128)} %get-tuple-element.180), channel_id=1, source_target_pairs={{0,8},{8,16},{16,24},{24,32},{32,40},{40,48},{48,56},{56,64},{64,7... | collective-permute-start | bytes 9224 | tf_op jit(solution)/shard_map/ppermute | solution.py:29
  12.7 21.3 %collective-permute-start.2 = (f32[3,256,1]{2,0,1:T(4,128)S(1)}, f32[3,256,1]{2,0,1:T(4,128)S(1)}, u32[]{:S(2)}, u32[]{:S(2)}) collective-permute-start(f32[3,256,1]{2,0,1:T(4,128)S(1)} %get-tuple-element.181), channel_id=1, source_target_pairs={{8,0},{16,8},{24,16},{32,24},{40,32},{48,40},{56,48},{64,56},{72,6... | collective-permute-start | bytes 9224 | tf_op jit(solution)/shard_map/ppermute | solution.py:30
  20.7 7.0 %collective-permute-start = (s32[1,4]{1,0:T(1,128)S(1)}, s32[1,4]{1,0:T(1,128)S(1)}, u32[]{:S(2)}, u32[]{:S(2)}) collective-permute-start(s32[1,4]{1,0:T(1,128)S(1)} %constant_dynamic-slice_fusion.6), channel_id=1, source_target_pairs={{0,64},{8,72},{16,80},{24,88},{32,96},{40,104},{48,112},{56,120},{... | collective-permute-start | bytes 56 | tf_op jit(solution)/shard_map/ppermute | solution.py:38
  25.0 140.4 %copy-start.34 = (pred[3]{0:T(512)(128)(4,1)}, pred[3]{0:T(512)(128)(4,1)S(1)}, u32[]{:S(2)}) copy-start(pred[3]{0:T(512)(128)(4,1)S(1)} %iota_compare_fusion.4) | copy-start | bytes 13
  25.7 104.9 %copy-start.43 = (s32[1024]{0:T(1024)}, s32[1024]{0:T(1024)S(1)}, u32[]{:S(2)}) copy-start(s32[1024]{0:T(1024)S(1)} %pad_clamp_fusion.1) | copy-start | bytes 12292
  27.8 26.5 %copy-start.25 = (f32[1,256,1]{2,0,1:T(1,128)}, f32[1,256,1]{2,0,1:T(1,128)S(1)}, u32[]{:S(2)}) copy-start(f32[1,256,1]{2,0,1:T(1,128)S(1)} %collective-permute-done.5) | copy-start | bytes 3076
  27.9 26.5 %copy-start.27 = (f32[1,256,1]{2,0,1:T(1,128)}, f32[1,256,1]{2,0,1:T(1,128)S(1)}, u32[]{:S(2)}) copy-start(f32[1,256,1]{2,0,1:T(1,128)S(1)} %collective-permute-done.6) | copy-start | bytes 3076
  27.9 15.8 %collective-permute-start.7 = (f32[1,1,258]{2,0,1:T(1,128)S(1)}, f32[1,1,258]{2,0,1:T(1,128)S(1)}, u32[]{:S(2)}, u32[]{:S(2)}) collective-permute-start(f32[1,1,258]{2,0,1:T(1,128)S(1)} %get-tuple-element.188), channel_id=1, source_target_pairs={{0,1},{1,2},{2,3},{3,4},{4,5},{5,6},{6,7},{8,9},{9,10},{10,11},{11... | collective-permute-start | bytes 3104 | tf_op jit(solution)/shard_map/ppermute | solution.py:29
  32.1 11.7 %collective-permute-start.8 = (f32[1,1,258]{2,0,1:T(1,128)S(1)}, f32[1,1,258]{2,0,1:T(1,128)S(1)}, u32[]{:S(2)}, u32[]{:S(2)}) collective-permute-start(f32[1,1,258]{2,0,1:T(1,128)S(1)} %get-tuple-element.189), channel_id=1, source_target_pairs={{1,0},{2,1},{3,2},{4,3},{5,4},{6,5},{7,6},{9,8},{10,9},{11,10},{12... | collective-permute-start | bytes 3104 | tf_op jit(solution)/shard_map/ppermute | solution.py:30
  34.1 9.7 %collective-permute-start.3 = (f32[3,1,258]{2,0,1:T(4,128)S(1)}, f32[3,1,258]{2,0,1:T(4,128)S(1)}, u32[]{:S(2)}, u32[]{:S(2)}) collective-permute-start(f32[3,1,258]{2,0,1:T(4,128)S(1)} %get-tuple-element.154), channel_id=1, source_target_pairs={{0,1},{1,2},{2,3},{3,4},{4,5},{5,6},{6,7},{8,9},{9,10},{10,11},{11... | collective-permute-start | bytes 9296 | tf_op jit(solution)/shard_map/ppermute | solution.py:29
  41.6 9.1 %collective-permute-start.4 = (f32[3,1,258]{2,0,1:T(4,128)S(1)}, f32[3,1,258]{2,0,1:T(4,128)S(1)}, u32[]{:S(2)}, u32[]{:S(2)}) collective-permute-start(f32[3,1,258]{2,0,1:T(4,128)S(1)} %get-tuple-element.155), channel_id=1, source_target_pairs={{1,0},{2,1},{3,2},{4,3},{5,4},{6,5},{7,6},{9,8},{10,9},{11,10},{12... | collective-permute-start | bytes 9296 | tf_op jit(solution)/shard_map/ppermute | solution.py:30
  43.8 11.0 %copy-start.45 = (f32[1,1,258]{2,0,1:T(1,128)}, f32[1,1,258]{2,0,1:T(1,128)S(1)}, u32[]{:S(2)}) copy-start(f32[1,1,258]{2,0,1:T(1,128)S(1)} %collective-permute-done.7) | copy-start | bytes 3100
  43.8 11.0 %copy-start.47 = (f32[1,1,258]{2,0,1:T(1,128)}, f32[1,1,258]{2,0,1:T(1,128)S(1)}, u32[]{:S(2)}) copy-start(f32[1,1,258]{2,0,1:T(1,128)S(1)} %collective-permute-done.8) | copy-start | bytes 3100
  56.7 12.5 %collective-permute-start.9 = (f32[1,4,130,130]{3,1,2,0:T(4,128)S(1)}, f32[1,4,130,130]{3,1,2,0:T(4,128)S(1)}, u32[]{:S(2)}, u32[]{:S(2)}) collective-permute-start(f32[1,4,130,130]{3,1,2,0:T(4,128)S(1)} %constant_dynamic-slice_fusion.5), channel_id=1, source_target_pairs={{0,64},{8,72},{16,80},{24,88},{32,96},{40,104},{48,112},{56,120},{... | collective-permute-start | bytes 811208 | tf_op jit(solution)/shard_map/ppermute | solution.py:38
  58.3 100.9 %copy-start.29 = (pred[3,130]{0,1:T(8,128)(4,1)}, pred[3,130]{0,1:T(8,128)(4,1)S(1)}, u32[]{:S(2)}) copy-start(pred[3,130]{0,1:T(8,128)(4,1)S(1)} %get-tuple-element.196) | copy-start | bytes 1174
  58.5 100.7 %copy-start.31 = (pred[3,130]{0,1:T(8,128)(4,1)}, pred[3,130]{0,1:T(8,128)(4,1)S(1)}, u32[]{:S(2)}) copy-start(pred[3,130]{0,1:T(8,128)(4,1)S(1)} %get-tuple-element.198) | copy-start | bytes 1174
  78.2 2.1 copy-start.40
  88.6 4.5 %copy-start.57 = (s32[4]{0:T(128)S(1)}, s32[4]{0:T(128)}, u32[]{:S(2)}) copy-start(s32[4]{0:T(128)} %get-tuple-element.6) | copy-start | bytes 52
  88.6 5.1 %copy-start.52 = (pred[1,2,2,128]{3,2,1,0:T(4,128)(4,1)S(1)}, pred[1,2,2,128]{3,2,1,0:T(4,128)(4,1)}, u32[]{:S(2)}) copy-start(pred[1,2,2,128]{3,2,1,0:T(4,128)(4,1)} %broadcast_bitcast_fusion) | copy-start | bytes 1540
  89.3 8.5 %collective-permute-start.10 = (f32[1,3,128,128]{3,1,2,0:T(4,128)S(1)}, f32[1,3,128,128]{3,1,2,0:T(4,128)S(1)}, u32[]{:S(2)}, u32[]{:S(2)}) collective-permute-start(f32[1,3,128,128]{3,1,2,0:T(4,128)S(1)} %bitcast.282), channel_id=1, source_target_pairs={{0,64},{8,72},{16,80},{24,88},{32,96},{40,104},{48,112},{56,120},{... | collective-permute-start | bytes 589832 | tf_op jit(solution)/shard_map/ppermute | solution.py:38
  94.0 7.2 %copy-start.22 = (pred[256,256]{1,0:T(8,128)(4,1)}, pred[256,256]{1,0:T(8,128)(4,1)S(1)}, u32[]{:S(2)}) copy-start(pred[256,256]{1,0:T(8,128)(4,1)S(1)} %copy.341) | copy-start | bytes 196612
  94.0 4.6 %copy-start.44 = (s32[1024]{0:T(1024)}, s32[1024]{0:T(1024)S(1)}, u32[]{:S(2)}) copy-start(s32[1024]{0:T(1024)S(1)} %pad_clamp_fusion) | copy-start | bytes 12292
  98.6 1.9 copy-start.1
  101.2 13.0 %copy-start.10 = (f32[1,256,256]{2,1,0:T(8,128)}, f32[1,256,256]{2,1,0:T(8,128)S(1)}, u32[]{:S(2)}) copy-start(f32[1,256,256]{2,1,0:T(8,128)S(1)} %divide_bitcast_fusion) | copy-start | bytes 786436
  101.6 18.4 %copy-start.26 = (f32[1,256,1]{2,0,1:T(1,128)S(1)}, f32[1,256,1]{2,0,1:T(1,128)}, u32[]{:S(2)}) copy-start(f32[1,256,1]{2,0,1:T(1,128)} %copy-done.25) | copy-start | bytes 3076
  101.6 18.4 %copy-start.28 = (f32[1,256,1]{2,0,1:T(1,128)S(1)}, f32[1,256,1]{2,0,1:T(1,128)}, u32[]{:S(2)}) copy-start(f32[1,256,1]{2,0,1:T(1,128)} %copy-done.27) | copy-start | bytes 3076
  101.6 18.4 %copy-start.46 = (f32[1,1,258]{2,0,1:T(1,128)S(1)}, f32[1,1,258]{2,0,1:T(1,128)}, u32[]{:S(2)}) copy-start(f32[1,1,258]{2,0,1:T(1,128)} %copy-done.45) | copy-start | bytes 3100
  101.6 18.4 %copy-start.48 = (f32[1,1,258]{2,0,1:T(1,128)S(1)}, f32[1,1,258]{2,0,1:T(1,128)}, u32[]{:S(2)}) copy-start(f32[1,1,258]{2,0,1:T(1,128)} %copy-done.47) | copy-start | bytes 3100
  101.9 9.1 %collective-permute-start.11 = (f32[3,256,1]{2,1,0:T(8,128)S(1)}, f32[3,256,1]{2,1,0:T(8,128)S(1)}, u32[]{:S(2)}, u32[]{:S(2)}) collective-permute-start(f32[3,256,1]{2,1,0:T(8,128)S(1)} %get-tuple-element.184), channel_id=1, source_target_pairs={{0,8},{8,16},{16,24},{24,32},{32,40},{40,48},{48,56},{56,64},{64,7... | collective-permute-start | bytes 9224 | tf_op jit(solution)/shard_map/ppermute | solution.py:29
  103.8 10.2 %collective-permute-start.12 = (f32[3,256,1]{2,1,0:T(8,128)S(1)}, f32[3,256,1]{2,1,0:T(8,128)S(1)}, u32[]{:S(2)}, u32[]{:S(2)}) collective-permute-start(f32[3,256,1]{2,1,0:T(8,128)S(1)} %get-tuple-element.185), channel_id=1, source_target_pairs={{8,0},{16,8},{24,16},{32,24},{40,32},{48,40},{56,48},{64,56},{72,6... | collective-permute-start | bytes 9224 | tf_op jit(solution)/shard_map/ppermute | solution.py:30
  114.2 7.1 %collective-permute-start.13 = (f32[3,1,258]{2,1,0:T(1,128)S(1)}, f32[3,1,258]{2,1,0:T(1,128)S(1)}, u32[]{:S(2)}, u32[]{:S(2)}) collective-permute-start(f32[3,1,258]{2,1,0:T(1,128)S(1)} %get-tuple-element.164), channel_id=1, source_target_pairs={{0,1},{1,2},{2,3},{3,4},{4,5},{5,6},{6,7},{8,9},{9,10},{10,11},{11... | collective-permute-start | bytes 9296 | tf_op jit(solution)/shard_map/ppermute | solution.py:29
  116.1 9.1 %collective-permute-start.14 = (f32[3,1,258]{2,1,0:T(1,128)S(1)}, f32[3,1,258]{2,1,0:T(1,128)S(1)}, u32[]{:S(2)}, u32[]{:S(2)}) collective-permute-start(f32[3,1,258]{2,1,0:T(1,128)S(1)} %get-tuple-element.165), channel_id=1, source_target_pairs={{1,0},{2,1},{3,2},{4,3},{5,4},{6,5},{7,6},{9,8},{10,9},{11,10},{12... | collective-permute-start | bytes 9296 | tf_op jit(solution)/shard_map/ppermute | solution.py:30
  128.3 16.4 %collective-permute-start.15 = (f32[1,4,130,130]{3,1,2,0:T(4,128)S(1)}, f32[1,4,130,130]{3,1,2,0:T(4,128)S(1)}, u32[]{:S(2)}, u32[]{:S(2)}) collective-permute-start(f32[1,4,130,130]{3,1,2,0:T(4,128)S(1)} %constant_dynamic-slice_fusion.3), channel_id=1, source_target_pairs={{0,64},{8,72},{16,80},{24,88},{32,96},{40,104},{48,112},{56,120},{... | collective-permute-start | bytes 811208 | tf_op jit(solution)/shard_map/ppermute | solution.py:38
  155.0 2.1 copy-start.41
  166.1 9.9 %collective-permute-start.16 = (f32[1,3,128,128]{3,1,2,0:T(4,128)S(1)}, f32[1,3,128,128]{3,1,2,0:T(4,128)S(1)}, u32[]{:S(2)}, u32[]{:S(2)}) collective-permute-start(f32[1,3,128,128]{3,1,2,0:T(4,128)S(1)} %bitcast.283), channel_id=1, source_target_pairs={{0,64},{8,72},{16,80},{24,88},{32,96},{40,104},{48,112},{56,120},{... | collective-permute-start | bytes 589832 | tf_op jit(solution)/shard_map/ppermute | solution.py:38
  176.8 2.1 copy-start.23
  178.9 1.6 copy-start.9
  182.9 14.1 %collective-permute-start.17 = (f32[3,256,1]{2,0,1:T(4,128)S(1)}, f32[3,256,1]{2,0,1:T(4,128)S(1)}, u32[]{:S(2)}, u32[]{:S(2)}) collective-permute-start(f32[3,256,1]{2,0,1:T(4,128)S(1)} %get-tuple-element.178), channel_id=1, source_target_pairs={{0,8},{8,16},{16,24},{24,32},{32,40},{40,48},{48,56},{56,64},{64,7... | collective-permute-start | bytes 9224 | tf_op jit(solution)/shard_map/ppermute | solution.py:29
  184.8 12.8 %collective-permute-start.18 = (f32[3,256,1]{2,0,1:T(4,128)S(1)}, f32[3,256,1]{2,0,1:T(4,128)S(1)}, u32[]{:S(2)}, u32[]{:S(2)}) collective-permute-start(f32[3,256,1]{2,0,1:T(4,128)S(1)} %get-tuple-element.179), channel_id=1, source_target_pairs={{8,0},{16,8},{24,16},{32,24},{40,32},{48,40},{56,48},{64,56},{72,6... | collective-permute-start | bytes 9224 | tf_op jit(solution)/shard_map/ppermute | solution.py:30
  197.6 12.8 %copy-start.3 = (f32[4,4,130,130]{3,1,2,0:T(4,128)S(1)}, f32[4,4,130,130]{3,1,2,0:T(4,128)}, u32[]{:S(2)}) copy-start(f32[4,4,130,130]{3,1,2,0:T(4,128)} %copy-done.2) | copy-start | bytes 3244804
  197.6 6.0 %collective-permute-start.19 = (f32[3,1,258]{2,0,1:T(4,128)S(1)}, f32[3,1,258]{2,0,1:T(4,128)S(1)}, u32[]{:S(2)}, u32[]{:S(2)}) collective-permute-start(f32[3,1,258]{2,0,1:T(4,128)S(1)} %get-tuple-element.152), channel_id=1, source_target_pairs={{0,1},{1,2},{2,3},{3,4},{4,5},{5,6},{6,7},{8,9},{9,10},{10,11},{11... | collective-permute-start | bytes 9296 | tf_op jit(solution)/shard_map/ppermute | solution.py:29
  199.9 9.1 %collective-permute-start.20 = (f32[3,1,258]{2,0,1:T(4,128)S(1)}, f32[3,1,258]{2,0,1:T(4,128)S(1)}, u32[]{:S(2)}, u32[]{:S(2)}) collective-permute-start(f32[3,1,258]{2,0,1:T(4,128)S(1)} %get-tuple-element.153), channel_id=1, source_target_pairs={{1,0},{2,1},{3,2},{4,3},{5,4},{6,5},{7,6},{9,8},{10,9},{11,10},{12... | collective-permute-start | bytes 9296 | tf_op jit(solution)/shard_map/ppermute | solution.py:30
  211.5 3.4 %copy-start.50 = (pred[130]{0:T(512)(128)(4,1)S(1)}, pred[130]{0:T(512)(128)(4,1)}, u32[]{:S(2)}) copy-start(pred[130]{0:T(512)(128)(4,1)} %get-tuple-element.201) | copy-start | bytes 394
  213.5 25.6 %collective-permute-start.21 = (f32[1,7,130,130]{3,0,2,1:T(1,128)}, f32[1,7,130,130]{3,0,2,1:T(1,128)}, u32[]{:S(2)}, u32[]{:S(2)}) collective-permute-start(f32[1,7,130,130]{3,0,2,1:T(1,128)} %copy.394), channel_id=1, source_target_pairs={{0,64},{8,72},{16,80},{24,88},{32,96},{40,104},{48,112},{56,120},{... | collective-permute-start | bytes 1419608 | tf_op jit(solution)/shard_map/ppermute | solution.py:38
  218.8 21.6 %copy-start.35 = (pred[3]{0:T(512)(128)(4,1)S(1)}, pred[3]{0:T(512)(128)(4,1)}, u32[]{:S(2)}) copy-start(pred[3]{0:T(512)(128)(4,1)} %copy-done.34) | copy-start | bytes 13
  242.5 2.3 copy-start
  254.7 1.4 copy-start.42
  254.8 1.5 copy-start.30
  256.2 1.7 copy-start.24
  256.2 1.7 copy-start.32
  271.1 1.6 copy-start.20
  271.6 2.4 copy-start.19
  283.3 2.9 copy-start.39
  292.3 2.0 copy-start.33
  292.3 2.0 copy-start.36
  295.0 10.2 %collective-permute-start.22 = (f32[1,3,128,128]{3,1,2,0:T(4,128)S(1)}, f32[1,3,128,128]{3,1,2,0:T(4,128)S(1)}, u32[]{:S(2)}, u32[]{:S(2)}) collective-permute-start(f32[1,3,128,128]{3,1,2,0:T(4,128)S(1)} %constant_dynamic-slice_fusion), channel_id=1, source_target_pairs={{0,64},{8,72},{16,80},{24,88},{32,96},{40,104},{48,112},{56,120},{... | collective-permute-start | bytes 589832 | tf_op jit(solution)/shard_map/ppermute | solution.py:38
  306.8 1.4 copy-start.5
  (17 other events, 17.0 us)
where the time goes:
time: 318 us; the launch traced here: 312 us
  other arithmetic  94.8 us (30%)
  waiting for transfers between devices  90.8 us (29%)
  starting transfers between devices  61.4 us (19%)
  local copies, waits for them, and re-layouts  58.8 us (18%)
  between operations  5.88 us (2%)
    ppermute x7, waiting for transfers between devices, swapped(): return lax.ppermute(value, axis, pairs)  58.9 us
    ppermute x8, starting transfers between devices, extended_2(): after = lax.ppermute(first, axis, down)  25.9 us
    ppermute x8, starting transfers between devices, extended_2(): before = lax.ppermute(last, axis, up)  23.6 us
    ppermute x8, waiting for transfers between devices, extended_2(): after = lax.ppermute(first, axis, down)  19.9 us
    ppermute x8, waiting for transfers between devices, extended_2(): before = lax.ppermute(last, axis, up)  12 us
    ppermute x7, starting transfers between devices, swapped(): return lax.ppermute(value, axis, pairs)  11.9 us
    unnamed x130, local copies, waits for them, and re-layouts  9.94 us
    gather x3, local copies, waits for them, and re-layouts, share_work(): kept_payload = payload[order[:slot_count]]  9.18 us
  transfers between devices with their start and end apart: 23, of which 13 were waited for; matrix products, arithmetic and copies ran while one was open for 8% of the time, Pallas kernels for 0%

commit v1 on v0

v1 whole, which is shorter than its diff:
```python
import functools
import math

import jax
import jax.numpy as jnp
from jax import lax
from jax.experimental import pallas as pl
from jax.experimental.pallas import tpu as pltpu
from jax.sharding import PartitionSpec as P

UPDATES = 20
GRAVITY = 9.81
HALF_STEP = 0.05
LOG_DRAG = math.log(9.81)
SPEED_EPS = 0.0001
BETA_ONE = 0.9
BETA_TWO = 0.999
LEARN_RATE = 0.05
ATAN_SCALE = 1.27
H, QX, QY, Z, LR, CH, CX, CY, WET = range(9)
NF = 9
TURNED = (H, QY, QX, Z, LR, CH, CY, CX, WET)
BLK = 8
VMEM_MB = 12


def from_prev_row(prev, cur):
    row = lax.broadcasted_iota(jnp.int32, cur.shape, 0)
    return pltpu.roll(jnp.where(row == cur.shape[0] - 1, prev, cur), 1, 0)


def from_next_row(cur, nxt):
    row = lax.broadcasted_iota(jnp.int32, cur.shape, 0)
    return pltpu.roll(jnp.where(row == 0, nxt, cur), cur.shape[0] - 1, 0)


def from_prev_col(x):
    return pltpu.roll(x, 1, 1)


def from_next_col(x):
    return pltpu.roll(x, x.shape[1] - 1, 1)


def flux_parts(h, qx, qy, slope_x, slope_y):
    inv = 1.0 / h
    u, v = qx * inv, qy * inv
    press = (0.5 * GRAVITY) * h * h
    k = HALF_STEP
    fx1, fy1 = k * qx, k * qy
    fx2, fxy, fy3 = k * (qx * u + press), k * (qx * v), k * (qy * v + press)
    h4, x4, y4 = 0.25 * h, 0.25 * qx, 0.25 * qy
    cols = [
        from_prev_col(h4 + fx1) + from_next_col(h4 - fx1),
        from_prev_col(x4 + fx2) + from_next_col(x4 - fx2) - h * slope_x,
        from_prev_col(y4 + fxy) + from_next_col(y4 - fxy) - h * slope_y,
    ]
    down = [h4 + fy1, x4 + fxy, y4 + fy3]
    up = [h4 - fy1, x4 - fxy, y4 - fy3]
    return cols, down, up, u, v


def drag_parts(h, qx, qy, rough):
    s2 = qx * qx + qy * qy + SPEED_EPS
    rs = lax.rsqrt(s2)
    b = jnp.exp(2.0 * rough + LOG_DRAG - (7.0 / 3.0) * jnp.log(h)) * (s2 * rs)
    w = 1.0 / (1.0 + b)
    return b, w, rs * rs


def gradient_passes(get, wet, n, lanes, scr, put_grad):
    SX, SY, UH, UX, UY, GA, GB, PH, PX, PY = range(10)

    def rows(i):
        return pl.ds(pl.multiple_of(i * BLK, BLK), BLK)

    def slopes(i):
        z = get(Z, i)
        zp, zn = get(Z, jnp.maximum(i - 1, 0)), get(Z, jnp.minimum(i + 1, n - 1))
        kg = HALF_STEP * GRAVITY
        sx = kg * (from_next_col(z) - from_prev_col(z))
        sy = kg * (from_next_row(z, zn) - from_prev_row(zp, z))
        return sx, sy

    def first_parts(i):
        sx, sy = slopes(i)
        scr[SX, rows(i), :] = sx
        scr[SY, rows(i), :] = sy
        cols, down, up, _, _ = flux_parts(get(H, i), get(QX, i), get(QY, i), sx, sy)
        return cols, down, up

    def first(i, carry):
        dprev, dcur, ucur, ccur = carry
        cols, down, up = first_parts(jnp.minimum(i + 1, n - 1))
        h, qx, qy = [
            from_prev_row(dprev[f], dcur[f]) + from_next_row(ucur[f], up[f]) + ccur[f]
            for f in range(3)
        ]
        b, w, _ = drag_parts(h, qx, qy, get(LR, i))
        m = wet(i)
        scr[UH, rows(i), :] = jnp.where(m, h, get(H, i))
        scr[UX, rows(i), :] = jnp.where(m, qx * w, get(QX, i))
        scr[UY, rows(i), :] = jnp.where(m, qy * w, get(QY, i))
        t = jnp.where(m, -2.0 * b * w * w, 0.0)
        scr[GA, rows(i), :] = t * qx
        scr[GB, rows(i), :] = t * qy
        return dcur, down, up, cols

    cols, down, up = first_parts(0)
    lax.fori_loop(0, n, first, (down, down, up, cols))

    def second_parts(i):
        r = rows(i)
        cols, down, up, u, v = flux_parts(
            scr[UH, r, :], scr[UX, r, :], scr[UY, r, :], scr[SX, r, :], scr[SY, r, :]
        )
        return cols, down, up, u, v

    def second(i, carry):
        dprev, dcur, ucur, ccur, u, v = carry
        cols, down, up, un, vn = second_parts(jnp.minimum(i + 1, n - 1))
        h, qx, qy = [
            from_prev_row(dprev[f], dcur[f]) + from_next_row(ucur[f], up[f]) + ccur[f]
            for f in range(3)
        ]
        b, w, inv_s2 = drag_parts(h, qx, qy, get(LR, i))
        m = wet(i)
        ch, cx, cy = get(CH, i), get(CX, i), get(CY, i)
        t = (cx * qx + cy * qy) * (w * w) * b
        ts = t * inv_s2
        scr[PH, rows(i), :] = jnp.where(m, ch + (7.0 / 3.0) * t / h, 0.0)
        scr[PX, rows(i), :] = jnp.where(m, cx * w - ts * qx, 0.0)
        scr[PY, rows(i), :] = jnp.where(m, cy * w - ts * qy, 0.0)
        put_grad(rows(i), jnp.where(m, -2.0 * t, 0.0), None)
        scr[SX, rows(i), :] = u
        scr[SY, rows(i), :] = v
        return dcur, down, up, cols, un, vn

    cols, down, up, u, v = second_parts(0)
    lax.fori_loop(0, n, second, (down, down, up, cols, u, v))

    def third(i, carry):
        r = rows(i)
        rp, rn = rows(jnp.maximum(i - 1, 0)), rows(jnp.minimum(i + 1, n - 1))
        ph, px, py = scr[PH, r, :], scr[PX, r, :], scr[PY, r, :]

        def four(f, cur):
            return (
                from_next_col(cur),
                from_prev_col(cur),
                from_next_row(cur, scr[f, rn, :]),
                from_prev_row(scr[f, rp, :], cur),
            )

        he, hw, hs, hn = four(PH, ph)
        xe, xw, xs, xn = four(PX, px)
        ye, yw, ys, yn = four(PY, py)
        u, v = scr[SX, r, :], scr[SY, r, :]
        k = HALF_STEP
        cross = k * ((ye - yw) + (xs - xn))
        cot_x = (
            0.25 * ((xe + xw) + (xs + xn))
            + k * (he - hw)
            + (2.0 * k) * u * (xe - xw)
            + v * cross
        )
        cot_y = (
            0.25 * ((ye + yw) + (ys + yn))
            + k * (hs - hn)
            + (2.0 * k) * v * (ys - yn)
            + u * cross
        )
        put_grad(r, None, scr[GA, r, :] * cot_x + scr[GB, r, :] * cot_y)
        return carry

    lax.fori_loop(0, n, third, 0)


def wet_rows(wet_ref, tile_row, shape, tile):
    lane = lax.broadcasted_iota(jnp.int32, shape, 1)
    left = (wet_ref[tile_row, 0] > 0).astype(jnp.float32)
    right = (wet_ref[tile_row, 1] > 0).astype(jnp.float32)
    return jnp.where(lane < tile, left, right)


def place(axis):
    index = lax.axis_index(axis)
    return index, lax.axis_size(axis)


def three_rows(block, first, mirrored, sign):
    natural = block[first : first + 3, :]
    reverse = jnp.concatenate([block[first + 2 - d : first + 3 - d, :] for d in range(3)], 0)
    return jnp.where(mirrored, sign * reverse, natural)


def pack_rows_kernel(wet_ref, wt, wb, gt, gb, lt, lb, ct, cb, a_ref, b_ref):
    gy, ny = place("gy")
    even = gy % 2 == 0
    a_ref[...] = jnp.zeros_like(a_ref)
    b_ref[...] = jnp.zeros_like(b_ref)
    tile = a_ref.shape[1] // 2
    shape = (8, a_ref.shape[1])
    top = [wt[0], wt[1], wt[2], gt[...], lt[...], ct[0], ct[1], ct[2], wet_rows(wet_ref, 0, shape, tile)]
    bot = [wb[0], wb[1], wb[2], gb[...], lb[...], cb[0], cb[1], cb[2], wet_rows(wet_ref, 1, shape, tile)]
    for f in range(NF):
        sign = -1.0 if f in (QY, CY) else 1.0
        t = three_rows(top[f], 0, gy == 0, sign)
        b = three_rows(bot[f], 5, gy == ny - 1, sign)
        a_ref[3 * f : 3 * f + 3, :] = jnp.where(even, b, t)
        b_ref[3 * f : 3 * f + 3, :] = jnp.where(even, t, b)


def inner_kernel(wet_ref, w_ref, z_ref, lr_ref, c_ref, g_ref, rs_ref, tl_ref, tr_ref, scr):
    height, lanes = z_ref.shape
    n = height // BLK
    tile_blocks = n // 2
    tile = lanes // 2
    shape = (BLK, lanes)

    def get(f, i):
        r = pl.ds(pl.multiple_of(i * BLK, BLK), BLK)
        if f <= QY:
            return w_ref[f, r, :]
        if f == Z:
            return z_ref[r, :]
        if f == LR:
            return lr_ref[r, :]
        return c_ref[f - CH, r, :]

    def wet(i):
        lane = lax.broadcasted_iota(jnp.int32, shape, 1)
        row = i // tile_blocks
        return jnp.where(lane < tile, wet_ref[row, 0], wet_ref[row, 1]) > 0

    def put_grad(r, second, first):
        if first is None:
            g_ref[r, :] = second
        else:
            g_ref[r, :] += first

    gradient_passes(get, wet, n, lanes, scr, put_grad)
    for f in range(NF - 1):
        rs_ref[f, 0:8, :] = get(f, 0)
        rs_ref[f, 8:16, :] = get(f, n - 1)
        if f <= QY:
            ref = w_ref.at[f]
        elif f == Z:
            ref = z_ref
        elif f == LR:
            ref = lr_ref
        else:
            ref = c_ref.at[f - CH]
        lane = lax.broadcasted_iota(jnp.int32, (height, 128), 1)
        both = jnp.where(lane < 64, ref[:, 0:128], ref[:, lanes - 128 : lanes])
        turned = both.T
        tl_ref[f] = turned[0:8, :]
        tr_ref[f] = turned[120:128, :]
    rs_ref[WET, 0:8, :] = wet_rows(wet_ref, 0, shape, tile)
    rs_ref[WET, 8:16, :] = wet_rows(wet_ref, 1, shape, tile)
    lane = lax.broadcasted_iota(jnp.int32, (8, height), 1)

    def wet_cols(col):
        top = (wet_ref[0, col] > 0).astype(jnp.float32)
        bottom = (wet_ref[1, col] > 0).astype(jnp.float32)
        return jnp.where(lane < height // 2, top, bottom)

    tl_ref[WET] = wet_cols(0)
    tr_ref[WET] = wet_cols(1)


def pack_cols_kernel(ya_ref, yb_ref, tl_ref, tr_ref, a_ref, b_ref, pl_ref, pr_ref, k_scr):
    gx, nx = place("gx")
    gy, _ = place("gy")
    even_y = gy % 2 == 0
    lanes = ya_ref.shape[1]
    below = jnp.where(even_y, ya_ref[...], yb_ref[...])
    above = jnp.where(even_y, yb_ref[...], ya_ref[...])
    lane = lax.broadcasted_iota(jnp.int32, (above.shape[0], 128), 1)
    above = jnp.where(lane < 64, above[:, 0:128], above[:, lanes - 128 : lanes])
    below = jnp.where(lane < 64, below[:, 0:128], below[:, lanes - 128 : lanes])
    k_scr[...] = jnp.zeros_like(k_scr)
    for f in range(NF):
        k_scr[6 * f : 6 * f + 3, :] = above[3 * f : 3 * f + 3, :]
        k_scr[6 * f + 3 : 6 * f + 6, :] = below[3 * f : 3 * f + 3, :]
    turned = k_scr[...].T
    left_corner, right_corner = turned[0:8, :], turned[120:128, :]
    pl_ref[...] = left_corner
    pr_ref[...] = right_corner
    even = gx % 2 == 0
    a_ref[...] = jnp.zeros_like(a_ref)
    b_ref[...] = jnp.zeros_like(b_ref)
    first, last = gx == 0, gx == nx - 1
    for f in range(NF):
        sign = -1.0 if f in (QX, CX) else 1.0
        t = three_rows(tl_ref[f], 0, first, sign)
        b = three_rows(tr_ref[f], 5, last, sign)
        a_ref[3 * f : 3 * f + 3, :] = jnp.where(even, b, t)
        b_ref[3 * f : 3 * f + 3, :] = jnp.where(even, t, b)
    lane = lax.broadcasted_iota(jnp.int32, (3, 128), 1)
    flip = ((lane >= 6 * QX) & (lane < 6 * QX + 6)) | ((lane >= 6 * CX) & (lane < 6 * CX + 6))
    sign = jnp.where(flip, -1.0, 1.0)
    t = three_rows(left_corner, 0, first, sign)
    b = three_rows(right_corner, 5, last, sign)
    a_ref[32:35, 0:128] = jnp.where(even, b, t)
    b_ref[32:35, 0:128] = jnp.where(even, t, b)


def strip_gradient(s_ref, scr, g_ref):
    n = s_ref.shape[1] // BLK

    def get(f, i):
        return s_ref[f, pl.ds(pl.multiple_of(i * BLK, BLK), BLK), :]

    def put_grad(r, second, first):
        if first is None:
            g_ref[r, :] = second
        else:
            g_ref[r, :] += first

    gradient_passes(get, lambda i: get(WET, i) > 0.5, n, s_ref.shape[2], scr, put_grad)


def arctan_ratio(y, x):
    a = jnp.abs(y)
    big, small = jnp.maximum(a, x), jnp.minimum(a, x)
    far = small > 0.41421356 * big
    t = jnp.where(far, small - big, small) / jnp.where(far, small + big, big)
    z = t * t
    p = ((8.05374449538e-2 * z - 1.38776856032e-1) * z + 1.99777106478e-1) * z - 3.33329491539e-1
    r = p * z * t + t + jnp.where(far, math.pi / 4, 0.0)
    r = jnp.where(a > x, math.pi / 2 - r, r)
    return jnp.where(y < 0, -r, r)


def rim_kernel(
    ya_ref, yb_ref, xa_ref, xb_ref, rs_ref, tl_ref, tr_ref, pl_ref, pr_ref, g_ref, lr_ref, m_ref, v_ref,
    nr_ref, nm_ref, nv_ref, row_s, col_s, row_scr, col_scr, row_g, col_g, turn_scr, side_scr,
):
    gx, nx = place("gx")
    gy, _ = place("gy")
    even_x, even_y = gx % 2 == 0, gy % 2 == 0
    height, lanes = lr_ref.shape
    for f in range(NF):
        r = slice(3 * f, 3 * f + 3)
        ya, yb = ya_ref[r, :], yb_ref[r, :]
        row_s[f, 0:8, :] = jnp.ones((8, lanes), jnp.float32)
        row_s[f, 24:32, :] = jnp.ones((8, lanes), jnp.float32)
        row_s[f, 5:8, :] = jnp.where(even_y, yb, ya)
        row_s[f, 24:27, :] = jnp.where(even_y, ya, yb)
        row_s[f, 8:24, :] = rs_ref[f]
    strip_gradient(row_s, row_scr, row_g)
    left_in = jnp.where(even_x, xb_ref[...], xa_ref[...])
    right_in = jnp.where(even_x, xa_ref[...], xb_ref[...])
    for f, t in enumerate(TURNED):
        shift = (125 - 6 * f) % 128
        r = slice(3 * f, 3 * f + 3)
        col_s[t, 0:8, :] = jnp.ones((8, col_s.shape[2]), jnp.float32)
        col_s[t, 24:32, :] = jnp.ones((8, col_s.shape[2]), jnp.float32)
        col_s[t, 5:8, 0:height] = left_in[r, :]
        col_s[t, 24:27, 0:height] = right_in[r, :]
        col_s[t, 8:16, 0:height] = tl_ref[f]
        col_s[t, 16:24, 0:height] = tr_ref[f]
        far = slice(height, height + 128)
        col_s[t, 5:8, far] = pltpu.roll(left_in[32:40, 0:128], shift, 1)[0:3, :]
        col_s[t, 24:27, far] = pltpu.roll(right_in[32:40, 0:128], shift, 1)[0:3, :]
        col_s[t, 8:16, far] = pltpu.roll(pl_ref[...], shift, 1)
        col_s[t, 16:24, far] = pltpu.roll(pr_ref[...], shift, 1)
    strip_gradient(col_s, col_scr, col_g)
    turn_scr[...] = jnp.zeros_like(turn_scr)
    turn_scr[0:8, :] = col_g[8:16, 0:height]
    turn_scr[120:128, :] = col_g[16:24, 0:height]
    side_scr[...] = turn_scr[...].T
    lane = lax.broadcasted_iota(jnp.int32, (16, lanes), 1)
    beside = (lane < 3) | (lane >= lanes - 3)

    def update(r, rim):
        g = rim(g_ref[r, :])
        side = side_scr[r, :]
        g = jnp.where(beside, jnp.concatenate([side] * (lanes // 128), 1), g)
        nm = BETA_ONE * m_ref[r, :] + (1.0 - BETA_ONE) * g
        nv = BETA_TWO * v_ref[r, :] + (1.0 - BETA_TWO) * g * g
        nm_ref[r, :] = nm
        nv_ref[r, :] = nv
        root = jnp.sqrt(nv * (1.0 / (1.0 - BETA_TWO**UPDATES)))
        turn = arctan_ratio(nm * (1.0 / (1.0 - BETA_ONE**UPDATES)), root)
        nr_ref[r, :] = lr_ref[r, :] - (LEARN_RATE * ATAN_SCALE) * turn

    def inside(i, carry):
        update(pl.ds(pl.multiple_of(i * 16, 16), 16), lambda g: g)
        return carry

    row = lax.broadcasted_iota(jnp.int32, (16, lanes), 0)
    update(slice(0, 16), lambda g: jnp.where(row < 3, row_g[8:24, :], g))
    lax.fori_loop(1, height // 16 - 1, inside, 0)
    update(slice(height - 16, height), lambda g: jnp.where(row >= 13, row_g[8:24, :], g))


def swap_pairs(n, odd):
    pairs = []
    for i in range(n):
        j = i ^ 1 if not odd else ((i + 1) ^ 1) - 1
        pairs.append((i, j if 0 <= j < n else i))
    return pairs


def call(kernel, out_shapes, scratch=(), in_specs=None, flops=0, name=None):
    params = pltpu.CompilerParams(vmem_limit_bytes=VMEM_MB << 20)
    shapes = [jax.ShapeDtypeStruct(s, jnp.float32) for s in out_shapes]
    kwargs = {} if in_specs is None else {"in_specs": in_specs}
    return pl.pallas_call(
        kernel,
        out_shape=shapes,
        scratch_shapes=list(scratch),
        compiler_params=params,
        cost_estimate=pl.CostEstimate(flops=flops, bytes_accessed=flops // 8, transcendentals=0),
        name=name,
        **kwargs,
    )


def on_device(water, ground, rough, moment, second, wet_tiles, cot):
    height, lanes = ground.shape
    smem = pl.BlockSpec(memory_space=pltpu.SMEM)
    whole = pl.BlockSpec(memory_space=pltpu.VMEM)
    last = height // 8 - 1
    top3 = pl.BlockSpec((3, 8, lanes), lambda i: (0, 0, 0))
    bot3 = pl.BlockSpec((3, 8, lanes), lambda i: (0, last, 0))
    top1 = pl.BlockSpec((8, lanes), lambda i: (0, 0))
    bot1 = pl.BlockSpec((8, lanes), lambda i: (last, 0))
    pay = jax.ShapeDtypeStruct((32, lanes), jnp.float32)
    pay_spec = pl.BlockSpec((32, lanes), lambda i: (0, 0))
    y_a, y_b = pl.pallas_call(
        pack_rows_kernel,
        grid=(1,),
        in_specs=[smem, top3, bot3, top1, bot1, top1, bot1, top3, bot3],
        out_specs=[pay_spec, pay_spec],
        out_shape=[pay, pay],
        compiler_params=pltpu.CompilerParams(vmem_limit_bytes=VMEM_MB << 20),
        name="pack_rows",
    )(wet_tiles, water, water, ground, ground, rough, rough, cot, cot)
    ny, nx = lax.axis_size("gy"), lax.axis_size("gx")
    y_a = lax.ppermute(y_a, "gy", swap_pairs(ny, False))
    y_b = lax.ppermute(y_b, "gy", swap_pairs(ny, True))
    grad, row_own, col_left, col_right = call(
        inner_kernel,
        [(height, lanes), (NF, 16, lanes), (NF, 8, height), (NF, 8, height)],
        scratch=[pltpu.VMEM((10, height, lanes), jnp.float32)],
        in_specs=[smem, whole, whole, whole, whole],
        flops=20_000_000,
        name="inner",
    )(wet_tiles, water, ground, rough, cot)
    x_a, x_b, corner_left, corner_right = call(
        pack_cols_kernel,
        [(40, height), (40, height), (8, 128), (8, 128)],
        scratch=[pltpu.VMEM((128, 128), jnp.float32)],
        name="pack_cols",
    )(y_a, y_b, col_left, col_right)
    x_a = lax.ppermute(x_a, "gx", swap_pairs(nx, False))
    x_b = lax.ppermute(x_b, "gx", swap_pairs(nx, True))
    return tuple(
        call(
            rim_kernel,
            [(height, lanes)] * 3,
            scratch=[
                pltpu.VMEM((NF, 32, lanes), jnp.float32),
                pltpu.VMEM((NF, 32, height + 128), jnp.float32),
                pltpu.VMEM((10, 32, lanes), jnp.float32),
                pltpu.VMEM((10, 32, height + 128), jnp.float32),
                pltpu.VMEM((32, lanes), jnp.float32),
                pltpu.VMEM((32, height + 128), jnp.float32),
                pltpu.VMEM((128, height), jnp.float32),
                pltpu.VMEM((height, 128), jnp.float32),
            ],
            name="rim",
        )(
            y_a, y_b, x_a, x_b, row_own, col_left, col_right, corner_left, corner_right,
            grad, rough, moment, second,
        )
    )


def solution(mesh):
    flat = P("gy", "gx")
    deep = P(None, "gy", "gx")
    return jax.shard_map(
        on_device,
        mesh=mesh,
        in_specs=(deep, flat, flat, flat, flat, flat, deep),
        out_specs=(flat, flat, flat),
        check_vma=False,
    )
```

time: 318 us -> 34.3 us (0.11)
  the two profiles are of different devices: /device:TPU:46 before, /device:TPU:57 now
where the time goes in v1:
time: 34.3 us; the launch traced here: 34 us
  Pallas kernels  15 us (44%)
  starting transfers between devices  9.71 us (28%)
  local copies, waits for them, and re-layouts  4.86 us (14%)
  waiting for transfers between devices  3.7 us (11%)
  between operations  0.74 us (2%)
    pallas_call x1, Pallas kernels, on_device(): call(inner_kernel, [(height, lanes), (NF, 16, lanes), (NF, 8, height), (N...  9.85 us
    unnamed x16, local copies, waits for them, and re-layouts  4.86 us
    pallas_call x1, Pallas kernels, on_device(): call(rim_kernel, [(height, lanes)] * 3, scratch=[pltpu.VMEM((NF, 32, lane...  4.42 us
    ppermute x1, starting transfers between devices, on_device(): y_b = lax.ppermute(y_b, 'gy', swap_pairs(ny, True))  4.38 us
    ppermute x1, waiting for transfers between devices, on_device(): x_b = lax.ppermute(x_b, 'gx', swap_pairs(nx, True))  3.69 us
    ppermute x1, starting transfers between devices, on_device(): x_b = lax.ppermute(x_b, 'gx', swap_pairs(nx, True))  2.73 us
    ppermute x1, starting transfers between devices, on_device(): x_a = lax.ppermute(x_a, 'gx', swap_pairs(nx, False))  1.31 us
    ppermute x1, starting transfers between devices, on_device(): y_a = lax.ppermute(y_a, 'gy', swap_pairs(ny, False))  1.29 us
  transfers between devices with their start and end apart: 4, of which 1 were waited for; matrix products, arithmetic and copies ran while one was open for 0% of the time, Pallas kernels for 29%

profile of v1, /device:TPU:57, one launch (start us, length us, event | category | flops | bytes accessed | tf_op | source)
XLA Modules:
  0.0 34.0 jit_solution(5855555310921843202)
XLA Ops:
  0.6 0.0 copy-start
  0.6 1.1 %copy-done = f32[3,256,256]{2,1,0:T(8,128)S(1)} copy-done((f32[3,256,256]{2,1,0:T(8,128)S(1)}, f32[3,256,256]{2,1,0:T(8,128)}, u32[]{:S(2)}) %copy-start) | copy-done | bytes 786456
  1.8 0.0 copy-start.1
  1.8 1.1 %copy-done.1 = f32[3,256,256]{2,1,0:T(8,128)S(1)} copy-done((f32[3,256,256]{2,1,0:T(8,128)S(1)}, f32[3,256,256]{2,1,0:T(8,128)}, u32[]{:S(2)}) %copy-start.1) | copy-done | bytes 786456
  2.9 0.0 copy-start.2
  2.9 0.9 %copy-done.2 = f32[256,256]{1,0:T(8,128)S(1)} copy-done((f32[256,256]{1,0:T(8,128)S(1)}, f32[256,256]{1,0:T(8,128)}, u32[]{:S(2)}) %copy-start.2) | copy-done | bytes 262168
  3.8 0.0 copy-start.4
  3.9 0.9 %copy-done.4 = f32[256,256]{1,0:T(8,128)S(1)} copy-done((f32[256,256]{1,0:T(8,128)S(1)}, f32[256,256]{1,0:T(8,128)}, u32[]{:S(2)}) %copy-start.4) | copy-done | bytes 262168
  4.8 0.0 copy-start.7
  4.8 0.7 %copy-done.7 = s32[2,2]{1,0:T(2,128)S(1)} copy-done((s32[2,2]{1,0:T(2,128)S(1)}, s32[2,2]{1,0:T(2,128)}, u32[]{:S(2)}) %copy-start.7) | copy-done | bytes 40
  5.5 0.6 %pack_rows.1 = (f32[32,256]{1,0:T(8,128)S(1)}, f32[32,256]{1,0:T(8,128)S(1)}) custom-call(s32[2,2]{1,0:T(2,128)S(1)} %copy-done.7, f32[3,256,256]{2,1,0:T(8,128)S(1)} %copy-done, f32[3,256,256]{2,1,0:T(8,128)S(1)} %copy-done, f32[256,256]{1,0:T(8,128)S(1)} %copy-done.4, f32[256,256]{1,0:T(8,128)S(1)} %copy-done.4, f32[256,256]{1,0:T(8,128)S(1)} %copy-done.2, ...), custom_call_target="tpu_custom_call" | custom-call | tf_op jit(solution)/shard_map/pack_rows/pallas_call | solution.py:433
  6.1 1.3 %collective-permute-start = (f32[32,256]{1,0:T(8,128)S(1)}, f32[32,256]{1,0:T(8,128)S(1)}, u32[]{:S(2)}, u32[]{:S(2)}) collective-permute-start(f32[32,256]{1,0:T(8,128)S(1)} %get-tuple-element.13), channel_id=1, source_target_pairs={{0,1},{1,0},{2,3},{3,2},{4,5},{5,4},{6,7},{7,6},{8,9},{9,8},{10,11... | collective-permute-start | bytes 98312 | tf_op jit(solution)/shard_map/ppermute | solution.py:443
  7.4 4.4 %collective-permute-start.1 = (f32[32,256]{1,0:T(8,128)S(1)}, f32[32,256]{1,0:T(8,128)S(1)}, u32[]{:S(2)}, u32[]{:S(2)}) collective-permute-start(f32[32,256]{1,0:T(8,128)S(1)} %get-tuple-element.14), channel_id=1, source_target_pairs={{0,0},{1,2},{2,1},{3,4},{4,3},{5,6},{6,5},{7,7},{8,8},{9,10},{10,9... | collective-permute-start | bytes 98312 | tf_op jit(solution)/shard_map/ppermute | solution.py:444
  11.8 0.0 copy-start.3
  11.8 0.0 copy-start.5
  11.8 0.0 copy-start.6
  11.8 9.9 %inner.1 = (f32[256,256]{1,0:T(8,128)S(1)}, f32[9,16,256]{2,1,0:T(8,128)S(1)}, f32[9,8,256]{2,1,0:T(8,128)S(1)}, f32[9,8,256]{2,1,0:T(8,128)S(1)}) custom-call(s32[2,2]{1,0:T(2,128)S(1)} %copy-done.7, f32[3,256,256]{2,1,0:T(8,128)S(1)} %copy-done, f32[256,256]{1,0:T(8,128)S(1)} %copy-done.4, f32[256,256]{1,0:T(8,128)S(1)} %copy-done.2, ...), custom_call_target="tpu_custom_call" | custom-call | flops 20000000 | bytes 2500000 | tf_op jit(solution)/shard_map/inner/pallas_call | solution.py:445
  21.7 0.0 collective-permute-done.ya_ref
  21.7 0.0 collective-permute-done.1.yb_ref
  21.7 0.1 pack_cols.1
  21.8 1.3 %collective-permute-start.2 = (f32[40,256]{1,0:T(8,128)S(1)}, f32[40,256]{1,0:T(8,128)S(1)}, u32[]{:S(2)}, u32[]{:S(2)}) collective-permute-start(f32[40,256]{1,0:T(8,128)S(1)} %get-tuple-element.17), channel_id=1, source_target_pairs={{0,8},{8,0},{16,24},{24,16},{32,40},{40,32},{48,56},{56,48},{64,72... | collective-permute-start | bytes 122888 | tf_op jit(solution)/shard_map/ppermute | solution.py:459
  23.1 2.7 %collective-permute-start.3 = (f32[40,256]{1,0:T(8,128)S(1)}, f32[40,256]{1,0:T(8,128)S(1)}, u32[]{:S(2)}, u32[]{:S(2)}) collective-permute-start(f32[40,256]{1,0:T(8,128)S(1)} %get-tuple-element.18), channel_id=1, source_target_pairs={{0,0},{8,16},{16,8},{24,32},{32,24},{40,48},{48,40},{56,64},{64,56... | collective-permute-start | bytes 122888 | tf_op jit(solution)/shard_map/ppermute | solution.py:460
  25.8 0.0 collective-permute-done.2.xa_ref
  25.8 3.7 %collective-permute-done.3.xb_ref = f32[40,256]{1,0:T(8,128)S(1)} collective-permute-done((f32[40,256]{1,0:T(8,128)S(1)}, f32[40,256]{1,0:T(8,128)S(1)}, u32[]{:S(2)}, u32[]{:S(2)}) %collective-permute-start.3) | collective-permute-done | bytes 40992 | tf_op jit(solution)/shard_map/ppermute | solution.py:460
  29.5 0.0 copy-done.3
  29.5 0.0 copy-done.5
  29.5 0.0 copy-done.6
  29.6 4.4 %rim.1 = (f32[256,256]{1,0:T(8,128)}, f32[256,256]{1,0:T(8,128)}, f32[256,256]{1,0:T(8,128)}) custom-call(f32[32,256]{1,0:T(8,128)S(1)} %collective-permute-done.ya_ref, f32[32,256]{1,0:T(8,128)S(1)} %collective-permute-done.1.yb_ref, f32[40,256]{1,0:T(8,128)S(1)} %collective-permute-done.2.xa_ref, f32[40,256]{1,0:T(8,128)S(1)} %collective-permute-done.3.xb_ref, ...), custom_call_target="tpu_custom_call" | custom-call | tf_op jit(solution)/shard_map/rim/pallas_call | solution.py:462
Async XLA Ops:
  0.6 1.1 %copy-start = (f32[3,256,256]{2,1,0:T(8,128)S(1)}, f32[3,256,256]{2,1,0:T(8,128)}, u32[]{:S(2)}) copy-start(f32[3,256,256]{2,1,0:T(8,128)} %w_ref.1) | copy-start | bytes 2359300
  1.8 1.1 %copy-start.1 = (f32[3,256,256]{2,1,0:T(8,128)S(1)}, f32[3,256,256]{2,1,0:T(8,128)}, u32[]{:S(2)}) copy-start(f32[3,256,256]{2,1,0:T(8,128)} %c_ref.1) | copy-start | bytes 2359300
  2.9 0.9 %copy-start.2 = (f32[256,256]{1,0:T(8,128)S(1)}, f32[256,256]{1,0:T(8,128)}, u32[]{:S(2)}) copy-start(f32[256,256]{1,0:T(8,128)} %lr_ref.3) | copy-start | bytes 786436
  3.8 0.9 %copy-start.4 = (f32[256,256]{1,0:T(8,128)S(1)}, f32[256,256]{1,0:T(8,128)}, u32[]{:S(2)}) copy-start(f32[256,256]{1,0:T(8,128)} %z_ref.1) | copy-start | bytes 786436
  4.8 0.7 %copy-start.7 = (s32[2,2]{1,0:T(2,128)S(1)}, s32[2,2]{1,0:T(2,128)}, u32[]{:S(2)}) copy-start(s32[2,2]{1,0:T(2,128)} %wet_ref.3) | copy-start | bytes 52
  6.1 15.6 %collective-permute-start = (f32[32,256]{1,0:T(8,128)S(1)}, f32[32,256]{1,0:T(8,128)S(1)}, u32[]{:S(2)}, u32[]{:S(2)}) collective-permute-start(f32[32,256]{1,0:T(8,128)S(1)} %get-tuple-element.13), channel_id=1, source_target_pairs={{0,1},{1,0},{2,3},{3,2},{4,5},{5,4},{6,7},{7,6},{8,9},{9,8},{10,11... | collective-permute-start | bytes 98312 | tf_op jit(solution)/shard_map/ppermute | solution.py:443
  7.4 14.3 %collective-permute-start.1 = (f32[32,256]{1,0:T(8,128)S(1)}, f32[32,256]{1,0:T(8,128)S(1)}, u32[]{:S(2)}, u32[]{:S(2)}) collective-permute-start(f32[32,256]{1,0:T(8,128)S(1)} %get-tuple-element.14), channel_id=1, source_target_pairs={{0,0},{1,2},{2,1},{3,4},{4,3},{5,6},{6,5},{7,7},{8,8},{9,10},{10,9... | collective-permute-start | bytes 98312 | tf_op jit(solution)/shard_map/ppermute | solution.py:444
  11.8 17.8 %copy-start.3 = (f32[256,256]{1,0:T(8,128)S(1)}, f32[256,256]{1,0:T(8,128)}, u32[]{:S(2)}) copy-start(f32[256,256]{1,0:T(8,128)} %lr_ref.3) | copy-start | bytes 786436
  11.8 17.8 %copy-start.5 = (f32[256,256]{1,0:T(8,128)S(1)}, f32[256,256]{1,0:T(8,128)}, u32[]{:S(2)}) copy-start(f32[256,256]{1,0:T(8,128)} %m_ref.1) | copy-start | bytes 786436
  11.8 17.8 %copy-start.6 = (f32[256,256]{1,0:T(8,128)S(1)}, f32[256,256]{1,0:T(8,128)}, u32[]{:S(2)}) copy-start(f32[256,256]{1,0:T(8,128)} %v_ref.1) | copy-start | bytes 786436
  21.8 4.1 %collective-permute-start.2 = (f32[40,256]{1,0:T(8,128)S(1)}, f32[40,256]{1,0:T(8,128)S(1)}, u32[]{:S(2)}, u32[]{:S(2)}) collective-permute-start(f32[40,256]{1,0:T(8,128)S(1)} %get-tuple-element.17), channel_id=1, source_target_pairs={{0,8},{8,0},{16,24},{24,16},{32,40},{40,32},{48,56},{56,48},{64,72... | collective-permute-start | bytes 122888 | tf_op jit(solution)/shard_map/ppermute | solution.py:459
  23.1 6.4 %collective-permute-start.3 = (f32[40,256]{1,0:T(8,128)S(1)}, f32[40,256]{1,0:T(8,128)S(1)}, u32[]{:S(2)}, u32[]{:S(2)}) collective-permute-start(f32[40,256]{1,0:T(8,128)S(1)} %get-tuple-element.18), channel_id=1, source_target_pairs={{0,0},{8,16},{16,8},{24,32},{32,24},{40,48},{48,40},{56,64},{64,56... | collective-permute-start | bytes 122888 | tf_op jit(solution)/shard_map/ppermute | solution.py:460

commit v2 on v1

v2 whole, which is shorter than its diff:
```python
import functools
import math

import jax
import jax.numpy as jnp
from jax import lax
from jax.experimental import pallas as pl
from jax.experimental.pallas import tpu as pltpu
from jax.sharding import PartitionSpec as P

UPDATES = 20
GRAVITY = 9.81
HALF_STEP = 0.05
LOG_DRAG = math.log(9.81)
SPEED_EPS = 0.0001
BETA_ONE = 0.9
BETA_TWO = 0.999
LEARN_RATE = 0.05
ATAN_SCALE = 1.27
H, QX, QY, Z, LR, CH, CX, CY, WET = range(9)
NF = 9
TURNED = (H, QY, QX, Z, LR, CH, CY, CX, WET)
BLK = 8
UNROLL = 8
VMEM_MB = 12


def from_prev_col(x):
    return pltpu.roll(x, 1, 1)


def from_next_col(x):
    return pltpu.roll(x, x.shape[1] - 1, 1)


def flux_parts(h, qx, qy, slope_x, slope_y):
    inv = 1.0 / h
    u, v = qx * inv, qy * inv
    press = (0.5 * GRAVITY) * h * h
    k = HALF_STEP
    fx1, fy1 = k * qx, k * qy
    fx2, fxy, fy3 = k * (qx * u + press), k * (qx * v), k * (qy * v + press)
    h4, x4, y4 = 0.25 * h, 0.25 * qx, 0.25 * qy
    cols = [
        from_prev_col(h4 + fx1) + from_next_col(h4 - fx1),
        from_prev_col(x4 + fx2) + from_next_col(x4 - fx2) - h * slope_x,
        from_prev_col(y4 + fxy) + from_next_col(y4 - fxy) - h * slope_y,
    ]
    down = [h4 + fy1, x4 + fxy, y4 + fy3]
    up = [h4 - fy1, x4 - fxy, y4 - fy3]
    return cols, down, up, u, v


def drag_parts(h, qx, qy, rough):
    s2 = qx * qx + qy * qy + SPEED_EPS
    rs = lax.rsqrt(s2)
    b = jnp.exp(2.0 * rough + LOG_DRAG - (7.0 / 3.0) * jnp.log(h)) * (s2 * rs)
    w = 1.0 / (1.0 + b)
    return b, w, rs * rs


def rows(j):
    if isinstance(j, int):
        return slice(j * BLK, j * BLK + BLK)
    return pl.ds(pl.multiple_of(j * BLK, BLK), BLK)


def take(ref, j, off=0):
    r = pl.ds(j * BLK + 8 + off, BLK)
    if off == 0 and not isinstance(j, int):
        r = pl.ds(pl.multiple_of(j * BLK + 8, 8), BLK)
    return jnp.concatenate([ref[t, r, :] for t in range(ref.shape[0])], 1)


def give(ref, j, value):
    put(ref, pl.ds(pl.multiple_of(j * BLK + 8, 8), BLK), value)


def put(ref, r, value, at=0):
    for t in range(value.shape[1] // 128):
        ref[at + t, r, :] = value[:, 128 * t : 128 * t + 128]


def looped(n, step):
    if n <= 8:
        for j in range(n):
            step(j)
        return

    def body(j, carry):
        step(j)
        return carry

    lax.fori_loop(0, n, body, 0, unroll=UNROLL)


UH, UX, UY, SX, SY, GA, GB = range(7)
N_AHEAD, N_ACROSS, N_SHIFTED = 7, 6, 9
DOWN, UP, ZS = 0, 3, 6
PH, PX, PY = range(3)
ADJ = 6
VU, VV, PG = 3, 4, 5


def gathered(shifted, across, j):
    r = rows(j)
    return [
        take(shifted.at[DOWN + f], j, -1) + take(shifted.at[UP + f], j, 1) + across[f, r, :]
        for f in range(3)
    ]


def first_pass(get, wet, n, scr, shifted, across):
    looped(n, lambda j: give(shifted.at[ZS], j, get(Z, j)))

    def parts(j):
        r = rows(j)
        kg = HALF_STEP * GRAVITY
        z = get(Z, j)
        sx = kg * (from_next_col(z) - from_prev_col(z))
        sy = kg * (take(shifted.at[ZS], j, 1) - take(shifted.at[ZS], j, -1))
        scr[SX, r, :] = sx
        scr[SY, r, :] = sy
        cols, down, up, _, _ = flux_parts(get(H, j), get(QX, j), get(QY, j), sx, sy)
        for f in range(3):
            across[f, r, :] = cols[f]
            give(shifted.at[DOWN + f], j, down[f])
            give(shifted.at[UP + f], j, up[f])

    looped(n, parts)

    def finish(j):
        r = rows(j)
        h, qx, qy = gathered(shifted, across, j)
        b, w, _ = drag_parts(h, qx, qy, get(LR, j))
        m = wet(j)
        scr[UH, r, :] = jnp.where(m, h, get(H, j))
        scr[UX, r, :] = jnp.where(m, qx * w, get(QX, j))
        scr[UY, r, :] = jnp.where(m, qy * w, get(QY, j))
        t = jnp.where(m, -2.0 * b * w * w, 0.0)
        scr[GA, r, :] = t * qx
        scr[GB, r, :] = t * qy

    looped(n, finish)


def last_passes(get, wet, n, scr, shifted, across, put_grad):
    def parts(j):
        r = rows(j)
        cols, down, up, u, v = flux_parts(*(scr[f, r, :] for f in (UH, UX, UY, SX, SY)))
        across[VU, r, :] = u
        across[VV, r, :] = v
        for f in range(3):
            across[f, r, :] = cols[f]
            give(shifted.at[DOWN + f], j, down[f])
            give(shifted.at[UP + f], j, up[f])

    looped(n, parts)

    def finish(j):
        h, qx, qy = gathered(shifted, across, j)
        b, w, inv_s2 = drag_parts(h, qx, qy, get(LR, j))
        m = wet(j)
        ch, cx, cy = get(CH, j), get(CX, j), get(CY, j)
        t = (cx * qx + cy * qy) * (w * w) * b
        ts = t * inv_s2
        return [
            jnp.where(m, ch + (7.0 / 3.0) * t / h, 0.0),
            jnp.where(m, cx * w - ts * qx, 0.0),
            jnp.where(m, cy * w - ts * qy, 0.0),
            jnp.where(m, -2.0 * t, 0.0),
        ]

    def finish_all(j):
        for f, value in enumerate(finish(j)):
            if f < 3:
                give(shifted.at[ADJ + f], j, value)
            else:
                across[PG, rows(j), :] = value

    looped(n, finish_all)

    def back(j):
        r = rows(j)

        def four(f):
            ref = shifted.at[ADJ + f]
            cur = take(ref, j)
            return from_next_col(cur), from_prev_col(cur), take(ref, j, 1), take(ref, j, -1)

        he, hw, hs, hn = four(PH)
        xe, xw, xs, xn = four(PX)
        ye, yw, ys, yn = four(PY)
        u, v = across[VU, r, :], across[VV, r, :]
        k = HALF_STEP
        cross = k * ((ye - yw) + (xs - xn))
        cot_x = (
            0.25 * ((xe + xw) + (xs + xn))
            + k * (he - hw)
            + (2.0 * k) * u * (xe - xw)
            + v * cross
        )
        cot_y = (
            0.25 * ((ye + yw) + (ys + yn))
            + k * (hs - hn)
            + (2.0 * k) * v * (ys - yn)
            + u * cross
        )
        put_grad(j, across[PG, r, :] + scr[GA, r, :] * cot_x + scr[GB, r, :] * cot_y)

    looped(n, back)


def place(axis):
    index = lax.axis_index(axis)
    return index, lax.axis_size(axis)


def three_rows(block, first, mirrored, sign):
    natural = block[first : first + 3, :]
    reverse = jnp.concatenate([block[first + 2 - d : first + 3 - d, :] for d in range(3)], 0)
    return jnp.where(mirrored, sign * reverse, natural)


def pack_rows_kernel(wet_hbm, w_hbm, z_hbm, lr_hbm, c_hbm, a_ref, b_ref, wet_ref, wet_s, top, bot, sems):
    height, lanes = z_hbm.shape
    copies = [pltpu.make_async_copy(wet_hbm, wet_s, sems.at[0])]
    for side, (buf, row) in enumerate(((top, 0), (bot, height - 8))):
        r = pl.ds(row, 8)
        for at, (src, dst) in enumerate((
            (w_hbm.at[:, r, :], buf.at[pl.ds(0, 3)]),
            (z_hbm.at[r, :], buf.at[Z]),
            (lr_hbm.at[r, :], buf.at[LR]),
            (c_hbm.at[:, r, :], buf.at[pl.ds(CH, 3)]),
        )):
            copies.append(pltpu.make_async_copy(src, dst, sems.at[1 + 4 * side + at]))
    for copy in copies:
        copy.start()
    gy, ny = place("gy")
    even = gy % 2 == 0
    lane = lax.broadcasted_iota(jnp.int32, (8, lanes), 1)
    a_ref[24:32, :] = jnp.zeros((8, lanes), jnp.float32)
    b_ref[24:32, :] = jnp.zeros((8, lanes), jnp.float32)
    for copy in copies:
        copy.wait()
    for row in range(2):
        left = (wet_s[row, 0] > 0).astype(jnp.float32)
        right = (wet_s[row, 1] > 0).astype(jnp.float32)
        wet_ref[8 * row : 8 * row + 8, :] = jnp.where(lane < lanes // 2, left, right)
    for f in range(NF):
        sign = -1.0 if f in (QY, CY) else 1.0
        t = three_rows(top[f] if f < WET else wet_ref[0:8, :], 0, gy == 0, sign)
        b = three_rows(bot[f] if f < WET else wet_ref[8:16, :], 5, gy == ny - 1, sign)
        a_ref[3 * f : 3 * f + 3, :] = jnp.where(even, b, t)
        b_ref[3 * f : 3 * f + 3, :] = jnp.where(even, t, b)


def tile_wet(wet_ref, j, n):
    return wet_ref[rows(j // (n // 2)), :] > 0.5


def forward_kernel(wet_ref, w_ref, z_ref, lr_ref, c_ref, scr, rs_ref, tl_ref, tr_ref, shifted, across):
    height, lanes = z_ref.shape
    n = height // BLK

    def field(f):
        if f <= QY:
            return w_ref.at[f]
        return z_ref if f == Z else lr_ref if f == LR else c_ref.at[f - CH]

    def get(f, j):
        return field(f)[rows(j), :]

    first_pass(get, lambda j: tile_wet(wet_ref, j, n), n, scr, shifted, across)
    lane = lax.broadcasted_iota(jnp.int32, (height, 128), 1)
    for f in range(WET):
        ref = field(f)
        rs_ref[f, 0:8, :] = ref[0:8, :]
        rs_ref[f, 8:16, :] = ref[height - 8 : height, :]
        turned = jnp.where(lane < 64, ref[:, 0:128], ref[:, lanes - 128 : lanes]).T
        tl_ref[f] = turned[0:8, :]
        tr_ref[f] = turned[120:128, :]
    top, bottom = wet_ref[0:8, :], wet_ref[8:16, :]
    rs_ref[WET, 0:8, :] = top
    rs_ref[WET, 8:16, :] = bottom
    half = lanes // 2
    tl_ref[WET] = jnp.concatenate([top[:, :half], bottom[:, :half]], 1)
    tr_ref[WET] = jnp.concatenate([top[:, half:], bottom[:, half:]], 1)


def backward_kernel(after_ref, wet_ref, lr_ref, c_ref, scr, g_ref, shifted, across):
    n = lr_ref.shape[0] // BLK

    def get(f, j):
        return (lr_ref if f == LR else c_ref.at[f - CH])[rows(j), :]

    def put_grad(j, value):
        g_ref[rows(j), :] = value

    last_passes(get, lambda j: tile_wet(wet_ref, j, n), n, scr, shifted, across, put_grad)


def pack_cols_kernel(ya_ref, yb_ref, tl_ref, tr_ref, a_ref, b_ref, pl_ref, pr_ref, k_scr):
    gx, nx = place("gx")
    gy, _ = place("gy")
    even_y = gy % 2 == 0
    lanes = ya_ref.shape[1]
    below = jnp.where(even_y, ya_ref[...], yb_ref[...])
    above = jnp.where(even_y, yb_ref[...], ya_ref[...])
    lane = lax.broadcasted_iota(jnp.int32, (above.shape[0], 128), 1)
    above = jnp.where(lane < 64, above[:, 0:128], above[:, lanes - 128 : lanes])
    below = jnp.where(lane < 64, below[:, 0:128], below[:, lanes - 128 : lanes])
    k_scr[...] = jnp.zeros_like(k_scr)
    for f in range(NF):
        k_scr[6 * f : 6 * f + 3, :] = above[3 * f : 3 * f + 3, :]
        k_scr[6 * f + 3 : 6 * f + 6, :] = below[3 * f : 3 * f + 3, :]
    turned = k_scr[...].T
    left_corner, right_corner = turned[0:8, :], turned[120:128, :]
    pl_ref[...] = left_corner
    pr_ref[...] = right_corner
    even = gx % 2 == 0
    a_ref[...] = jnp.zeros_like(a_ref)
    b_ref[...] = jnp.zeros_like(b_ref)
    first, last = gx == 0, gx == nx - 1
    for f in range(NF):
        sign = -1.0 if f in (QX, CX) else 1.0
        t = three_rows(tl_ref[f], 0, first, sign)
        b = three_rows(tr_ref[f], 5, last, sign)
        a_ref[3 * f : 3 * f + 3, :] = jnp.where(even, b, t)
        b_ref[3 * f : 3 * f + 3, :] = jnp.where(even, t, b)
    lane = lax.broadcasted_iota(jnp.int32, (3, 128), 1)
    flip = ((lane >= 6 * QX) & (lane < 6 * QX + 6)) | ((lane >= 6 * CX) & (lane < 6 * CX + 6))
    sign = jnp.where(flip, -1.0, 1.0)
    t = three_rows(left_corner, 0, first, sign)
    b = three_rows(right_corner, 5, last, sign)
    a_ref[32:35, 0:128] = jnp.where(even, b, t)
    b_ref[32:35, 0:128] = jnp.where(even, t, b)


def strip_gradient(s_ref, scr, shifted, across, g_ref):
    n = s_ref.shape[1] // BLK

    def get(f, j):
        return s_ref[f, rows(j), :]

    def wet(j):
        return get(WET, j) > 0.5

    def put_grad(j, value):
        g_ref[rows(j), :] = value

    first_pass(get, wet, n, scr, shifted, across)
    last_passes(get, wet, n, scr, shifted, across, put_grad)


def arctan_ratio(y, x):
    a = jnp.abs(y)
    big, small = jnp.maximum(a, x), jnp.minimum(a, x)
    far = small > 0.41421356 * big
    t = jnp.where(far, small - big, small) / jnp.where(far, small + big, big)
    z = t * t
    p = ((8.05374449538e-2 * z - 1.38776856032e-1) * z + 1.99777106478e-1) * z - 3.33329491539e-1
    r = p * z * t + t + jnp.where(far, math.pi / 4, 0.0)
    r = jnp.where(a > x, math.pi / 2 - r, r)
    return jnp.where(y < 0, -r, r)


def rim_kernel(
    ya_ref, yb_ref, xa_ref, xb_ref, rs_ref, tl_ref, tr_ref, pl_ref, pr_ref, g_ref, lr_ref, m_ref, v_ref,
    nr_ref, nm_ref, nv_ref, row_s, col_s, row_scr, col_scr, row_sh, col_sh, row_ac, col_ac, row_g, col_g, turn_scr, side_scr,
):
    gx, nx = place("gx")
    gy, _ = place("gy")
    even_x, even_y = gx % 2 == 0, gy % 2 == 0
    height, lanes = lr_ref.shape
    for f in range(NF):
        r = slice(3 * f, 3 * f + 3)
        ya, yb = ya_ref[r, :], yb_ref[r, :]
        row_s[f, 0:8, :] = jnp.ones((8, lanes), jnp.float32)
        row_s[f, 24:32, :] = jnp.ones((8, lanes), jnp.float32)
        row_s[f, 5:8, :] = jnp.where(even_y, yb, ya)
        row_s[f, 24:27, :] = jnp.where(even_y, ya, yb)
        row_s[f, 8:24, :] = rs_ref[f]
    strip_gradient(row_s, row_scr, row_sh, row_ac, row_g)
    left_in = jnp.where(even_x, xb_ref[...], xa_ref[...])
    right_in = jnp.where(even_x, xa_ref[...], xb_ref[...])
    for f, t in enumerate(TURNED):
        shift = (125 - 6 * f) % 128
        r = slice(3 * f, 3 * f + 3)
        col_s[t, 0:8, :] = jnp.ones((8, height + 128), jnp.float32)
        col_s[t, 24:32, :] = jnp.ones((8, height + 128), jnp.float32)
        col_s[t, 5:8, 0:height] = left_in[r, :]
        col_s[t, 24:27, 0:height] = right_in[r, :]
        col_s[t, 8:16, 0:height] = tl_ref[f]
        col_s[t, 16:24, 0:height] = tr_ref[f]
        col_s[t, 5:8, height:] = pltpu.roll(left_in[32:40, 0:128], shift, 1)[0:3, :]
        col_s[t, 24:27, height:] = pltpu.roll(right_in[32:40, 0:128], shift, 1)[0:3, :]
        col_s[t, 8:16, height:] = pltpu.roll(pl_ref[...], shift, 1)
        col_s[t, 16:24, height:] = pltpu.roll(pr_ref[...], shift, 1)
    strip_gradient(col_s, col_scr, col_sh, col_ac, col_g)
    turn_scr[...] = jnp.zeros_like(turn_scr)
    turn_scr[0:8, :] = col_g[8:16, 0:height]
    turn_scr[120:128, :] = col_g[16:24, 0:height]
    side_scr[...] = turn_scr[...].T
    lane = lax.broadcasted_iota(jnp.int32, (16, lanes), 1)
    beside = (lane < 3) | (lane >= lanes - 3)

    def update(r, rim):
        g = rim(g_ref[r, :])
        side = side_scr[r, :]
        g = jnp.where(beside, jnp.concatenate([side] * (lanes // 128), 1), g)
        nm = BETA_ONE * m_ref[r, :] + (1.0 - BETA_ONE) * g
        nv = BETA_TWO * v_ref[r, :] + (1.0 - BETA_TWO) * g * g
        nm_ref[r, :] = nm
        nv_ref[r, :] = nv
        root = jnp.sqrt(nv * (1.0 / (1.0 - BETA_TWO**UPDATES)))
        turn = arctan_ratio(nm * (1.0 / (1.0 - BETA_ONE**UPDATES)), root)
        nr_ref[r, :] = lr_ref[r, :] - (LEARN_RATE * ATAN_SCALE) * turn

    def inside(i, carry):
        update(pl.ds(pl.multiple_of(i * 16, 16), 16), lambda g: g)
        return carry

    row = lax.broadcasted_iota(jnp.int32, (16, lanes), 0)
    update(slice(0, 16), lambda g: jnp.where(row < 3, row_g[8:24, :], g))
    lax.fori_loop(1, height // 16 - 1, inside, 0)
    update(slice(height - 16, height), lambda g: jnp.where(row >= 13, row_g[8:24, :], g))


def swap_pairs(n, odd):
    pairs = []
    for i in range(n):
        j = i ^ 1 if not odd else ((i + 1) ^ 1) - 1
        pairs.append((i, j if 0 <= j < n else i))
    return pairs


def call(kernel, out_shapes, scratch=(), in_specs=None, flops=0, name=None, vmem_mb=VMEM_MB):
    params = pltpu.CompilerParams(vmem_limit_bytes=vmem_mb << 20)
    shapes = [jax.ShapeDtypeStruct(s, jnp.float32) for s in out_shapes]
    kwargs = {} if in_specs is None else {"in_specs": in_specs}
    return pl.pallas_call(
        kernel,
        out_shape=shapes,
        scratch_shapes=list(scratch),
        compiler_params=params,
        cost_estimate=pl.CostEstimate(flops=flops, bytes_accessed=flops // 8, transcendentals=0),
        name=name,
        **kwargs,
    )


def on_device(water, ground, rough, moment, second, wet_tiles, cot):
    height, lanes = ground.shape
    hbm = pl.BlockSpec(memory_space=pltpu.HBM)
    y_a, y_b, wet = call(
        pack_rows_kernel,
        [(32, lanes), (32, lanes), (16, lanes)],
        scratch=[
            pltpu.SMEM((2, 2), jnp.int32),
            pltpu.VMEM((8, 8, lanes), jnp.float32),
            pltpu.VMEM((8, 8, lanes), jnp.float32),
            pltpu.SemaphoreType.DMA((9,)),
        ],
        in_specs=[hbm] * 5,
        name="pack_rows",
        vmem_mb=60,
    )(wet_tiles, water, ground, rough, cot)
    ny, nx = lax.axis_size("gy"), lax.axis_size("gx")
    y_a = lax.ppermute(y_a, "gy", swap_pairs(ny, False))
    y_b = lax.ppermute(y_b, "gy", swap_pairs(ny, True))
    scratch = [
        pltpu.VMEM((N_SHIFTED, lanes // 128, height + 16, 128), jnp.float32),
        pltpu.VMEM((N_ACROSS, height, lanes), jnp.float32),
    ]
    ahead, row_own, col_left, col_right = call(
        forward_kernel,
        [(N_AHEAD, height, lanes), (NF, 16, lanes), (NF, 8, height), (NF, 8, height)],
        scratch=scratch,
        flops=20_000_000,
        name="forward",
    )(wet, water, ground, rough, cot)
    x_a, x_b, corner_left, corner_right = call(
        pack_cols_kernel,
        [(40, height), (40, height), (8, 128), (8, 128)],
        scratch=[pltpu.VMEM((128, 128), jnp.float32)],
        name="pack_cols",
    )(y_a, y_b, col_left, col_right)
    (grad,) = call(
        backward_kernel,
        [(height, lanes)],
        scratch=scratch,
        flops=20_000_000,
        name="backward",
    )(corner_left, wet, rough, cot, ahead)
    x_a = lax.ppermute(x_a, "gx", swap_pairs(nx, False))
    x_b = lax.ppermute(x_b, "gx", swap_pairs(nx, True))
    return tuple(
        call(
            rim_kernel,
            [(height, lanes)] * 3,
            scratch=[
                pltpu.VMEM((NF, 32, lanes), jnp.float32),
                pltpu.VMEM((NF, 32, height + 128), jnp.float32),
                pltpu.VMEM((N_AHEAD, 32, lanes), jnp.float32),
                pltpu.VMEM((N_AHEAD, 32, height + 128), jnp.float32),
                pltpu.VMEM((N_SHIFTED, lanes // 128, 48, 128), jnp.float32),
                pltpu.VMEM((N_SHIFTED, height // 128 + 1, 48, 128), jnp.float32),
                pltpu.VMEM((N_ACROSS, 32, lanes), jnp.float32),
                pltpu.VMEM((N_ACROSS, 32, height + 128), jnp.float32),
                pltpu.VMEM((32, lanes), jnp.float32),
                pltpu.VMEM((32, height + 128), jnp.float32),
                pltpu.VMEM((128, height), jnp.float32),
                pltpu.VMEM((height, 128), jnp.float32),
            ],
            name="rim",
        )(
            y_a, y_b, x_a, x_b, row_own, col_left, col_right, corner_left, corner_right,
            grad, rough, moment, second,
        )
    )


def solution(mesh):
    flat = P("gy", "gx")
    deep = P(None, "gy", "gx")
    return jax.shard_map(
        on_device,
        mesh=mesh,
        in_specs=(deep, flat, flat, flat, flat, flat, deep),
        out_specs=(flat, flat, flat),
        check_vma=False,
    )
```

time: 34.3 us -> 23.6 us (0.69)
  Pallas kernels: 15 us -> 8.3 us
  local copies, waits for them, and re-layouts: 4.86 us -> 0.74 us
  starting transfers between devices: 9.71 us -> 11.6 us
  waiting for transfers between devices: 3.7 us -> 1.92 us
    pallas_call x2 -> x3, Pallas kernels: 10.4 us -> 5.86 us  [the longest x1 2.52 us: on_device(): call(backward_kernel, [(height, lanes)], scratch=scratch, flops=20000000,...]
    unnamed x16 -> x14, local copies, waits for them, and re-layouts: 4.86 us -> 0.74 us
    ppermute x1, waiting for transfers between devices: 3.69 us -> 0.26 us  [on_device(): x_b = lax.ppermute(x_b, 'gx', swap_pairs(nx, True))]
    pallas_call x1, Pallas kernels: 4.42 us -> 2.35 us  [on_device(): call(rim_kernel, [(height, lanes)] * 3, scratch=[pltpu.VMEM((NF, 32, lane...]
    ppermute x1, waiting for transfers between devices: 0.01 us -> 1.65 us  [on_device(): y_b = lax.ppermute(y_b, 'gy', swap_pairs(ny, True))]
    ppermute x1, starting transfers between devices: 1.31 us -> 2.28 us  [on_device(): x_a = lax.ppermute(x_a, 'gx', swap_pairs(nx, False))]
    ppermute x1, starting transfers between devices: 2.73 us -> 3.63 us  [on_device(): x_b = lax.ppermute(x_b, 'gx', swap_pairs(nx, True))]
  transfers between devices with their start and end apart: 4 -> 4, of which waited for: 1 -> 2; matrix products, arithmetic and copies ran while one was open for 0% -> 0% of each run, Pallas kernels for 29% -> 18%
where the time goes in v2:
time: 23.6 us; the launch traced here: 23.3 us
  starting transfers between devices  11.6 us (49%)
  Pallas kernels  8.3 us (35%)
  waiting for transfers between devices  1.92 us (8%)
  between operations  0.79 us (3%)
  local copies, waits for them, and re-layouts  0.74 us (3%)
    ppermute x1, starting transfers between devices, on_device(): y_b = lax.ppermute(y_b, 'gy', swap_pairs(ny, True))  4.38 us
    ppermute x1, starting transfers between devices, on_device(): x_b = lax.ppermute(x_b, 'gx', swap_pairs(nx, True))  3.63 us
    pallas_call x1, Pallas kernels, on_device(): call(backward_kernel, [(height, lanes)], scratch=scratch, flops=20000000,...  2.52 us
    pallas_call x1, Pallas kernels, on_device(): call(rim_kernel, [(height, lanes)] * 3, scratch=[pltpu.VMEM((NF, 32, lane...  2.35 us
    ppermute x1, starting transfers between devices, on_device(): x_a = lax.ppermute(x_a, 'gx', swap_pairs(nx, False))  2.28 us
    pallas_call x1, Pallas kernels, on_device(): call(pack_rows_kernel, [(32, lanes), (32, lanes), (16, lanes)], scratch=[...  1.71 us
    ppermute x1, waiting for transfers between devices, on_device(): y_b = lax.ppermute(y_b, 'gy', swap_pairs(ny, True))  1.65 us
    pallas_call x1, Pallas kernels, on_device(): call(forward_kernel, [(N_AHEAD, height, lanes), (NF, 16, lanes), (NF, 8,...  1.63 us
  transfers between devices with their start and end apart: 4, of which 2 were waited for; matrix products, arithmetic and copies ran while one was open for 0% of the time, Pallas kernels for 18%

profile of v2, /device:TPU:57, one launch (start us, length us, event | category | flops | bytes accessed | tf_op | source)
XLA Modules:
  0.0 23.3 jit_solution(16715558220676244231)
XLA Ops:
  0.6 0.0 copy-start.2
  0.6 0.0 copy-start.3
  0.7 0.0 copy-start.1
  0.7 0.0 copy-start
  0.7 1.7 %pack_rows.1 = (f32[32,256]{1,0:T(8,128)}, f32[32,256]{1,0:T(8,128)}, f32[16,256]{1,0:T(8,128)}) custom-call(s32[2,2]{1,0:T(2,128)} %wet_hbm.1, f32[3,256,256]{2,1,0:T(8,128)} %w_ref.1, f32[256,256]{1,0:T(8,128)} %z_ref.1, f32[256,256]{1,0:T(8,128)} %lr_ref.5, f32[3,256,256]{2,1,0:T(8,128)} %c_ref.3), custom_call_target="tpu_custom_call" | custom-call | tf_op jit(solution)/shard_map/pack_rows/pallas_call | solution.py:456
  2.4 1.3 %collective-permute-start = (f32[32,256]{1,0:T(8,128)}, f32[32,256]{1,0:T(8,128)S(1)}, u32[]{:S(2)}, u32[]{:S(2)}) collective-permute-start(f32[32,256]{1,0:T(8,128)} %get-tuple-element.14), channel_id=1, source_target_pairs={{0,1},{1,0},{2,3},{3,2},{4,5},{5,4},{6,7},{7,6},{8,9},{9,8},{10,11... | collective-permute-start | bytes 98312 | tf_op jit(solution)/shard_map/ppermute | solution.py:470
  3.7 4.4 %collective-permute-start.1 = (f32[32,256]{1,0:T(8,128)}, f32[32,256]{1,0:T(8,128)S(1)}, u32[]{:S(2)}, u32[]{:S(2)}) collective-permute-start(f32[32,256]{1,0:T(8,128)} %get-tuple-element.15), channel_id=1, source_target_pairs={{0,0},{1,2},{2,1},{3,4},{4,3},{5,6},{6,5},{7,7},{8,8},{9,10},{10,9... | collective-permute-start | bytes 98312 | tf_op jit(solution)/shard_map/ppermute | solution.py:471
  8.1 0.0 copy-done.2
  8.1 0.0 copy-done.3
  8.1 0.0 copy-done.1
  8.1 0.0 copy-done
  8.1 0.0 copy-start.6
  8.1 0.7 %copy-done.6 = f32[16,256]{1,0:T(8,128)S(1)} copy-done((f32[16,256]{1,0:T(8,128)S(1)}, f32[16,256]{1,0:T(8,128)}, u32[]{:S(2)}) %copy-start.6) | copy-done | bytes 16408
  8.8 1.6 %forward.1 = (f32[7,256,256]{2,1,0:T(8,128)S(1)}, f32[9,16,256]{2,1,0:T(8,128)S(1)}, f32[9,8,256]{2,1,0:T(8,128)S(1)}, f32[9,8,256]{2,1,0:T(8,128)S(1)}) custom-call(f32[16,256]{1,0:T(8,128)S(1)} %copy-done.6, f32[3,256,256]{2,1,0:T(8,128)S(1)} %copy-done.2, f32[256,256]{1,0:T(8,128)S(1)} %copy-done.3, f32[256,256]{1,0:T(8,128)S(1)} %copy-done.1, ...), custom_call_target="tpu_custom_call" | custom-call | flops 20000000 | bytes 2500000 | tf_op jit(solution)/shard_map/forward/pallas_call | solution.py:476
  10.5 0.0 copy-start.4
  10.5 0.0 copy-start.5
  10.5 0.0 collective-permute-done.ya_ref
  10.5 1.6 %collective-permute-done.1.yb_ref = f32[32,256]{1,0:T(8,128)S(1)} collective-permute-done((f32[32,256]{1,0:T(8,128)}, f32[32,256]{1,0:T(8,128)S(1)}, u32[]{:S(2)}, u32[]{:S(2)}) %collective-permute-start.1) | collective-permute-done | bytes 32800 | tf_op jit(solution)/shard_map/ppermute | solution.py:471
  12.1 0.1 pack_cols.1
  12.3 2.3 %collective-permute-start.2 = (f32[40,256]{1,0:T(8,128)S(1)}, f32[40,256]{1,0:T(8,128)S(1)}, u32[]{:S(2)}, u32[]{:S(2)}) collective-permute-start(f32[40,256]{1,0:T(8,128)S(1)} %get-tuple-element.19), channel_id=1, source_target_pairs={{0,8},{8,0},{16,24},{24,16},{32,40},{40,32},{48,56},{56,48},{64,72... | collective-permute-start | bytes 122888 | tf_op jit(solution)/shard_map/ppermute | solution.py:496
  14.5 3.6 %collective-permute-start.3 = (f32[40,256]{1,0:T(8,128)S(1)}, f32[40,256]{1,0:T(8,128)S(1)}, u32[]{:S(2)}, u32[]{:S(2)}) collective-permute-start(f32[40,256]{1,0:T(8,128)S(1)} %get-tuple-element.20), channel_id=1, source_target_pairs={{0,0},{8,16},{16,8},{24,32},{32,24},{40,48},{48,40},{56,64},{64,56... | collective-permute-start | bytes 122888 | tf_op jit(solution)/shard_map/ppermute | solution.py:497
  18.2 2.5 %backward.1.g_ref = f32[256,256]{1,0:T(8,128)S(1)} custom-call(f32[8,128]{1,0:T(8,128)S(1)} %get-tuple-element.22.after_ref.pl_ref, f32[16,256]{1,0:T(8,128)S(1)} %copy-done.6, f32[256,256]{1,0:T(8,128)S(1)} %copy-done.1, f32[3,256,256]{2,1,0:T(8,128)S(1)} %copy-done, f32[7,256,256]{2,1,0:T(8,128)S(1)} %get-tuple-element.24.scr), custom_call_target="tpu_custom_call" | custom-call | flops 20000000 | bytes 2500000 | tf_op jit(solution)/shard_map/backward/pallas_call | solution.py:489
  20.7 0.0 collective-permute-done.2.xa_ref
  20.7 0.3 %collective-permute-done.3.xb_ref = f32[40,256]{1,0:T(8,128)S(1)} collective-permute-done((f32[40,256]{1,0:T(8,128)S(1)}, f32[40,256]{1,0:T(8,128)S(1)}, u32[]{:S(2)}, u32[]{:S(2)}) %collective-permute-start.3) | collective-permute-done | bytes 40992 | tf_op jit(solution)/shard_map/ppermute | solution.py:497
  21.0 0.0 copy-done.4
  21.0 0.0 copy-done.5
  21.0 2.3 %rim.1 = (f32[256,256]{1,0:T(8,128)}, f32[256,256]{1,0:T(8,128)}, f32[256,256]{1,0:T(8,128)}) custom-call(f32[32,256]{1,0:T(8,128)S(1)} %collective-permute-done.ya_ref, f32[32,256]{1,0:T(8,128)S(1)} %collective-permute-done.1.yb_ref, f32[40,256]{1,0:T(8,128)S(1)} %collective-permute-done.2.xa_ref, f32[40,256]{1,0:T(8,128)S(1)} %collective-permute-done.3.xb_ref, ...), custom_call_target="tpu_custom_call" | custom-call | tf_op jit(solution)/shard_map/rim/pallas_call | solution.py:499
Async XLA Ops:
  0.6 7.4 %copy-start.2 = (f32[3,256,256]{2,1,0:T(8,128)S(1)}, f32[3,256,256]{2,1,0:T(8,128)}, u32[]{:S(2)}) copy-start(f32[3,256,256]{2,1,0:T(8,128)} %w_ref.1) | copy-start | bytes 2359300
  0.6 7.4 %copy-start.3 = (f32[256,256]{1,0:T(8,128)S(1)}, f32[256,256]{1,0:T(8,128)}, u32[]{:S(2)}) copy-start(f32[256,256]{1,0:T(8,128)} %z_ref.1) | copy-start | bytes 786436
  0.7 7.4 %copy-start.1 = (f32[256,256]{1,0:T(8,128)S(1)}, f32[256,256]{1,0:T(8,128)}, u32[]{:S(2)}) copy-start(f32[256,256]{1,0:T(8,128)} %lr_ref.5) | copy-start | bytes 786436
  0.7 7.4 %copy-start = (f32[3,256,256]{2,1,0:T(8,128)S(1)}, f32[3,256,256]{2,1,0:T(8,128)}, u32[]{:S(2)}) copy-start(f32[3,256,256]{2,1,0:T(8,128)} %c_ref.3) | copy-start | bytes 2359300
  2.4 8.1 %collective-permute-start = (f32[32,256]{1,0:T(8,128)}, f32[32,256]{1,0:T(8,128)S(1)}, u32[]{:S(2)}, u32[]{:S(2)}) collective-permute-start(f32[32,256]{1,0:T(8,128)} %get-tuple-element.14), channel_id=1, source_target_pairs={{0,1},{1,0},{2,3},{3,2},{4,5},{5,4},{6,7},{7,6},{8,9},{9,8},{10,11... | collective-permute-start | bytes 98312 | tf_op jit(solution)/shard_map/ppermute | solution.py:470
  3.7 8.5 %collective-permute-start.1 = (f32[32,256]{1,0:T(8,128)}, f32[32,256]{1,0:T(8,128)S(1)}, u32[]{:S(2)}, u32[]{:S(2)}) collective-permute-start(f32[32,256]{1,0:T(8,128)} %get-tuple-element.15), channel_id=1, source_target_pairs={{0,0},{1,2},{2,1},{3,4},{4,3},{5,6},{6,5},{7,7},{8,8},{9,10},{10,9... | collective-permute-start | bytes 98312 | tf_op jit(solution)/shard_map/ppermute | solution.py:471
  8.1 0.7 %copy-start.6 = (f32[16,256]{1,0:T(8,128)S(1)}, f32[16,256]{1,0:T(8,128)}, u32[]{:S(2)}) copy-start(f32[16,256]{1,0:T(8,128)} %get-tuple-element.16.wet_ref) | copy-start | bytes 49156
  10.5 10.5 %copy-start.4 = (f32[256,256]{1,0:T(8,128)S(1)}, f32[256,256]{1,0:T(8,128)}, u32[]{:S(2)}) copy-start(f32[256,256]{1,0:T(8,128)} %m_ref.1) | copy-start | bytes 786436
  10.5 10.5 %copy-start.5 = (f32[256,256]{1,0:T(8,128)S(1)}, f32[256,256]{1,0:T(8,128)}, u32[]{:S(2)}) copy-start(f32[256,256]{1,0:T(8,128)} %v_ref.1) | copy-start | bytes 786436
  12.3 8.5 %collective-permute-start.2 = (f32[40,256]{1,0:T(8,128)S(1)}, f32[40,256]{1,0:T(8,128)S(1)}, u32[]{:S(2)}, u32[]{:S(2)}) collective-permute-start(f32[40,256]{1,0:T(8,128)S(1)} %get-tuple-element.19), channel_id=1, source_target_pairs={{0,8},{8,0},{16,24},{24,16},{32,40},{40,32},{48,56},{56,48},{64,72... | collective-permute-start | bytes 122888 | tf_op jit(solution)/shard_map/ppermute | solution.py:496
  14.5 6.4 %collective-permute-start.3 = (f32[40,256]{1,0:T(8,128)S(1)}, f32[40,256]{1,0:T(8,128)S(1)}, u32[]{:S(2)}, u32[]{:S(2)}) collective-permute-start(f32[40,256]{1,0:T(8,128)S(1)} %get-tuple-element.20), channel_id=1, source_target_pairs={{0,0},{8,16},{16,8},{24,32},{32,24},{40,48},{48,40},{56,64},{64,56... | collective-permute-start | bytes 122888 | tf_op jit(solution)/shard_map/ppermute | solution.py:497

commit v3 on v2

--- a/solution.py
+++ b/solution.py
@@ -222,7 +222,7 @@
     return jnp.where(mirrored, sign * reverse, natural)
 
 
-def pack_rows_kernel(wet_hbm, w_hbm, z_hbm, lr_hbm, c_hbm, a_ref, b_ref, wet_ref, wet_s, top, bot, sems):
+def pack_rows_kernel(wet_hbm, w_hbm, z_hbm, lr_hbm, c_hbm, b_ref, a_ref, wet_ref, wet_s, top, bot, sems):
     height, lanes = z_hbm.shape
     copies = [pltpu.make_async_copy(wet_hbm, wet_s, sems.at[0])]
     for side, (buf, row) in enumerate(((top, 0), (bot, height - 8))):
@@ -300,7 +300,7 @@
     last_passes(get, lambda j: tile_wet(wet_ref, j, n), n, scr, shifted, across, put_grad)
 
 
-def pack_cols_kernel(ya_ref, yb_ref, tl_ref, tr_ref, a_ref, b_ref, pl_ref, pr_ref, k_scr):
+def pack_cols_kernel(yb_ref, ya_ref, tl_ref, tr_ref, b_ref, a_ref, pl_ref, pr_ref, k_scr):
     gx, nx = place("gx")
     gy, _ = place("gy")
     even_y = gy % 2 == 0
@@ -366,7 +366,7 @@
 
 
 def rim_kernel(
-    ya_ref, yb_ref, xa_ref, xb_ref, rs_ref, tl_ref, tr_ref, pl_ref, pr_ref, g_ref, lr_ref, m_ref, v_ref,
+    yb_ref, ya_ref, xb_ref, xa_ref, rs_ref, tl_ref, tr_ref, pl_ref, pr_ref, g_ref, lr_ref, m_ref, v_ref,
     nr_ref, nm_ref, nv_ref, row_s, col_s, row_scr, col_scr, row_sh, col_sh, row_ac, col_ac, row_g, col_g, turn_scr, side_scr,
 ):
     gx, nx = place("gx")
@@ -453,7 +453,7 @@
 def on_device(water, ground, rough, moment, second, wet_tiles, cot):
     height, lanes = ground.shape
     hbm = pl.BlockSpec(memory_space=pltpu.HBM)
-    y_a, y_b, wet = call(
+    y_b, y_a, wet = call(
         pack_rows_kernel,
         [(32, lanes), (32, lanes), (16, lanes)],
         scratch=[
@@ -464,11 +464,11 @@
         ],
         in_specs=[hbm] * 5,
         name="pack_rows",
-        vmem_mb=60,
-    )(wet_tiles, water, ground, rough, cot)
+        vmem_mb=12,
+    )(*(pltpu.with_memory_space_constraint(x, pltpu.HBM) for x in (wet_tiles, water, ground, rough, cot)))
     ny, nx = lax.axis_size("gy"), lax.axis_size("gx")
+    y_b = lax.ppermute(y_b, "gy", swap_pairs(ny, True))
     y_a = lax.ppermute(y_a, "gy", swap_pairs(ny, False))
-    y_b = lax.ppermute(y_b, "gy", swap_pairs(ny, True))
     scratch = [
         pltpu.VMEM((N_SHIFTED, lanes // 128, height + 16, 128), jnp.float32),
         pltpu.VMEM((N_ACROSS, height, lanes), jnp.float32),
@@ -480,12 +480,12 @@
         flops=20_000_000,
         name="forward",
     )(wet, water, ground, rough, cot)
-    x_a, x_b, corner_left, corner_right = call(
+    x_b, x_a, corner_left, corner_right = call(
         pack_cols_kernel,
         [(40, height), (40, height), (8, 128), (8, 128)],
         scratch=[pltpu.VMEM((128, 128), jnp.float32)],
         name="pack_cols",
-    )(y_a, y_b, col_left, col_right)
+    )(y_b, y_a, col_left, col_right)
     (grad,) = call(
         backward_kernel,
         [(height, lanes)],
@@ -493,8 +493,8 @@
         flops=20_000_000,
         name="backward",
     )(corner_left, wet, rough, cot, ahead)
+    x_b = lax.ppermute(x_b, "gx", swap_pairs(nx, True))
     x_a = lax.ppermute(x_a, "gx", swap_pairs(nx, False))
-    x_b = lax.ppermute(x_b, "gx", swap_pairs(nx, True))
     return tuple(
         call(
             rim_kernel,
@@ -515,7 +515,7 @@
             ],
             name="rim",
         )(
-            y_a, y_b, x_a, x_b, row_own, col_left, col_right, corner_left, corner_right,
+            y_b, y_a, x_b, x_a, row_own, col_left, col_right, corner_left, corner_right,
             grad, rough, moment, second,
         )
     )

time: 23.6 us -> 20.8 us (0.88)
  starting transfers between devices: 11.6 us -> 10.7 us
  local copies, waits for them, and re-layouts: 0.74 us -> 0.03 us
  Pallas kernels: 8.3 us -> 7.7 us
  waiting for transfers between devices: 1.92 us -> 1.41 us
    ppermute x1, starting transfers between devices: 2.28 us -> 0.09 us  [on_device(): x_a = lax.ppermute(x_a, 'gx', swap_pairs(nx, False))]
    ppermute x1, starting transfers between devices: 3.63 us -> 5.44 us  [on_device(): x_b = lax.ppermute(x_b, 'gx', swap_pairs(nx, True))]
    ppermute x1, starting transfers between devices: 1.29 us -> 0.09 us  [on_device(): y_a = lax.ppermute(y_a, 'gy', swap_pairs(ny, False))]
    unnamed x14 -> x12, local copies, waits for them, and re-layouts: 0.74 us -> 0.03 us
    ppermute x1, starting transfers between devices: 4.38 us -> 5.06 us  [on_device(): y_b = lax.ppermute(y_b, 'gy', swap_pairs(ny, True))]
    pallas_call x1, Pallas kernels: 1.71 us -> 1.08 us  [on_device(): call(pack_rows_kernel, [(32, lanes), (32, lanes), (16, lanes)], scratch=[...]
    ppermute x1, waiting for transfers between devices: 0.26 us -> 0.01 us  [on_device(): x_b = lax.ppermute(x_b, 'gx', swap_pairs(nx, True))]
    ppermute x1, waiting for transfers between devices: 1.65 us -> 1.4 us  [on_device(): y_b = lax.ppermute(y_b, 'gy', swap_pairs(ny, True))]
  transfers between devices with their start and end apart: 4 -> 4, of which waited for: 2 -> 1; matrix products, arithmetic and copies ran while one was open for 0% -> 0% of each run, Pallas kernels for 18% -> 20%
where the time goes in v3:
time: 20.8 us; the launch traced here: 20.6 us
  starting transfers between devices  10.7 us (51%)
  Pallas kernels  7.7 us (37%)
  waiting for transfers between devices  1.41 us (7%)
  between operations  0.81 us (4%)
    ppermute x1, starting transfers between devices, on_device(): x_b = lax.ppermute(x_b, 'gx', swap_pairs(nx, True))  5.44 us
    ppermute x1, starting transfers between devices, on_device(): y_b = lax.ppermute(y_b, 'gy', swap_pairs(ny, True))  5.06 us
    pallas_call x1, Pallas kernels, on_device(): call(backward_kernel, [(height, lanes)], scratch=scratch, flops=20000000,...  2.52 us
    pallas_call x1, Pallas kernels, on_device(): call(rim_kernel, [(height, lanes)] * 3, scratch=[pltpu.VMEM((NF, 32, lane...  2.35 us
    pallas_call x1, Pallas kernels, on_device(): call(forward_kernel, [(N_AHEAD, height, lanes), (NF, 16, lanes), (NF, 8,...  1.64 us
    ppermute x1, waiting for transfers between devices, on_device(): y_b = lax.ppermute(y_b, 'gy', swap_pairs(ny, True))  1.4 us
    pallas_call x1, Pallas kernels, on_device(): call(pack_rows_kernel, [(32, lanes), (32, lanes), (16, lanes)], scratch=[...  1.08 us
  transfers between devices with their start and end apart: 4, of which 1 were waited for; matrix products, arithmetic and copies ran while one was open for 0% of the time, Pallas kernels for 20%

profile of v3, /device:TPU:57, one launch (start us, length us, event | category | flops | bytes accessed | tf_op | source)
XLA Modules:
  0.0 20.6 jit_solution(2444592832611955287)
XLA Ops:
  0.6 0.0 copy-start.2
  0.6 0.0 copy-start.3
  0.7 0.0 copy-start.1
  0.7 0.0 copy-start
  0.7 1.1 %pack_rows.1 = (f32[32,256]{1,0:T(8,128)S(1)}, f32[32,256]{1,0:T(8,128)S(1)}, f32[16,256]{1,0:T(8,128)S(1)}) custom-call(s32[2,2]{1,0:T(2,128)} %wet_hbm.1, f32[3,256,256]{2,1,0:T(8,128)} %w_ref.1, f32[256,256]{1,0:T(8,128)} %z_ref.1, f32[256,256]{1,0:T(8,128)} %lr_ref.5, f32[3,256,256]{2,1,0:T(8,128)} %c_ref.3), custom_call_target="tpu_custom_call" | custom-call | tf_op jit(solution)/shard_map/pack_rows/pallas_call | solution.py:456
  1.8 5.1 %collective-permute-start = (f32[32,256]{1,0:T(8,128)S(1)}, f32[32,256]{1,0:T(8,128)S(1)}, u32[]{:S(2)}, u32[]{:S(2)}) collective-permute-start(f32[32,256]{1,0:T(8,128)S(1)} %get-tuple-element.14), channel_id=1, source_target_pairs={{0,0},{1,2},{2,1},{3,4},{4,3},{5,6},{6,5},{7,7},{8,8},{9,10},{10,9... | collective-permute-start | bytes 98312 | tf_op jit(solution)/shard_map/ppermute | solution.py:470
  6.8 0.1 collective-permute-start.1
  6.9 0.0 copy-done.2
  6.9 0.0 copy-done.3
  6.9 0.0 copy-done.1
  7.0 0.0 copy-done
  7.0 1.6 %forward.1 = (f32[7,256,256]{2,1,0:T(8,128)S(1)}, f32[9,16,256]{2,1,0:T(8,128)S(1)}, f32[9,8,256]{2,1,0:T(8,128)S(1)}, f32[9,8,256]{2,1,0:T(8,128)S(1)}) custom-call(f32[16,256]{1,0:T(8,128)S(1)} %get-tuple-element.16.wet_ref, f32[3,256,256]{2,1,0:T(8,128)S(1)} %copy-done.2, f32[256,256]{1,0:T(8,128)S(1)} %copy-done.3, f32[256,256]{1,0:T(8,128)S(1)} %copy-done.1, ...), custom_call_target="tpu_custom_call" | custom-call | flops 20000000 | bytes 2500000 | tf_op jit(solution)/shard_map/forward/pallas_call | solution.py:476
  8.6 0.0 copy-start.4
  8.6 0.0 copy-start.5
  8.6 1.4 %collective-permute-done.yb_ref = f32[32,256]{1,0:T(8,128)S(1)} collective-permute-done((f32[32,256]{1,0:T(8,128)S(1)}, f32[32,256]{1,0:T(8,128)S(1)}, u32[]{:S(2)}, u32[]{:S(2)}) %collective-permute-start) | collective-permute-done | bytes 32800 | tf_op jit(solution)/shard_map/ppermute | solution.py:470
  10.0 0.0 collective-permute-done.1.ya_ref
  10.0 0.1 pack_cols.1
  10.1 5.4 %collective-permute-start.2 = (f32[40,256]{1,0:T(8,128)S(1)}, f32[40,256]{1,0:T(8,128)S(1)}, u32[]{:S(2)}, u32[]{:S(2)}) collective-permute-start(f32[40,256]{1,0:T(8,128)S(1)} %get-tuple-element.19), channel_id=1, source_target_pairs={{0,0},{8,16},{16,8},{24,32},{32,24},{40,48},{48,40},{56,64},{64,56... | collective-permute-start | bytes 122888 | tf_op jit(solution)/shard_map/ppermute | solution.py:496
  15.6 0.1 collective-permute-start.3
  15.7 2.5 %backward.1.g_ref = f32[256,256]{1,0:T(8,128)S(1)} custom-call(f32[8,128]{1,0:T(8,128)S(1)} %get-tuple-element.22.after_ref.pl_ref, f32[16,256]{1,0:T(8,128)S(1)} %get-tuple-element.16.wet_ref, f32[256,256]{1,0:T(8,128)S(1)} %copy-done.1, f32[3,256,256]{2,1,0:T(8,128)S(1)} %copy-done, f32[7,256,256]{2,1,0:T(8,128)S(1)} %get-tuple-element.24.scr), custom_call_target="tpu_custom_call" | custom-call | flops 20000000 | bytes 2500000 | tf_op jit(solution)/shard_map/backward/pallas_call | solution.py:489
  18.2 0.0 collective-permute-done.2.xb_ref
  18.2 0.0 collective-permute-done.3.xa_ref
  18.2 0.0 copy-done.4
  18.2 0.0 copy-done.5
  18.3 2.4 %rim.1 = (f32[256,256]{1,0:T(8,128)}, f32[256,256]{1,0:T(8,128)}, f32[256,256]{1,0:T(8,128)}) custom-call(f32[32,256]{1,0:T(8,128)S(1)} %collective-permute-done.yb_ref, f32[32,256]{1,0:T(8,128)S(1)} %collective-permute-done.1.ya_ref, f32[40,256]{1,0:T(8,128)S(1)} %collective-permute-done.2.xb_ref, f32[40,256]{1,0:T(8,128)S(1)} %collective-permute-done.3.xa_ref, ...), custom_call_target="tpu_custom_call" | custom-call | tf_op jit(solution)/shard_map/rim/pallas_call | solution.py:499
Async XLA Ops:
  0.6 6.3 %copy-start.2 = (f32[3,256,256]{2,1,0:T(8,128)S(1)}, f32[3,256,256]{2,1,0:T(8,128)}, u32[]{:S(2)}) copy-start(f32[3,256,256]{2,1,0:T(8,128)} %w_ref.1) | copy-start | bytes 2359300
  0.6 6.3 %copy-start.3 = (f32[256,256]{1,0:T(8,128)S(1)}, f32[256,256]{1,0:T(8,128)}, u32[]{:S(2)}) copy-start(f32[256,256]{1,0:T(8,128)} %z_ref.1) | copy-start | bytes 786436
  0.7 6.3 %copy-start.1 = (f32[256,256]{1,0:T(8,128)S(1)}, f32[256,256]{1,0:T(8,128)}, u32[]{:S(2)}) copy-start(f32[256,256]{1,0:T(8,128)} %lr_ref.5) | copy-start | bytes 786436
  0.7 6.3 %copy-start = (f32[3,256,256]{2,1,0:T(8,128)S(1)}, f32[3,256,256]{2,1,0:T(8,128)}, u32[]{:S(2)}) copy-start(f32[3,256,256]{2,1,0:T(8,128)} %c_ref.3) | copy-start | bytes 2359300
  1.8 8.3 %collective-permute-start = (f32[32,256]{1,0:T(8,128)S(1)}, f32[32,256]{1,0:T(8,128)S(1)}, u32[]{:S(2)}, u32[]{:S(2)}) collective-permute-start(f32[32,256]{1,0:T(8,128)S(1)} %get-tuple-element.14), channel_id=1, source_target_pairs={{0,0},{1,2},{2,1},{3,4},{4,3},{5,6},{6,5},{7,7},{8,8},{9,10},{10,9... | collective-permute-start | bytes 98312 | tf_op jit(solution)/shard_map/ppermute | solution.py:470
  6.8 3.2 %collective-permute-start.1 = (f32[32,256]{1,0:T(8,128)S(1)}, f32[32,256]{1,0:T(8,128)S(1)}, u32[]{:S(2)}, u32[]{:S(2)}) collective-permute-start(f32[32,256]{1,0:T(8,128)S(1)} %get-tuple-element.15), channel_id=1, source_target_pairs={{0,1},{1,0},{2,3},{3,2},{4,5},{5,4},{6,7},{7,6},{8,9},{9,8},{10,11... | collective-permute-start | bytes 98312 | tf_op jit(solution)/shard_map/ppermute | solution.py:471
  8.6 9.6 %copy-start.4 = (f32[256,256]{1,0:T(8,128)S(1)}, f32[256,256]{1,0:T(8,128)}, u32[]{:S(2)}) copy-start(f32[256,256]{1,0:T(8,128)} %m_ref.1) | copy-start | bytes 786436
  8.6 9.6 %copy-start.5 = (f32[256,256]{1,0:T(8,128)S(1)}, f32[256,256]{1,0:T(8,128)}, u32[]{:S(2)}) copy-start(f32[256,256]{1,0:T(8,128)} %v_ref.1) | copy-start | bytes 786436
  10.1 8.1 %collective-permute-start.2 = (f32[40,256]{1,0:T(8,128)S(1)}, f32[40,256]{1,0:T(8,128)S(1)}, u32[]{:S(2)}, u32[]{:S(2)}) collective-permute-start(f32[40,256]{1,0:T(8,128)S(1)} %get-tuple-element.19), channel_id=1, source_target_pairs={{0,0},{8,16},{16,8},{24,32},{32,24},{40,48},{48,40},{56,64},{64,56... | collective-permute-start | bytes 122888 | tf_op jit(solution)/shard_map/ppermute | solution.py:496
  15.6 2.6 %collective-permute-start.3 = (f32[40,256]{1,0:T(8,128)S(1)}, f32[40,256]{1,0:T(8,128)S(1)}, u32[]{:S(2)}, u32[]{:S(2)}) collective-permute-start(f32[40,256]{1,0:T(8,128)S(1)} %get-tuple-element.20), channel_id=1, source_target_pairs={{0,8},{8,0},{16,24},{24,16},{32,40},{40,32},{48,56},{56,48},{64,72... | collective-permute-start | bytes 122888 | tf_op jit(solution)/shard_map/ppermute | solution.py:497

commit v4 on v3

--- a/solution.py
+++ b/solution.py
@@ -1,4 +1,3 @@
-import functools
 import math
 
 import jax
@@ -300,13 +299,14 @@
     last_passes(get, lambda j: tile_wet(wet_ref, j, n), n, scr, shifted, across, put_grad)
 
 
-def pack_cols_kernel(yb_ref, ya_ref, tl_ref, tr_ref, b_ref, a_ref, pl_ref, pr_ref, k_scr):
+def pack_cols_kernel(yb_ref, ya_ref, yw_ref, tl_ref, tr_ref, b_ref, a_ref, pl_ref, pr_ref, k_scr):
     gx, nx = place("gx")
-    gy, _ = place("gy")
+    gy, ny = place("gy")
     even_y = gy % 2 == 0
     lanes = ya_ref.shape[1]
-    below = jnp.where(even_y, ya_ref[...], yb_ref[...])
-    above = jnp.where(even_y, yb_ref[...], ya_ref[...])
+    y_b = jnp.where((gy == 0) | (gy == ny - 1), yw_ref[...], yb_ref[...])
+    below = jnp.where(even_y, ya_ref[...], y_b)
+    above = jnp.where(even_y, y_b, ya_ref[...])
     lane = lax.broadcasted_iota(jnp.int32, (above.shape[0], 128), 1)
     above = jnp.where(lane < 64, above[:, 0:128], above[:, lanes - 128 : lanes])
     below = jnp.where(lane < 64, below[:, 0:128], below[:, lanes - 128 : lanes])
@@ -366,24 +366,26 @@
 
 
 def rim_kernel(
-    yb_ref, ya_ref, xb_ref, xa_ref, rs_ref, tl_ref, tr_ref, pl_ref, pr_ref, g_ref, lr_ref, m_ref, v_ref,
+    yb_ref, ya_ref, yw_ref, xb_ref, xa_ref, xw_ref, rs_ref, tl_ref, tr_ref, pl_ref, pr_ref, g_ref, lr_ref, m_ref, v_ref,
     nr_ref, nm_ref, nv_ref, row_s, col_s, row_scr, col_scr, row_sh, col_sh, row_ac, col_ac, row_g, col_g, turn_scr, side_scr,
 ):
     gx, nx = place("gx")
-    gy, _ = place("gy")
+    gy, ny = place("gy")
     even_x, even_y = gx % 2 == 0, gy % 2 == 0
+    at_wall_x, at_wall_y = (gx == 0) | (gx == nx - 1), (gy == 0) | (gy == ny - 1)
     height, lanes = lr_ref.shape
     for f in range(NF):
         r = slice(3 * f, 3 * f + 3)
-        ya, yb = ya_ref[r, :], yb_ref[r, :]
+        ya, yb = ya_ref[r, :], jnp.where(at_wall_y, yw_ref[r, :], yb_ref[r, :])
         row_s[f, 0:8, :] = jnp.ones((8, lanes), jnp.float32)
         row_s[f, 24:32, :] = jnp.ones((8, lanes), jnp.float32)
         row_s[f, 5:8, :] = jnp.where(even_y, yb, ya)
         row_s[f, 24:27, :] = jnp.where(even_y, ya, yb)
         row_s[f, 8:24, :] = rs_ref[f]
     strip_gradient(row_s, row_scr, row_sh, row_ac, row_g)
-    left_in = jnp.where(even_x, xb_ref[...], xa_ref[...])
-    right_in = jnp.where(even_x, xa_ref[...], xb_ref[...])
+    x_b = jnp.where(at_wall_x, xw_ref[...], xb_ref[...])
+    left_in = jnp.where(even_x, x_b, xa_ref[...])
+    right_in = jnp.where(even_x, xa_ref[...], x_b)
     for f, t in enumerate(TURNED):
         shift = (125 - 6 * f) % 128
         r = slice(3 * f, 3 * f + 3)
@@ -427,15 +429,29 @@
     update(slice(height - 16, height), lambda g: jnp.where(row >= 13, row_g[8:24, :], g))
 
 
-def swap_pairs(n, odd):
+def swap_pairs(nx, ny, axis, odd):
     pairs = []
-    for i in range(n):
-        j = i ^ 1 if not odd else ((i + 1) ^ 1) - 1
-        pairs.append((i, j if 0 <= j < n else i))
+    for x in range(nx):
+        for y in range(ny):
+            u, v = x, y
+            if axis == "gx":
+                u = x ^ 1 if not odd else ((x + 1) ^ 1) - 1
+                if not 0 <= u < nx:
+                    u, v = x, y ^ 1
+            else:
+                v = y ^ 1 if not odd else ((y + 1) ^ 1) - 1
+                if not 0 <= v < ny:
+                    u, v = x ^ 1, y
+            pairs.append((x * ny + y, u * ny + v))
     return pairs
 
 
-def call(kernel, out_shapes, scratch=(), in_specs=None, flops=0, name=None, vmem_mb=VMEM_MB):
+def swapped(value, axis, odd):
+    pairs = swap_pairs(lax.axis_size("gx"), lax.axis_size("gy"), axis, odd)
+    return lax.ppermute(value, ("gx", "gy"), pairs)
+
+
+def call(kernel, out_shapes, scratch=(), in_specs=None, flops=0, vmem_mb=VMEM_MB):
     params = pltpu.CompilerParams(vmem_limit_bytes=vmem_mb << 20)
     shapes = [jax.ShapeDtypeStruct(s, jnp.float32) for s in out_shapes]
     kwargs = {} if in_specs is None else {"in_specs": in_specs}
@@ -445,7 +461,6 @@
         scratch_shapes=list(scratch),
         compiler_params=params,
         cost_estimate=pl.CostEstimate(flops=flops, bytes_accessed=flops // 8, transcendentals=0),
-        name=name,
         **kwargs,
     )
 
@@ -463,12 +478,9 @@
             pltpu.SemaphoreType.DMA((9,)),
         ],
         in_specs=[hbm] * 5,
-        name="pack_rows",
         vmem_mb=12,
     )(*(pltpu.with_memory_space_constraint(x, pltpu.HBM) for x in (wet_tiles, water, ground, rough, cot)))
-    ny, nx = lax.axis_size("gy"), lax.axis_size("gx")
-    y_b = lax.ppermute(y_b, "gy", swap_pairs(ny, True))
-    y_a = lax.ppermute(y_a, "gy", swap_pairs(ny, False))
+    y_wall, y_b, y_a = y_b, swapped(y_b, "gy", True), swapped(y_a, "gy", False)
     scratch = [
         pltpu.VMEM((N_SHIFTED, lanes // 128, height + 16, 128), jnp.float32),
         pltpu.VMEM((N_ACROSS, height, lanes), jnp.float32),
@@ -478,23 +490,16 @@
         [(N_AHEAD, height, lanes), (NF, 16, lanes), (NF, 8, height), (NF, 8, height)],
         scratch=scratch,
         flops=20_000_000,
-        name="forward",
     )(wet, water, ground, rough, cot)
     x_b, x_a, corner_left, corner_right = call(
         pack_cols_kernel,
         [(40, height), (40, height), (8, 128), (8, 128)],
         scratch=[pltpu.VMEM((128, 128), jnp.float32)],
-        name="pack_cols",
-    )(y_b, y_a, col_left, col_right)
+    )(y_b, y_a, y_wall, col_left, col_right)
     (grad,) = call(
-        backward_kernel,
-        [(height, lanes)],
-        scratch=scratch,
-        flops=20_000_000,
-        name="backward",
+        backward_kernel, [(height, lanes)], scratch=scratch, flops=20_000_000
     )(corner_left, wet, rough, cot, ahead)
-    x_b = lax.ppermute(x_b, "gx", swap_pairs(nx, True))
-    x_a = lax.ppermute(x_a, "gx", swap_pairs(nx, False))
+    x_wall, x_b, x_a = x_b, swapped(x_b, "gx", True), swapped(x_a, "gx", False)
     return tuple(
         call(
             rim_kernel,
@@ -513,9 +518,8 @@
                 pltpu.VMEM((128, height), jnp.float32),
                 pltpu.VMEM((height, 128), jnp.float32),
             ],
-            name="rim",
         )(
-            y_b, y_a, x_b, x_a, row_own, col_left, col_right, corner_left, corner_right,
+            y_b, y_a, y_wall, x_b, x_a, x_wall, row_own, col_left, col_right, corner_left, corner_right,
             grad, rough, moment, second,
         )
     )
@@ -524,6 +528,7 @@
 def solution(mesh):
     flat = P("gy", "gx")
     deep = P(None, "gy", "gx")
+
     return jax.shard_map(
         on_device,
         mesh=mesh,

time: 20.8 us -> 18.9 us (0.909)
  starting transfers between devices: 10.7 us -> 7.75 us
  waiting for transfers between devices: 1.41 us -> 2.5 us
    ppermute x4, starting transfers between devices: 10.7 us -> 7.75 us  [swapped(): return lax.ppermute(value, ('gx', 'gy'), pairs)]
    ppermute x4, waiting for transfers between devices: 1.41 us -> 2.5 us  [swapped(): return lax.ppermute(value, ('gx', 'gy'), pairs)]
  transfers between devices with their start and end apart: 4 -> 4, of which waited for: 1 -> 2; matrix products, arithmetic and copies ran while one was open for 0% -> 0% of each run, Pallas kernels for 20% -> 22%
where the time goes in v4:
time: 18.9 us; the launch traced here: 18.7 us
  starting transfers between devices  7.75 us (41%)
  Pallas kernels  7.72 us (41%)
  waiting for transfers between devices  2.5 us (13%)
  between operations  0.74 us (4%)
    ppermute x4, starting transfers between devices, swapped(): return lax.ppermute(value, ('gx', 'gy'), pairs)  7.75 us
    pallas_call x1, Pallas kernels, on_device(): call(backward_kernel, [(height, lanes)], scratch=scratch, flops=20000000)  2.52 us
    ppermute x4, waiting for transfers between devices, swapped(): return lax.ppermute(value, ('gx', 'gy'), pairs)  2.5 us
    pallas_call x1, Pallas kernels, on_device(): call(rim_kernel, [(height, lanes)] * 3, scratch=[pltpu.VMEM((NF, 32, lane...  2.35 us
    pallas_call x1, Pallas kernels, on_device(): call(forward_kernel, [(N_AHEAD, height, lanes), (NF, 16, lanes), (NF, 8,...  1.64 us
    pallas_call x1, Pallas kernels, on_device(): call(pack_rows_kernel, [(32, lanes), (32, lanes), (16, lanes)], scratch=[...  1.08 us
  transfers between devices with their start and end apart: 4, of which 2 were waited for; matrix products, arithmetic and copies ran while one was open for 0% of the time, Pallas kernels for 22%

profile of v4, /device:TPU:57, one launch (start us, length us, event | category | flops | bytes accessed | tf_op | source)
XLA Modules:
  0.0 18.7 jit_solution(6952598435908371382)
XLA Ops:
  0.6 0.0 copy-start.1
  0.6 0.0 copy-start
  0.7 0.0 copy-start.3
  0.7 0.0 copy-start.2
  0.7 1.1 %shard_map.94 = (f32[32,256]{1,0:T(8,128)S(1)}, f32[32,256]{1,0:T(8,128)S(1)}, f32[16,256]{1,0:T(8,128)S(1)}) custom-call(s32[2,2]{1,0:T(2,128)} %wet_hbm.1, f32[3,256,256]{2,1,0:T(8,128)} %w_ref.1, f32[256,256]{1,0:T(8,128)} %z_ref.1, f32[256,256]{1,0:T(8,128)} %lr_ref.5, f32[3,256,256]{2,1,0:T(8,128)} %c_ref.3), custom_call_target="tpu_custom_call" | custom-call | tf_op jit(solution)/shard_map/pallas_call | solution.py:471
  1.8 1.3 %collective-permute-start.1 = (f32[32,256]{1,0:T(8,128)S(1)}, f32[32,256]{1,0:T(8,128)S(1)}, u32[]{:S(2)}, u32[]{:S(2)}) collective-permute-start(f32[32,256]{1,0:T(8,128)S(1)} %get-tuple-element.15), channel_id=1, source_target_pairs={{0,1},{1,0},{2,3},{3,2},{4,5},{5,4},{6,7},{7,6},{8,9},{9,8},{10,11... | collective-permute-start | bytes 98312 | tf_op jit(solution)/shard_map/ppermute | solution.py:451
  3.1 2.5 %collective-permute-start = (f32[32,256]{1,0:T(8,128)S(1)}, f32[32,256]{1,0:T(8,128)S(1)}, u32[]{:S(2)}, u32[]{:S(2)}) collective-permute-start(f32[32,256]{1,0:T(8,128)S(1)} %get-tuple-element.14.yw_ref), channel_id=1, source_target_pairs={{0,8},{1,2},{2,1},{3,4},{4,3},{5,6},{6,5},{7,15},{8,0},{9,10},{10,... | collective-permute-start | bytes 98312 | tf_op jit(solution)/shard_map/ppermute | solution.py:451
  5.5 0.0 copy-done.1
  5.5 0.0 copy-done
  5.5 0.0 copy-done.3
  5.5 0.0 copy-done.2
  5.6 1.6 %shard_map.95 = (f32[7,256,256]{2,1,0:T(8,128)S(1)}, f32[9,16,256]{2,1,0:T(8,128)S(1)}, f32[9,8,256]{2,1,0:T(8,128)S(1)}, f32[9,8,256]{2,1,0:T(8,128)S(1)}) custom-call(f32[16,256]{1,0:T(8,128)S(1)} %get-tuple-element.16.wet_ref, f32[3,256,256]{2,1,0:T(8,128)S(1)} %copy-done.2, f32[256,256]{1,0:T(8,128)S(1)} %copy-done.3, f32[256,256]{1,0:T(8,128)S(1)} %copy-done.1, ...), custom_call_target="tpu_custom_call" | custom-call | flops 20000000 | bytes 2500000 | tf_op jit(solution)/shard_map/pallas_call | solution.py:488
  7.2 0.0 copy-start.4
  7.2 0.0 copy-start.5
  7.2 0.0 collective-permute-done.1.ya_ref
  7.2 2.2 %collective-permute-done.yb_ref = f32[32,256]{1,0:T(8,128)S(1)} collective-permute-done((f32[32,256]{1,0:T(8,128)S(1)}, f32[32,256]{1,0:T(8,128)S(1)}, u32[]{:S(2)}, u32[]{:S(2)}) %collective-permute-start) | collective-permute-done | bytes 32800 | tf_op jit(solution)/shard_map/ppermute | solution.py:451
  9.4 0.1 shard_map.96
  9.6 2.2 %collective-permute-start.3 = (f32[40,256]{1,0:T(8,128)S(1)}, f32[40,256]{1,0:T(8,128)S(1)}, u32[]{:S(2)}, u32[]{:S(2)}) collective-permute-start(f32[40,256]{1,0:T(8,128)S(1)} %get-tuple-element.20), channel_id=1, source_target_pairs={{0,8},{1,9},{2,10},{3,11},{4,12},{5,13},{6,14},{7,15},{8,0},{9,1},... | collective-permute-start | bytes 122888 | tf_op jit(solution)/shard_map/ppermute | solution.py:451
  11.8 1.8 %collective-permute-start.2 = (f32[40,256]{1,0:T(8,128)S(1)}, f32[40,256]{1,0:T(8,128)S(1)}, u32[]{:S(2)}, u32[]{:S(2)}) collective-permute-start(f32[40,256]{1,0:T(8,128)S(1)} %get-tuple-element.19.xw_ref), channel_id=1, source_target_pairs={{0,1},{1,0},{2,3},{3,2},{4,5},{5,4},{6,7},{7,6},{8,16},{9,17},{10,... | collective-permute-start | bytes 122888 | tf_op jit(solution)/shard_map/ppermute | solution.py:451
  13.6 2.5 %shard_map.97.g_ref = f32[256,256]{1,0:T(8,128)S(1)} custom-call(f32[8,128]{1,0:T(8,128)S(1)} %get-tuple-element.22.after_ref.pl_ref, f32[16,256]{1,0:T(8,128)S(1)} %get-tuple-element.16.wet_ref, f32[256,256]{1,0:T(8,128)S(1)} %copy-done.1, f32[3,256,256]{2,1,0:T(8,128)S(1)} %copy-done, f32[7,256,256]{2,1,0:T(8,128)S(1)} %get-tuple-element.24.scr), custom_call_target="tpu_custom_call" | custom-call | flops 20000000 | bytes 2500000 | tf_op jit(solution)/shard_map/pallas_call | solution.py:499
  16.1 0.0 collective-permute-done.3.xa_ref
  16.1 0.3 %collective-permute-done.2.xb_ref = f32[40,256]{1,0:T(8,128)S(1)} collective-permute-done((f32[40,256]{1,0:T(8,128)S(1)}, f32[40,256]{1,0:T(8,128)S(1)}, u32[]{:S(2)}, u32[]{:S(2)}) %collective-permute-start.2) | collective-permute-done | bytes 40992 | tf_op jit(solution)/shard_map/ppermute | solution.py:451
  16.4 0.0 copy-done.4
  16.4 0.0 copy-done.5
  16.4 2.4 %shard_map.98 = (f32[256,256]{1,0:T(8,128)}, f32[256,256]{1,0:T(8,128)}, f32[256,256]{1,0:T(8,128)}) custom-call(f32[32,256]{1,0:T(8,128)S(1)} %collective-permute-done.yb_ref, f32[32,256]{1,0:T(8,128)S(1)} %collective-permute-done.1.ya_ref, f32[32,256]{1,0:T(8,128)S(1)} %get-tuple-element.14.yw_ref, f32[40,256]{1,0:T(8,128)S(1)} %collective-permute-done.2.xb_ref, ...), custom_call_target="tpu_custom_call" | custom-call | tf_op jit(solution)/shard_map/pallas_call | solution.py:504
Async XLA Ops:
  0.6 4.9 %copy-start.1 = (f32[256,256]{1,0:T(8,128)S(1)}, f32[256,256]{1,0:T(8,128)}, u32[]{:S(2)}) copy-start(f32[256,256]{1,0:T(8,128)} %lr_ref.5) | copy-start | bytes 786436
  0.6 4.9 %copy-start = (f32[3,256,256]{2,1,0:T(8,128)S(1)}, f32[3,256,256]{2,1,0:T(8,128)}, u32[]{:S(2)}) copy-start(f32[3,256,256]{2,1,0:T(8,128)} %c_ref.3) | copy-start | bytes 2359300
  0.7 4.9 %copy-start.3 = (f32[256,256]{1,0:T(8,128)S(1)}, f32[256,256]{1,0:T(8,128)}, u32[]{:S(2)}) copy-start(f32[256,256]{1,0:T(8,128)} %z_ref.1) | copy-start | bytes 786436
  0.7 4.9 %copy-start.2 = (f32[3,256,256]{2,1,0:T(8,128)S(1)}, f32[3,256,256]{2,1,0:T(8,128)}, u32[]{:S(2)}) copy-start(f32[3,256,256]{2,1,0:T(8,128)} %w_ref.1) | copy-start | bytes 2359300
  1.8 5.5 %collective-permute-start.1 = (f32[32,256]{1,0:T(8,128)S(1)}, f32[32,256]{1,0:T(8,128)S(1)}, u32[]{:S(2)}, u32[]{:S(2)}) collective-permute-start(f32[32,256]{1,0:T(8,128)S(1)} %get-tuple-element.15), channel_id=1, source_target_pairs={{0,1},{1,0},{2,3},{3,2},{4,5},{5,4},{6,7},{7,6},{8,9},{9,8},{10,11... | collective-permute-start | bytes 98312 | tf_op jit(solution)/shard_map/ppermute | solution.py:451
  3.1 6.4 %collective-permute-start = (f32[32,256]{1,0:T(8,128)S(1)}, f32[32,256]{1,0:T(8,128)S(1)}, u32[]{:S(2)}, u32[]{:S(2)}) collective-permute-start(f32[32,256]{1,0:T(8,128)S(1)} %get-tuple-element.14.yw_ref), channel_id=1, source_target_pairs={{0,8},{1,2},{2,1},{3,4},{4,3},{5,6},{6,5},{7,15},{8,0},{9,10},{10,... | collective-permute-start | bytes 98312 | tf_op jit(solution)/shard_map/ppermute | solution.py:451
  7.2 9.2 %copy-start.4 = (f32[256,256]{1,0:T(8,128)S(1)}, f32[256,256]{1,0:T(8,128)}, u32[]{:S(2)}) copy-start(f32[256,256]{1,0:T(8,128)} %m_ref.1) | copy-start | bytes 786436
  7.2 9.2 %copy-start.5 = (f32[256,256]{1,0:T(8,128)S(1)}, f32[256,256]{1,0:T(8,128)}, u32[]{:S(2)}) copy-start(f32[256,256]{1,0:T(8,128)} %v_ref.1) | copy-start | bytes 786436
  9.6 6.5 %collective-permute-start.3 = (f32[40,256]{1,0:T(8,128)S(1)}, f32[40,256]{1,0:T(8,128)S(1)}, u32[]{:S(2)}, u32[]{:S(2)}) collective-permute-start(f32[40,256]{1,0:T(8,128)S(1)} %get-tuple-element.20), channel_id=1, source_target_pairs={{0,8},{1,9},{2,10},{3,11},{4,12},{5,13},{6,14},{7,15},{8,0},{9,1},... | collective-permute-start | bytes 122888 | tf_op jit(solution)/shard_map/ppermute | solution.py:451
  11.8 4.6 %collective-permute-start.2 = (f32[40,256]{1,0:T(8,128)S(1)}, f32[40,256]{1,0:T(8,128)S(1)}, u32[]{:S(2)}, u32[]{:S(2)}) collective-permute-start(f32[40,256]{1,0:T(8,128)S(1)} %get-tuple-element.19.xw_ref), channel_id=1, source_target_pairs={{0,1},{1,0},{2,3},{3,2},{4,5},{5,4},{6,7},{7,6},{8,16},{9,17},{10,... | collective-permute-start | bytes 122888 | tf_op jit(solution)/shard_map/ppermute | solution.py:451

commit v5 on v4

--- a/solution.py
+++ b/solution.py
@@ -143,7 +143,7 @@
     looped(n, finish)
 
 
-def last_passes(get, wet, n, scr, shifted, across, put_grad):
+def second_pass(get, wet, n, scr, shifted, across):
     def parts(j):
         r = rows(j)
         cols, down, up, u, v = flux_parts(*(scr[f, r, :] for f in (UH, UX, UY, SX, SY)))
@@ -179,6 +179,8 @@
 
     looped(n, finish_all)
 
+
+def third_pass(n, scr, shifted, across, put_grad):
     def back(j):
         r = rows(j)
 
@@ -258,7 +260,7 @@
     return wet_ref[rows(j // (n // 2)), :] > 0.5
 
 
-def forward_kernel(wet_ref, w_ref, z_ref, lr_ref, c_ref, scr, rs_ref, tl_ref, tr_ref, shifted, across):
+def forward_kernel(wet_ref, w_ref, z_ref, lr_ref, c_ref, scr, shifted, across, rs_ref, tl_ref, tr_ref):
     height, lanes = z_ref.shape
     n = height // BLK
 
@@ -271,6 +273,7 @@
         return field(f)[rows(j), :]
 
     first_pass(get, lambda j: tile_wet(wet_ref, j, n), n, scr, shifted, across)
+    second_pass(get, lambda j: tile_wet(wet_ref, j, n), n, scr, shifted, across)
     lane = lax.broadcasted_iota(jnp.int32, (height, 128), 1)
     for f in range(WET):
         ref = field(f)
@@ -287,16 +290,80 @@
     tr_ref[WET] = jnp.concatenate([top[:, half:], bottom[:, half:]], 1)
 
 
-def backward_kernel(after_ref, wet_ref, lr_ref, c_ref, scr, g_ref, shifted, across):
-    n = lr_ref.shape[0] // BLK
+def strip_gradient(s_ref, scr, shifted, across, g_ref):
+    n = s_ref.shape[1] // BLK
 
     def get(f, j):
-        return (lr_ref if f == LR else c_ref.at[f - CH])[rows(j), :]
+        return s_ref[f, rows(j), :]
+
+    def wet(j):
+        return get(WET, j) > 0.5
 
     def put_grad(j, value):
         g_ref[rows(j), :] = value
 
-    last_passes(get, lambda j: tile_wet(wet_ref, j, n), n, scr, shifted, across, put_grad)
+    first_pass(get, wet, n, scr, shifted, across)
+    second_pass(get, wet, n, scr, shifted, across)
+    third_pass(n, scr, shifted, across, put_grad)
+
+
+def arctan_ratio(y, x):
+    a = jnp.abs(y)
+    big, small = jnp.maximum(a, x), jnp.minimum(a, x)
+    far = small > 0.41421356 * big
+    t = jnp.where(far, small - big, small) / jnp.where(far, small + big, big)
+    z = t * t
+    p = ((8.05374449538e-2 * z - 1.38776856032e-1) * z + 1.99777106478e-1) * z - 3.33329491539e-1
+    r = p * z * t + t + jnp.where(far, math.pi / 4, 0.0)
+    r = jnp.where(a > x, math.pi / 2 - r, r)
+    return jnp.where(y < 0, -r, r)
+
+
+def updated(g, rough, moment, second):
+    nm = BETA_ONE * moment + (1.0 - BETA_ONE) * g
+    nv = BETA_TWO * second + (1.0 - BETA_TWO) * g * g
+    root = jnp.sqrt(nv * (1.0 / (1.0 - BETA_TWO**UPDATES)))
+    turn = arctan_ratio(nm * (1.0 / (1.0 - BETA_ONE**UPDATES)), root)
+    return rough - (LEARN_RATE * ATAN_SCALE) * turn, nm, nv
+
+
+def backward_kernel(
+    after_ref, ya_ref, yb_ref, yw_ref, rs_ref, scr, shifted, across, lr_ref, m_ref, v_ref,
+    nr_ref, nm_ref, nv_ref, ml_ref, mr_ref, g_ref, row_s, row_scr, row_sh, row_ac, row_g,
+):
+    gy, ny = place("gy")
+    even_y, at_wall_y = gy % 2 == 0, (gy == 0) | (gy == ny - 1)
+    height, lanes = lr_ref.shape
+
+    def put_grad(j, value):
+        g_ref[rows(j), :] = value
+
+    third_pass(height // BLK, scr, shifted, across, put_grad)
+    for f in range(NF):
+        r = slice(3 * f, 3 * f + 3)
+        ya, yb = ya_ref[r, :], jnp.where(at_wall_y, yw_ref[r, :], yb_ref[r, :])
+        row_s[f, 0:8, :] = jnp.ones((8, lanes), jnp.float32)
+        row_s[f, 24:32, :] = jnp.ones((8, lanes), jnp.float32)
+        row_s[f, 5:8, :] = jnp.where(even_y, yb, ya)
+        row_s[f, 24:27, :] = jnp.where(even_y, ya, yb)
+        row_s[f, 8:24, :] = rs_ref[f]
+    strip_gradient(row_s, row_scr, row_sh, row_ac, row_g)
+    row = lax.broadcasted_iota(jnp.int32, (8, lanes), 0)
+    g_ref[0:8, :] = jnp.where(row < 3, row_g[8:16, :], g_ref[0:8, :])
+    g_ref[height - 8 : height, :] = jnp.where(row >= 5, row_g[16:24, :], g_ref[height - 8 : height, :])
+
+    def update(j):
+        r = rows(j)
+        nr_ref[r, :], nm_ref[r, :], nv_ref[r, :] = updated(
+            g_ref[r, :], lr_ref[r, :], m_ref[r, :], v_ref[r, :]
+        )
+
+    looped(height // BLK, update)
+    lane = lax.broadcasted_iota(jnp.int32, (height, 128), 1)
+    for f, ref in enumerate((m_ref, v_ref)):
+        turned = jnp.where(lane < 64, ref[:, 0:128], ref[:, lanes - 128 : lanes]).T
+        ml_ref[f] = turned[0:8, :]
+        mr_ref[f] = turned[120:128, :]
 
 
 def pack_cols_kernel(yb_ref, ya_ref, yw_ref, tl_ref, tr_ref, b_ref, a_ref, pl_ref, pr_ref, k_scr):
@@ -337,52 +404,13 @@
     b_ref[32:35, 0:128] = jnp.where(even, t, b)
 
 
-def strip_gradient(s_ref, scr, shifted, across, g_ref):
-    n = s_ref.shape[1] // BLK
-
-    def get(f, j):
-        return s_ref[f, rows(j), :]
-
-    def wet(j):
-        return get(WET, j) > 0.5
-
-    def put_grad(j, value):
-        g_ref[rows(j), :] = value
-
-    first_pass(get, wet, n, scr, shifted, across)
-    last_passes(get, wet, n, scr, shifted, across, put_grad)
-
-
-def arctan_ratio(y, x):
-    a = jnp.abs(y)
-    big, small = jnp.maximum(a, x), jnp.minimum(a, x)
-    far = small > 0.41421356 * big
-    t = jnp.where(far, small - big, small) / jnp.where(far, small + big, big)
-    z = t * t
-    p = ((8.05374449538e-2 * z - 1.38776856032e-1) * z + 1.99777106478e-1) * z - 3.33329491539e-1
-    r = p * z * t + t + jnp.where(far, math.pi / 4, 0.0)
-    r = jnp.where(a > x, math.pi / 2 - r, r)
-    return jnp.where(y < 0, -r, r)
-
-
 def rim_kernel(
-    yb_ref, ya_ref, yw_ref, xb_ref, xa_ref, xw_ref, rs_ref, tl_ref, tr_ref, pl_ref, pr_ref, g_ref, lr_ref, m_ref, v_ref,
-    nr_ref, nm_ref, nv_ref, row_s, col_s, row_scr, col_scr, row_sh, col_sh, row_ac, col_ac, row_g, col_g, turn_scr, side_scr,
+    xa_ref, xb_ref, xw_ref, tl_ref, tr_ref, pl_ref, pr_ref, ml_ref, mr_ref, ir_ref, im_ref, iv_ref,
+    nr_ref, nm_ref, nv_ref, col_s, col_scr, col_sh, col_ac, col_g, turn_scr,
 ):
     gx, nx = place("gx")
-    gy, ny = place("gy")
-    even_x, even_y = gx % 2 == 0, gy % 2 == 0
-    at_wall_x, at_wall_y = (gx == 0) | (gx == nx - 1), (gy == 0) | (gy == ny - 1)
-    height, lanes = lr_ref.shape
-    for f in range(NF):
-        r = slice(3 * f, 3 * f + 3)
-        ya, yb = ya_ref[r, :], jnp.where(at_wall_y, yw_ref[r, :], yb_ref[r, :])
-        row_s[f, 0:8, :] = jnp.ones((8, lanes), jnp.float32)
-        row_s[f, 24:32, :] = jnp.ones((8, lanes), jnp.float32)
-        row_s[f, 5:8, :] = jnp.where(even_y, yb, ya)
-        row_s[f, 24:27, :] = jnp.where(even_y, ya, yb)
-        row_s[f, 8:24, :] = rs_ref[f]
-    strip_gradient(row_s, row_scr, row_sh, row_ac, row_g)
+    even_x, at_wall_x = gx % 2 == 0, (gx == 0) | (gx == nx - 1)
+    height, lanes = ir_ref.shape
     x_b = jnp.where(at_wall_x, xw_ref[...], xb_ref[...])
     left_in = jnp.where(even_x, x_b, xa_ref[...])
     right_in = jnp.where(even_x, xa_ref[...], x_b)
@@ -400,33 +428,16 @@
         col_s[t, 8:16, height:] = pltpu.roll(pl_ref[...], shift, 1)
         col_s[t, 16:24, height:] = pltpu.roll(pr_ref[...], shift, 1)
     strip_gradient(col_s, col_scr, col_sh, col_ac, col_g)
-    turn_scr[...] = jnp.zeros_like(turn_scr)
-    turn_scr[0:8, :] = col_g[8:16, 0:height]
-    turn_scr[120:128, :] = col_g[16:24, 0:height]
-    side_scr[...] = turn_scr[...].T
-    lane = lax.broadcasted_iota(jnp.int32, (16, lanes), 1)
-    beside = (lane < 3) | (lane >= lanes - 3)
-
-    def update(r, rim):
-        g = rim(g_ref[r, :])
-        side = side_scr[r, :]
-        g = jnp.where(beside, jnp.concatenate([side] * (lanes // 128), 1), g)
-        nm = BETA_ONE * m_ref[r, :] + (1.0 - BETA_ONE) * g
-        nv = BETA_TWO * v_ref[r, :] + (1.0 - BETA_TWO) * g * g
-        nm_ref[r, :] = nm
-        nv_ref[r, :] = nv
-        root = jnp.sqrt(nv * (1.0 / (1.0 - BETA_TWO**UPDATES)))
-        turn = arctan_ratio(nm * (1.0 / (1.0 - BETA_ONE**UPDATES)), root)
-        nr_ref[r, :] = lr_ref[r, :] - (LEARN_RATE * ATAN_SCALE) * turn
-
-    def inside(i, carry):
-        update(pl.ds(pl.multiple_of(i * 16, 16), 16), lambda g: g)
-        return carry
-
-    row = lax.broadcasted_iota(jnp.int32, (16, lanes), 0)
-    update(slice(0, 16), lambda g: jnp.where(row < 3, row_g[8:24, :], g))
-    lax.fori_loop(1, height // 16 - 1, inside, 0)
-    update(slice(height - 16, height), lambda g: jnp.where(row >= 13, row_g[8:24, :], g))
+    turn_scr[:, 8:120, :] = jnp.zeros((3, 112, height), jnp.float32)
+    for r, g, t_ref, s_ref in ((slice(0, 8), 8, tl_ref, ml_ref), (slice(120, 128), 16, tr_ref, mr_ref)):
+        new = updated(col_g[g : g + 8, 0:height], t_ref[LR], s_ref[0], s_ref[1])
+        for f in range(3):
+            turn_scr[f, r, :] = new[f]
+    lane = lax.broadcasted_iota(jnp.int32, (height, 128), 1)
+    for f, (src, dst) in enumerate(((ir_ref, nr_ref), (im_ref, nm_ref), (iv_ref, nv_ref))):
+        side = turn_scr[f].T
+        dst[:, 0:128] = jnp.where(lane < 3, side, src[:, 0:128])
+        dst[:, lanes - 128 : lanes] = jnp.where(lane >= 125, side, src[:, lanes - 128 : lanes])
 
 
 def swap_pairs(nx, ny, axis, odd):
@@ -481,46 +492,48 @@
         vmem_mb=12,
     )(*(pltpu.with_memory_space_constraint(x, pltpu.HBM) for x in (wet_tiles, water, ground, rough, cot)))
     y_wall, y_b, y_a = y_b, swapped(y_b, "gy", True), swapped(y_a, "gy", False)
-    scratch = [
-        pltpu.VMEM((N_SHIFTED, lanes // 128, height + 16, 128), jnp.float32),
-        pltpu.VMEM((N_ACROSS, height, lanes), jnp.float32),
+    kept = [
+        (N_AHEAD, height, lanes),
+        (N_SHIFTED, lanes // 128, height + 16, 128),
+        (N_ACROSS, height, lanes),
     ]
-    ahead, row_own, col_left, col_right = call(
-        forward_kernel,
-        [(N_AHEAD, height, lanes), (NF, 16, lanes), (NF, 8, height), (NF, 8, height)],
-        scratch=scratch,
-        flops=20_000_000,
+    scr, shifted, across, row_own, col_left, col_right = call(
+        forward_kernel, [*kept, (NF, 16, lanes), (NF, 8, height), (NF, 8, height)], flops=20_000_000
     )(wet, water, ground, rough, cot)
     x_b, x_a, corner_left, corner_right = call(
         pack_cols_kernel,
         [(40, height), (40, height), (8, 128), (8, 128)],
         scratch=[pltpu.VMEM((128, 128), jnp.float32)],
     )(y_b, y_a, y_wall, col_left, col_right)
-    (grad,) = call(
-        backward_kernel, [(height, lanes)], scratch=scratch, flops=20_000_000
-    )(corner_left, wet, rough, cot, ahead)
+    own_rough, own_moment, own_second, mom_left, mom_right = call(
+        backward_kernel,
+        [(height, lanes)] * 3 + [(2, 8, height)] * 2,
+        scratch=[
+            pltpu.VMEM((height, lanes), jnp.float32),
+            pltpu.VMEM((NF, 32, lanes), jnp.float32),
+            pltpu.VMEM((N_AHEAD, 32, lanes), jnp.float32),
+            pltpu.VMEM((N_SHIFTED, lanes // 128, 48, 128), jnp.float32),
+            pltpu.VMEM((N_ACROSS, 32, lanes), jnp.float32),
+            pltpu.VMEM((32, lanes), jnp.float32),
+        ],
+        flops=20_000_000,
+    )(corner_left, y_a, y_b, y_wall, row_own, scr, shifted, across, rough, moment, second)
     x_wall, x_b, x_a = x_b, swapped(x_b, "gx", True), swapped(x_a, "gx", False)
     return tuple(
         call(
             rim_kernel,
             [(height, lanes)] * 3,
             scratch=[
-                pltpu.VMEM((NF, 32, lanes), jnp.float32),
                 pltpu.VMEM((NF, 32, height + 128), jnp.float32),
-                pltpu.VMEM((N_AHEAD, 32, lanes), jnp.float32),
                 pltpu.VMEM((N_AHEAD, 32, height + 128), jnp.float32),
-                pltpu.VMEM((N_SHIFTED, lanes // 128, 48, 128), jnp.float32),
                 pltpu.VMEM((N_SHIFTED, height // 128 + 1, 48, 128), jnp.float32),
-                pltpu.VMEM((N_ACROSS, 32, lanes), jnp.float32),
                 pltpu.VMEM((N_ACROSS, 32, height + 128), jnp.float32),
-                pltpu.VMEM((32, lanes), jnp.float32),
                 pltpu.VMEM((32, height + 128), jnp.float32),
-                pltpu.VMEM((128, height), jnp.float32),
-                pltpu.VMEM((height, 128), jnp.float32),
+                pltpu.VMEM((3, 128, height), jnp.float32),
             ],
         )(
-            y_b, y_a, y_wall, x_b, x_a, x_wall, row_own, col_left, col_right, corner_left, corner_right,
-            grad, rough, moment, second,
+            x_a, x_b, x_wall, col_left, col_right, corner_left, corner_right,
+            mom_left, mom_right, own_rough, own_moment, own_second,
         )
     )
 

time: 18.9 us -> 18.1 us (0.958)
  waiting for transfers between devices: 2.5 us -> 1.55 us
    ppermute x4, waiting for transfers between devices: 2.5 us -> 1.55 us  [swapped(): return lax.ppermute(value, ('gx', 'gy'), pairs)]
  transfers between devices with their start and end apart: 4 -> 4, of which waited for: 2 -> 2; matrix products, arithmetic and copies ran while one was open for 0% -> 0% of each run, Pallas kernels for 22% -> 29%
where the time goes in v5:
time: 18.1 us; the launch traced here: 17.9 us
  starting transfers between devices  7.86 us (43%)
  Pallas kernels  7.77 us (43%)
  waiting for transfers between devices  1.55 us (9%)
  between operations  0.74 us (4%)
    ppermute x4, starting transfers between devices, swapped(): return lax.ppermute(value, ('gx', 'gy'), pairs)  7.86 us
    pallas_call x1, Pallas kernels, on_device(): call(forward_kernel, [*kept, (NF, 16, lanes), (NF, 8, height), (NF, 8, he...  3.43 us
    pallas_call x1, Pallas kernels, on_device(): call(backward_kernel, [(height, lanes)] * 3 + [(2, 8, height)] * 2, scrat...  1.69 us
    ppermute x4, waiting for transfers between devices, swapped(): return lax.ppermute(value, ('gx', 'gy'), pairs)  1.55 us
    pallas_call x1, Pallas kernels, on_device(): call(rim_kernel, [(height, lanes)] * 3, scratch=[pltpu.VMEM((NF, 32, heig...  1.45 us
    pallas_call x1, Pallas kernels, on_device(): call(pack_rows_kernel, [(32, lanes), (32, lanes), (16, lanes)], scratch=[...  1.07 us
  transfers between devices with their start and end apart: 4, of which 2 were waited for; matrix products, arithmetic and copies ran while one was open for 0% of the time, Pallas kernels for 29%

profile of v5, /device:TPU:57, one launch (start us, length us, event | category | flops | bytes accessed | tf_op | source)
XLA Modules:
  0.0 17.9 jit_solution(10548228315392292173)
XLA Ops:
  0.6 0.0 copy-start.2
  0.6 0.0 copy-start.1
  0.7 0.0 copy-start.3
  0.7 0.0 copy-start
  0.7 0.0 copy-start.5
  0.7 0.0 copy-start.4
  0.7 1.1 %shard_map.94 = (f32[32,256]{1,0:T(8,128)S(1)}, f32[32,256]{1,0:T(8,128)S(1)}, f32[16,256]{1,0:T(8,128)S(1)}) custom-call(s32[2,2]{1,0:T(2,128)} %wet_hbm.1, f32[3,256,256]{2,1,0:T(8,128)} %w_ref.1, f32[256,256]{1,0:T(8,128)} %z_ref.1, f32[256,256]{1,0:T(8,128)} %lr_ref.3, f32[3,256,256]{2,1,0:T(8,128)} %c_ref.1), custom_call_target="tpu_custom_call" | custom-call | tf_op jit(solution)/shard_map/pallas_call | solution.py:482
  1.8 1.3 %collective-permute-start.1 = (f32[32,256]{1,0:T(8,128)S(1)}, f32[32,256]{1,0:T(8,128)S(1)}, u32[]{:S(2)}, u32[]{:S(2)}) collective-permute-start(f32[32,256]{1,0:T(8,128)S(1)} %get-tuple-element.22), channel_id=1, source_target_pairs={{0,1},{1,0},{2,3},{3,2},{4,5},{5,4},{6,7},{7,6},{8,9},{9,8},{10,11... | collective-permute-start | bytes 98312 | tf_op jit(solution)/shard_map/ppermute | solution.py:462
  3.1 2.5 %collective-permute-start = (f32[32,256]{1,0:T(8,128)S(1)}, f32[32,256]{1,0:T(8,128)S(1)}, u32[]{:S(2)}, u32[]{:S(2)}) collective-permute-start(f32[32,256]{1,0:T(8,128)S(1)} %get-tuple-element.21.yw_ref), channel_id=1, source_target_pairs={{0,8},{1,2},{2,1},{3,4},{4,3},{5,6},{6,5},{7,15},{8,0},{9,10},{10,... | collective-permute-start | bytes 98312 | tf_op jit(solution)/shard_map/ppermute | solution.py:462
  5.5 0.0 copy-done.2
  5.6 0.0 copy-done.1
  5.6 0.0 copy-done.3
  5.6 0.0 copy-done
  5.6 3.4 %shard_map.95 = (f32[7,256,256]{2,1,0:T(8,128)S(1)}, f32[9,2,272,128]{3,2,1,0:T(8,128)S(1)}, f32[6,256,256]{2,1,0:T(8,128)S(1)}, f32[9,16,256]{2,1,0:T(8,128)S(1...) custom-call(f32[16,256]{1,0:T(8,128)S(1)} %get-tuple-element.23.wet_ref, f32[3,256,256]{2,1,0:T(8,128)S(1)} %copy-done, ...), custom_call_target="tpu_custom_call" | custom-call | flops 20000000 | bytes 2500000 | tf_op jit(solution)/shard_map/pallas_call | solution.py:500
  9.0 0.0 collective-permute-done.1.ya_ref
  9.0 0.4 %collective-permute-done.yb_ref = f32[32,256]{1,0:T(8,128)S(1)} collective-permute-done((f32[32,256]{1,0:T(8,128)S(1)}, f32[32,256]{1,0:T(8,128)S(1)}, u32[]{:S(2)}, u32[]{:S(2)}) %collective-permute-start) | collective-permute-done | bytes 32800 | tf_op jit(solution)/shard_map/ppermute | solution.py:462
  9.4 0.1 shard_map.96
  9.6 2.3 %collective-permute-start.2 = (f32[40,256]{1,0:T(8,128)S(1)}, f32[40,256]{1,0:T(8,128)S(1)}, u32[]{:S(2)}, u32[]{:S(2)}) collective-permute-start(f32[40,256]{1,0:T(8,128)S(1)} %get-tuple-element.26), channel_id=1, source_target_pairs={{0,8},{1,9},{2,10},{3,11},{4,12},{5,13},{6,14},{7,15},{8,0},{9,1},... | collective-permute-start | bytes 122888 | tf_op jit(solution)/shard_map/ppermute | solution.py:462
  11.9 1.8 %collective-permute-start.3 = (f32[40,256]{1,0:T(8,128)S(1)}, f32[40,256]{1,0:T(8,128)S(1)}, u32[]{:S(2)}, u32[]{:S(2)}) collective-permute-start(f32[40,256]{1,0:T(8,128)S(1)} %get-tuple-element.27.xw_ref), channel_id=1, source_target_pairs={{0,1},{1,0},{2,3},{3,2},{4,5},{5,4},{6,7},{7,6},{8,16},{9,17},{10,... | collective-permute-start | bytes 122888 | tf_op jit(solution)/shard_map/ppermute | solution.py:462
  13.7 0.0 copy-done.5
  13.7 0.0 copy-done.4
  13.7 1.7 %shard_map.97 = (f32[256,256]{1,0:T(8,128)S(1)}, f32[256,256]{1,0:T(8,128)S(1)}, f32[256,256]{1,0:T(8,128)S(1)}, f32[2,8,256]{2,1,0:T(8,128)S(1)}, f32[2,8,256]{2,1,0:T(8,128)S(1)}) custom-call(f32[8,128]{1,0:T(8,128)S(1)} %get-tuple-element.28.after_ref.pl_ref, f32[32,256]{1,0:T(8,128)S(1)} %collective-permute-done.1.ya_ref, ...), custom_call_target="tpu_custom_call" | custom-call | flops 20000000 | bytes 2500000 | tf_op jit(solution)/shard_map/pallas_call | solution.py:508
  15.4 0.0 collective-permute-done.2.xa_ref
  15.4 1.1 %collective-permute-done.3.xb_ref = f32[40,256]{1,0:T(8,128)S(1)} collective-permute-done((f32[40,256]{1,0:T(8,128)S(1)}, f32[40,256]{1,0:T(8,128)S(1)}, u32[]{:S(2)}, u32[]{:S(2)}) %collective-permute-start.3) | collective-permute-done | bytes 40992 | tf_op jit(solution)/shard_map/ppermute | solution.py:462
  16.5 1.5 %shard_map.98 = (f32[256,256]{1,0:T(8,128)}, f32[256,256]{1,0:T(8,128)}, f32[256,256]{1,0:T(8,128)}) custom-call(f32[40,256]{1,0:T(8,128)S(1)} %collective-permute-done.2.xa_ref, f32[40,256]{1,0:T(8,128)S(1)} %collective-permute-done.3.xb_ref, f32[40,256]{1,0:T(8,128)S(1)} %get-tuple-element.27.xw_ref, f32[9,8,256]{2,1,0:T(8,128)S(1)} %get-tuple-element.24.tl_ref, ...), custom_call_target="tpu_custom_call" | custom-call | tf_op jit(solution)/shard_map/pallas_call | solution.py:523
Async XLA Ops:
  0.6 4.9 %copy-start.2 = (f32[256,256]{1,0:T(8,128)S(1)}, f32[256,256]{1,0:T(8,128)}, u32[]{:S(2)}) copy-start(f32[256,256]{1,0:T(8,128)} %lr_ref.3) | copy-start | bytes 786436
  0.6 4.9 %copy-start.1 = (f32[3,256,256]{2,1,0:T(8,128)S(1)}, f32[3,256,256]{2,1,0:T(8,128)}, u32[]{:S(2)}) copy-start(f32[3,256,256]{2,1,0:T(8,128)} %c_ref.1) | copy-start | bytes 2359300
  0.7 4.9 %copy-start.3 = (f32[256,256]{1,0:T(8,128)S(1)}, f32[256,256]{1,0:T(8,128)}, u32[]{:S(2)}) copy-start(f32[256,256]{1,0:T(8,128)} %z_ref.1) | copy-start | bytes 786436
  0.7 4.9 %copy-start = (f32[3,256,256]{2,1,0:T(8,128)S(1)}, f32[3,256,256]{2,1,0:T(8,128)}, u32[]{:S(2)}) copy-start(f32[3,256,256]{2,1,0:T(8,128)} %w_ref.1) | copy-start | bytes 2359300
  0.7 13.0 %copy-start.5 = (f32[256,256]{1,0:T(8,128)S(1)}, f32[256,256]{1,0:T(8,128)}, u32[]{:S(2)}) copy-start(f32[256,256]{1,0:T(8,128)} %v_ref.1) | copy-start | bytes 786436
  0.7 13.0 %copy-start.4 = (f32[256,256]{1,0:T(8,128)S(1)}, f32[256,256]{1,0:T(8,128)}, u32[]{:S(2)}) copy-start(f32[256,256]{1,0:T(8,128)} %m_ref.1) | copy-start | bytes 786436
  1.8 7.2 %collective-permute-start.1 = (f32[32,256]{1,0:T(8,128)S(1)}, f32[32,256]{1,0:T(8,128)S(1)}, u32[]{:S(2)}, u32[]{:S(2)}) collective-permute-start(f32[32,256]{1,0:T(8,128)S(1)} %get-tuple-element.22), channel_id=1, source_target_pairs={{0,1},{1,0},{2,3},{3,2},{4,5},{5,4},{6,7},{7,6},{8,9},{9,8},{10,11... | collective-permute-start | bytes 98312 | tf_op jit(solution)/shard_map/ppermute | solution.py:462
  3.1 6.4 %collective-permute-start = (f32[32,256]{1,0:T(8,128)S(1)}, f32[32,256]{1,0:T(8,128)S(1)}, u32[]{:S(2)}, u32[]{:S(2)}) collective-permute-start(f32[32,256]{1,0:T(8,128)S(1)} %get-tuple-element.21.yw_ref), channel_id=1, source_target_pairs={{0,8},{1,2},{2,1},{3,4},{4,3},{5,6},{6,5},{7,15},{8,0},{9,10},{10,... | collective-permute-start | bytes 98312 | tf_op jit(solution)/shard_map/ppermute | solution.py:462
  9.6 5.8 %collective-permute-start.2 = (f32[40,256]{1,0:T(8,128)S(1)}, f32[40,256]{1,0:T(8,128)S(1)}, u32[]{:S(2)}, u32[]{:S(2)}) collective-permute-start(f32[40,256]{1,0:T(8,128)S(1)} %get-tuple-element.26), channel_id=1, source_target_pairs={{0,8},{1,9},{2,10},{3,11},{4,12},{5,13},{6,14},{7,15},{8,0},{9,1},... | collective-permute-start | bytes 122888 | tf_op jit(solution)/shard_map/ppermute | solution.py:462
  11.9 4.6 %collective-permute-start.3 = (f32[40,256]{1,0:T(8,128)S(1)}, f32[40,256]{1,0:T(8,128)S(1)}, u32[]{:S(2)}, u32[]{:S(2)}) collective-permute-start(f32[40,256]{1,0:T(8,128)S(1)} %get-tuple-element.27.xw_ref), channel_id=1, source_target_pairs={{0,1},{1,0},{2,3},{3,2},{4,5},{5,4},{6,7},{7,6},{8,16},{9,17},{10,... | collective-permute-start | bytes 122888 | tf_op jit(solution)/shard_map/ppermute | solution.py:462

commit v6 on v5

--- a/solution.py
+++ b/solution.py
@@ -18,6 +18,9 @@
 ATAN_SCALE = 1.27
 H, QX, QY, Z, LR, CH, CX, CY, WET = range(9)
 NF = 9
+COUNT = (3, 3, 3, 3, 2, 1, 1, 1, 1)
+START = (0, 3, 6, 9, 12, 14, 15, 16, 17)
+SENT = 18
 TURNED = (H, QY, QX, Z, LR, CH, CY, CX, WET)
 BLK = 8
 UNROLL = 8
@@ -94,11 +97,10 @@
 
 
 UH, UX, UY, SX, SY, GA, GB = range(7)
-N_AHEAD, N_ACROSS, N_SHIFTED = 7, 6, 9
-DOWN, UP, ZS = 0, 3, 6
+N_AHEAD, N_ACROSS, N_SHIFTED = 7, 5, 6
+DOWN, UP = 0, 3
 PH, PX, PY = range(3)
-ADJ = 6
-VU, VV, PG = 3, 4, 5
+VU, VV = 3, 4
 
 
 def gathered(shifted, across, j):
@@ -109,15 +111,16 @@
     ]
 
 
-def first_pass(get, wet, n, scr, shifted, across):
-    looped(n, lambda j: give(shifted.at[ZS], j, get(Z, j)))
+def first_pass(get, wet, n, scr, shifted, across, adj):
+    zs = adj.at[0]
+    looped(n, lambda j: give(zs, j, get(Z, j)))
 
     def parts(j):
         r = rows(j)
         kg = HALF_STEP * GRAVITY
         z = get(Z, j)
         sx = kg * (from_next_col(z) - from_prev_col(z))
-        sy = kg * (take(shifted.at[ZS], j, 1) - take(shifted.at[ZS], j, -1))
+        sy = kg * (take(zs, j, 1) - take(zs, j, -1))
         scr[SX, r, :] = sx
         scr[SY, r, :] = sy
         cols, down, up, _, _ = flux_parts(get(H, j), get(QX, j), get(QY, j), sx, sy)
@@ -143,7 +146,7 @@
     looped(n, finish)
 
 
-def second_pass(get, wet, n, scr, shifted, across):
+def second_pass(get, wet, n, scr, shifted, across, adj, pg):
     def parts(j):
         r = rows(j)
         cols, down, up, u, v = flux_parts(*(scr[f, r, :] for f in (UH, UX, UY, SX, SY)))
@@ -173,19 +176,19 @@
     def finish_all(j):
         for f, value in enumerate(finish(j)):
             if f < 3:
-                give(shifted.at[ADJ + f], j, value)
+                give(adj.at[f], j, value)
             else:
-                across[PG, rows(j), :] = value
+                pg[rows(j), :] = value
 
     looped(n, finish_all)
 
 
-def third_pass(n, scr, shifted, across, put_grad):
+def third_pass(blocks, scr, across, adj, pg, put_grad):
     def back(j):
         r = rows(j)
 
         def four(f):
-            ref = shifted.at[ADJ + f]
+            ref = adj.at[f]
             cur = take(ref, j)
             return from_next_col(cur), from_prev_col(cur), take(ref, j, 1), take(ref, j, -1)
 
@@ -207,9 +210,13 @@
             + (2.0 * k) * v * (ys - yn)
             + u * cross
         )
-        put_grad(j, across[PG, r, :] + scr[GA, r, :] * cot_x + scr[GB, r, :] * cot_y)
-
-    looped(n, back)
+        put_grad(j, pg[r, :] + scr[GA, r, :] * cot_x + scr[GB, r, :] * cot_y)
+
+    if isinstance(blocks, int):
+        looped(blocks, back)
+    else:
+        for j in blocks:
+            back(j)
 
 
 def place(axis):
@@ -217,10 +224,18 @@
     return index, lax.axis_size(axis)
 
 
-def three_rows(block, first, mirrored, sign):
-    natural = block[first : first + 3, :]
-    reverse = jnp.concatenate([block[first + 2 - d : first + 3 - d, :] for d in range(3)], 0)
-    return jnp.where(mirrored, sign * reverse, natural)
+def top_rows(block, count, mirrored, sign):
+    reverse = jnp.concatenate([block[d : d + 1, :] for d in reversed(range(count))], 0)
+    return jnp.where(mirrored, sign * reverse, block[0:count, :])
+
+
+def bottom_rows(block, count, mirrored, sign):
+    reverse = jnp.concatenate([block[d : d + 1, :] for d in range(7, 7 - count, -1)], 0)
+    return jnp.where(mirrored, sign * reverse, block[8 - count : 8, :])
+
+
+def sent(f):
+    return slice(START[f], START[f] + COUNT[f])
 
 
 def pack_rows_kernel(wet_hbm, w_hbm, z_hbm, lr_hbm, c_hbm, b_ref, a_ref, wet_ref, wet_s, top, bot, sems):
@@ -240,8 +255,8 @@
     gy, ny = place("gy")
     even = gy % 2 == 0
     lane = lax.broadcasted_iota(jnp.int32, (8, lanes), 1)
-    a_ref[24:32, :] = jnp.zeros((8, lanes), jnp.float32)
-    b_ref[24:32, :] = jnp.zeros((8, lanes), jnp.float32)
+    a_ref[16:24, :] = jnp.zeros((8, lanes), jnp.float32)
+    b_ref[16:24, :] = jnp.zeros((8, lanes), jnp.float32)
     for copy in copies:
         copy.wait()
     for row in range(2):
@@ -250,17 +265,17 @@
         wet_ref[8 * row : 8 * row + 8, :] = jnp.where(lane < lanes // 2, left, right)
     for f in range(NF):
         sign = -1.0 if f in (QY, CY) else 1.0
-        t = three_rows(top[f] if f < WET else wet_ref[0:8, :], 0, gy == 0, sign)
-        b = three_rows(bot[f] if f < WET else wet_ref[8:16, :], 5, gy == ny - 1, sign)
-        a_ref[3 * f : 3 * f + 3, :] = jnp.where(even, b, t)
-        b_ref[3 * f : 3 * f + 3, :] = jnp.where(even, t, b)
+        t = top_rows(top[f] if f < WET else wet_ref[0:8, :], COUNT[f], gy == 0, sign)
+        b = bottom_rows(bot[f] if f < WET else wet_ref[8:16, :], COUNT[f], gy == ny - 1, sign)
+        a_ref[sent(f), :] = jnp.where(even, b, t)
+        b_ref[sent(f), :] = jnp.where(even, t, b)
 
 
 def tile_wet(wet_ref, j, n):
     return wet_ref[rows(j // (n // 2)), :] > 0.5
 
 
-def forward_kernel(wet_ref, w_ref, z_ref, lr_ref, c_ref, scr, shifted, across, rs_ref, tl_ref, tr_ref):
+def forward_kernel(wet_ref, w_ref, z_ref, lr_ref, c_ref, scr, across, adj, pg, rs_ref, tl_ref, tr_ref, shifted):
     height, lanes = z_ref.shape
     n = height // BLK
 
@@ -272,8 +287,8 @@
     def get(f, j):
         return field(f)[rows(j), :]
 
-    first_pass(get, lambda j: tile_wet(wet_ref, j, n), n, scr, shifted, across)
-    second_pass(get, lambda j: tile_wet(wet_ref, j, n), n, scr, shifted, across)
+    first_pass(get, lambda j: tile_wet(wet_ref, j, n), n, scr, shifted, across, adj)
+    second_pass(get, lambda j: tile_wet(wet_ref, j, n), n, scr, shifted, across, adj, pg)
     lane = lax.broadcasted_iota(jnp.int32, (height, 128), 1)
     for f in range(WET):
         ref = field(f)
@@ -290,7 +305,7 @@
     tr_ref[WET] = jnp.concatenate([top[:, half:], bottom[:, half:]], 1)
 
 
-def strip_gradient(s_ref, scr, shifted, across, g_ref):
+def strip_gradient(s_ref, scr, shifted, across, adj, pg, g_ref):
     n = s_ref.shape[1] // BLK
 
     def get(f, j):
@@ -302,9 +317,9 @@
     def put_grad(j, value):
         g_ref[rows(j), :] = value
 
-    first_pass(get, wet, n, scr, shifted, across)
-    second_pass(get, wet, n, scr, shifted, across)
-    third_pass(n, scr, shifted, across, put_grad)
+    first_pass(get, wet, n, scr, shifted, across, adj)
+    second_pass(get, wet, n, scr, shifted, across, adj, pg)
+    third_pass((1, 2), scr, across, adj, pg, put_grad)
 
 
 def arctan_ratio(y, x):
@@ -328,8 +343,8 @@
 
 
 def backward_kernel(
-    after_ref, ya_ref, yb_ref, yw_ref, rs_ref, scr, shifted, across, lr_ref, m_ref, v_ref,
-    nr_ref, nm_ref, nv_ref, ml_ref, mr_ref, g_ref, row_s, row_scr, row_sh, row_ac, row_g,
+    after_ref, ya_ref, yb_ref, yw_ref, rs_ref, scr, across, adj, pg, lr_ref, m_ref, v_ref,
+    nr_ref, nm_ref, nv_ref, ml_ref, mr_ref, g_ref, row_s, row_scr, row_sh, row_ac, row_adj, row_pg, row_g,
 ):
     gy, ny = place("gy")
     even_y, at_wall_y = gy % 2 == 0, (gy == 0) | (gy == ny - 1)
@@ -338,16 +353,16 @@
     def put_grad(j, value):
         g_ref[rows(j), :] = value
 
-    third_pass(height // BLK, scr, shifted, across, put_grad)
+    third_pass(height // BLK, scr, across, adj, pg, put_grad)
     for f in range(NF):
-        r = slice(3 * f, 3 * f + 3)
+        r, c = sent(f), COUNT[f]
         ya, yb = ya_ref[r, :], jnp.where(at_wall_y, yw_ref[r, :], yb_ref[r, :])
         row_s[f, 0:8, :] = jnp.ones((8, lanes), jnp.float32)
         row_s[f, 24:32, :] = jnp.ones((8, lanes), jnp.float32)
-        row_s[f, 5:8, :] = jnp.where(even_y, yb, ya)
-        row_s[f, 24:27, :] = jnp.where(even_y, ya, yb)
+        row_s[f, 8 - c : 8, :] = jnp.where(even_y, yb, ya)
+        row_s[f, 24 : 24 + c, :] = jnp.where(even_y, ya, yb)
         row_s[f, 8:24, :] = rs_ref[f]
-    strip_gradient(row_s, row_scr, row_sh, row_ac, row_g)
+    strip_gradient(row_s, row_scr, row_sh, row_ac, row_adj, row_pg, row_g)
     row = lax.broadcasted_iota(jnp.int32, (8, lanes), 0)
     g_ref[0:8, :] = jnp.where(row < 3, row_g[8:16, :], g_ref[0:8, :])
     g_ref[height - 8 : height, :] = jnp.where(row >= 5, row_g[16:24, :], g_ref[height - 8 : height, :])
@@ -379,8 +394,9 @@
     below = jnp.where(lane < 64, below[:, 0:128], below[:, lanes - 128 : lanes])
     k_scr[...] = jnp.zeros_like(k_scr)
     for f in range(NF):
-        k_scr[6 * f : 6 * f + 3, :] = above[3 * f : 3 * f + 3, :]
-        k_scr[6 * f + 3 : 6 * f + 6, :] = below[3 * f : 3 * f + 3, :]
+        c = 3 if f == WET else COUNT[f]
+        k_scr[6 * f + 3 - c : 6 * f + 3, :] = jnp.broadcast_to(above[sent(f), :], (c, 128))
+        k_scr[6 * f + 3 : 6 * f + 3 + c, :] = jnp.broadcast_to(below[sent(f), :], (c, 128))
     turned = k_scr[...].T
     left_corner, right_corner = turned[0:8, :], turned[120:128, :]
     pl_ref[...] = left_corner
@@ -391,22 +407,22 @@
     first, last = gx == 0, gx == nx - 1
     for f in range(NF):
         sign = -1.0 if f in (QX, CX) else 1.0
-        t = three_rows(tl_ref[f], 0, first, sign)
-        b = three_rows(tr_ref[f], 5, last, sign)
-        a_ref[3 * f : 3 * f + 3, :] = jnp.where(even, b, t)
-        b_ref[3 * f : 3 * f + 3, :] = jnp.where(even, t, b)
+        t = top_rows(tl_ref[f], COUNT[f], first, sign)
+        b = bottom_rows(tr_ref[f], COUNT[f], last, sign)
+        a_ref[sent(f), :] = jnp.where(even, b, t)
+        b_ref[sent(f), :] = jnp.where(even, t, b)
     lane = lax.broadcasted_iota(jnp.int32, (3, 128), 1)
     flip = ((lane >= 6 * QX) & (lane < 6 * QX + 6)) | ((lane >= 6 * CX) & (lane < 6 * CX + 6))
     sign = jnp.where(flip, -1.0, 1.0)
-    t = three_rows(left_corner, 0, first, sign)
-    b = three_rows(right_corner, 5, last, sign)
-    a_ref[32:35, 0:128] = jnp.where(even, b, t)
-    b_ref[32:35, 0:128] = jnp.where(even, t, b)
+    t = top_rows(left_corner, 3, first, sign)
+    b = bottom_rows(right_corner, 3, last, sign)
+    a_ref[SENT : SENT + 3, 0:128] = jnp.where(even, b, t)
+    b_ref[SENT : SENT + 3, 0:128] = jnp.where(even, t, b)
 
 
 def rim_kernel(
     xa_ref, xb_ref, xw_ref, tl_ref, tr_ref, pl_ref, pr_ref, ml_ref, mr_ref, ir_ref, im_ref, iv_ref,
-    nr_ref, nm_ref, nv_ref, col_s, col_scr, col_sh, col_ac, col_g, turn_scr,
+    nr_ref, nm_ref, nv_ref, col_s, col_scr, col_sh, col_ac, col_adj, col_pg, col_g, turn_scr,
 ):
     gx, nx = place("gx")
     even_x, at_wall_x = gx % 2 == 0, (gx == 0) | (gx == nx - 1)
@@ -416,18 +432,18 @@
     right_in = jnp.where(even_x, xa_ref[...], x_b)
     for f, t in enumerate(TURNED):
         shift = (125 - 6 * f) % 128
-        r = slice(3 * f, 3 * f + 3)
+        r, c = sent(f), COUNT[f]
         col_s[t, 0:8, :] = jnp.ones((8, height + 128), jnp.float32)
         col_s[t, 24:32, :] = jnp.ones((8, height + 128), jnp.float32)
-        col_s[t, 5:8, 0:height] = left_in[r, :]
-        col_s[t, 24:27, 0:height] = right_in[r, :]
+        col_s[t, 8 - c : 8, 0:height] = left_in[r, :]
+        col_s[t, 24 : 24 + c, 0:height] = right_in[r, :]
         col_s[t, 8:16, 0:height] = tl_ref[f]
         col_s[t, 16:24, 0:height] = tr_ref[f]
-        col_s[t, 5:8, height:] = pltpu.roll(left_in[32:40, 0:128], shift, 1)[0:3, :]
-        col_s[t, 24:27, height:] = pltpu.roll(right_in[32:40, 0:128], shift, 1)[0:3, :]
+        col_s[t, 5:8, height:] = pltpu.roll(left_in[16:24, 0:128], shift, 1)[2:5, :]
+        col_s[t, 24:27, height:] = pltpu.roll(right_in[16:24, 0:128], shift, 1)[2:5, :]
         col_s[t, 8:16, height:] = pltpu.roll(pl_ref[...], shift, 1)
         col_s[t, 16:24, height:] = pltpu.roll(pr_ref[...], shift, 1)
-    strip_gradient(col_s, col_scr, col_sh, col_ac, col_g)
+    strip_gradient(col_s, col_scr, col_sh, col_ac, col_adj, col_pg, col_g)
     turn_scr[:, 8:120, :] = jnp.zeros((3, 112, height), jnp.float32)
     for r, g, t_ref, s_ref in ((slice(0, 8), 8, tl_ref, ml_ref), (slice(120, 128), 16, tr_ref, mr_ref)):
         new = updated(col_g[g : g + 8, 0:height], t_ref[LR], s_ref[0], s_ref[1])
@@ -481,7 +497,7 @@
     hbm = pl.BlockSpec(memory_space=pltpu.HBM)
     y_b, y_a, wet = call(
         pack_rows_kernel,
-        [(32, lanes), (32, lanes), (16, lanes)],
+        [(24, lanes), (24, lanes), (16, lanes)],
         scratch=[
             pltpu.SMEM((2, 2), jnp.int32),
             pltpu.VMEM((8, 8, lanes), jnp.float32),
@@ -494,15 +510,19 @@
     y_wall, y_b, y_a = y_b, swapped(y_b, "gy", True), swapped(y_a, "gy", False)
     kept = [
         (N_AHEAD, height, lanes),
-        (N_SHIFTED, lanes // 128, height + 16, 128),
         (N_ACROSS, height, lanes),
+        (3, lanes // 128, height + 16, 128),
+        (height, lanes),
     ]
-    scr, shifted, across, row_own, col_left, col_right = call(
-        forward_kernel, [*kept, (NF, 16, lanes), (NF, 8, height), (NF, 8, height)], flops=20_000_000
+    scr, across, adj, pg, row_own, col_left, col_right = call(
+        forward_kernel,
+        [*kept, (NF, 16, lanes), (NF, 8, height), (NF, 8, height)],
+        scratch=[pltpu.VMEM((N_SHIFTED, lanes // 128, height + 16, 128), jnp.float32)],
+        flops=20_000_000,
     )(wet, water, ground, rough, cot)
     x_b, x_a, corner_left, corner_right = call(
         pack_cols_kernel,
-        [(40, height), (40, height), (8, 128), (8, 128)],
+        [(24, height), (24, height), (8, 128), (8, 128)],
         scratch=[pltpu.VMEM((128, 128), jnp.float32)],
     )(y_b, y_a, y_wall, col_left, col_right)
     own_rough, own_moment, own_second, mom_left, mom_right = call(
@@ -514,10 +534,12 @@
             pltpu.VMEM((N_AHEAD, 32, lanes), jnp.float32),
             pltpu.VMEM((N_SHIFTED, lanes // 128, 48, 128), jnp.float32),
             pltpu.VMEM((N_ACROSS, 32, lanes), jnp.float32),
+            pltpu.VMEM((3, lanes // 128, 48, 128), jnp.float32),
+            pltpu.VMEM((32, lanes), jnp.float32),
             pltpu.VMEM((32, lanes), jnp.float32),
         ],
         flops=20_000_000,
-    )(corner_left, y_a, y_b, y_wall, row_own, scr, shifted, across, rough, moment, second)
+    )(corner_left, y_a, y_b, y_wall, row_own, scr, across, adj, pg, rough, moment, second)
     x_wall, x_b, x_a = x_b, swapped(x_b, "gx", True), swapped(x_a, "gx", False)
     return tuple(
         call(
@@ -528,6 +550,8 @@
                 pltpu.VMEM((N_AHEAD, 32, height + 128), jnp.float32),
                 pltpu.VMEM((N_SHIFTED, height // 128 + 1, 48, 128), jnp.float32),
                 pltpu.VMEM((N_ACROSS, 32, height + 128), jnp.float32),
+                pltpu.VMEM((3, height // 128 + 1, 48, 128), jnp.float32),
+                pltpu.VMEM((32, height + 128), jnp.float32),
                 pltpu.VMEM((32, height + 128), jnp.float32),
                 pltpu.VMEM((3, 128, height), jnp.float32),
             ],

time: 18.1 us -> 17.5 us (0.967)
  Pallas kernels: 7.77 us -> 7.21 us
    pallas_call x1, Pallas kernels: 3.43 us -> 2.88 us  [on_device(): call(forward_kernel, [*kept, (NF, 16, lanes), (NF, 8, height), (NF, 8, he...]
  transfers between devices with their start and end apart: 4 -> 4, of which waited for: 2 -> 2; matrix products, arithmetic and copies ran while one was open for 0% -> 0% of each run, Pallas kernels for 29% -> 26%
where the time goes in v6:
time: 17.5 us; the launch traced here: 17.4 us
  starting transfers between devices  7.76 us (44%)
  Pallas kernels  7.21 us (41%)
  waiting for transfers between devices  1.66 us (9%)
  between operations  0.74 us (4%)
    ppermute x4, starting transfers between devices, swapped(): return lax.ppermute(value, ('gx', 'gy'), pairs)  7.76 us
    pallas_call x1, Pallas kernels, on_device(): call(forward_kernel, [*kept, (NF, 16, lanes), (NF, 8, height), (NF, 8, he...  2.88 us
    pallas_call x1, Pallas kernels, on_device(): call(backward_kernel, [(height, lanes)] * 3 + [(2, 8, height)] * 2, scrat...  1.7 us
    ppermute x4, waiting for transfers between devices, swapped(): return lax.ppermute(value, ('gx', 'gy'), pairs)  1.66 us
    pallas_call x1, Pallas kernels, on_device(): call(rim_kernel, [(height, lanes)] * 3, scratch=[pltpu.VMEM((NF, 32, heig...  1.46 us
    pallas_call x1, Pallas kernels, on_device(): call(pack_rows_kernel, [(24, lanes), (24, lanes), (16, lanes)], scratch=[...  1.06 us
  transfers between devices with their start and end apart: 4, of which 2 were waited for; matrix products, arithmetic and copies ran while one was open for 0% of the time, Pallas kernels for 26%

profile of v6, /device:TPU:57, one launch (start us, length us, event | category | flops | bytes accessed | tf_op | source)
XLA Modules:
  0.0 17.4 jit_solution(3038945799683693028)
XLA Ops:
  0.6 0.0 copy-start.2
  0.6 0.0 copy-start.1
  0.7 0.0 copy-start.3
  0.7 0.0 copy-start
  0.7 0.0 copy-start.5
  0.7 0.0 copy-start.4
  0.7 1.1 %shard_map.94 = (f32[24,256]{1,0:T(8,128)S(1)}, f32[24,256]{1,0:T(8,128)S(1)}, f32[16,256]{1,0:T(8,128)S(1)}) custom-call(s32[2,2]{1,0:T(2,128)} %wet_hbm.1, f32[3,256,256]{2,1,0:T(8,128)} %w_ref.1, f32[256,256]{1,0:T(8,128)} %z_ref.1, f32[256,256]{1,0:T(8,128)} %lr_ref.3, f32[3,256,256]{2,1,0:T(8,128)} %c_ref.1), custom_call_target="tpu_custom_call" | custom-call | tf_op jit(solution)/shard_map/pallas_call | solution.py:498
  1.8 1.3 %collective-permute-start.1 = (f32[24,256]{1,0:T(8,128)S(1)}, f32[24,256]{1,0:T(8,128)S(1)}, u32[]{:S(2)}, u32[]{:S(2)}) collective-permute-start(f32[24,256]{1,0:T(8,128)S(1)} %get-tuple-element.23), channel_id=1, source_target_pairs={{0,1},{1,0},{2,3},{3,2},{4,5},{5,4},{6,7},{7,6},{8,9},{9,8},{10,11... | collective-permute-start | bytes 73736 | tf_op jit(solution)/shard_map/ppermute | solution.py:478
  3.1 2.5 %collective-permute-start = (f32[24,256]{1,0:T(8,128)S(1)}, f32[24,256]{1,0:T(8,128)S(1)}, u32[]{:S(2)}, u32[]{:S(2)}) collective-permute-start(f32[24,256]{1,0:T(8,128)S(1)} %get-tuple-element.22.yw_ref), channel_id=1, source_target_pairs={{0,8},{1,2},{2,1},{3,4},{4,3},{5,6},{6,5},{7,15},{8,0},{9,10},{10,... | collective-permute-start | bytes 73736 | tf_op jit(solution)/shard_map/ppermute | solution.py:478
  5.5 0.0 copy-done.2
  5.5 0.0 copy-done.1
  5.5 0.0 copy-done.3
  5.6 0.0 copy-done
  5.6 2.9 %shard_map.95 = (f32[7,256,256]{2,1,0:T(8,128)S(1)}, f32[5,256,256]{2,1,0:T(8,128)S(1)}, f32[3,2,272,128]{3,2,1,0:T(8,128)S(1)}, f32[256,256]{1,0:T(8,128)S(1)},...) custom-call(f32[16,256]{1,0:T(8,128)S(1)} %get-tuple-element.24.wet_ref, ...), custom_call_target="tpu_custom_call" | custom-call | flops 20000000 | bytes 2500000 | tf_op jit(solution)/shard_map/pallas_call | solution.py:517
  8.4 0.0 collective-permute-done.1.ya_ref
  8.5 0.9 %collective-permute-done.yb_ref = f32[24,256]{1,0:T(8,128)S(1)} collective-permute-done((f32[24,256]{1,0:T(8,128)S(1)}, f32[24,256]{1,0:T(8,128)S(1)}, u32[]{:S(2)}, u32[]{:S(2)}) %collective-permute-start) | collective-permute-done | bytes 24608 | tf_op jit(solution)/shard_map/ppermute | solution.py:478
  9.3 0.1 shard_map.96
  9.5 2.2 %collective-permute-start.2 = (f32[24,256]{1,0:T(8,128)S(1)}, f32[24,256]{1,0:T(8,128)S(1)}, u32[]{:S(2)}, u32[]{:S(2)}) collective-permute-start(f32[24,256]{1,0:T(8,128)S(1)} %get-tuple-element.27), channel_id=1, source_target_pairs={{0,8},{1,9},{2,10},{3,11},{4,12},{5,13},{6,14},{7,15},{8,0},{9,1},... | collective-permute-start | bytes 73736 | tf_op jit(solution)/shard_map/ppermute | solution.py:478
  11.6 1.8 %collective-permute-start.3 = (f32[24,256]{1,0:T(8,128)S(1)}, f32[24,256]{1,0:T(8,128)S(1)}, u32[]{:S(2)}, u32[]{:S(2)}) collective-permute-start(f32[24,256]{1,0:T(8,128)S(1)} %get-tuple-element.28.xw_ref), channel_id=1, source_target_pairs={{0,1},{1,0},{2,3},{3,2},{4,5},{5,4},{6,7},{7,6},{8,16},{9,17},{10,... | collective-permute-start | bytes 73736 | tf_op jit(solution)/shard_map/ppermute | solution.py:478
  13.4 0.0 copy-done.5
  13.4 0.0 copy-done.4
  13.4 1.7 %shard_map.97 = (f32[256,256]{1,0:T(8,128)S(1)}, f32[256,256]{1,0:T(8,128)S(1)}, f32[256,256]{1,0:T(8,128)S(1)}, f32[2,8,256]{2,1,0:T(8,128)S(1)}, f32[2,8,256]{2,1,0:T(8,128)S(1)}) custom-call(f32[8,128]{1,0:T(8,128)S(1)} %get-tuple-element.29.after_ref.pl_ref, f32[24,256]{1,0:T(8,128)S(1)} %collective-permute-done.1.ya_ref, ...), custom_call_target="tpu_custom_call" | custom-call | flops 20000000 | bytes 2500000 | tf_op jit(solution)/shard_map/pallas_call | solution.py:528
  15.2 0.0 collective-permute-done.2.xa_ref
  15.2 0.8 %collective-permute-done.3.xb_ref = f32[24,256]{1,0:T(8,128)S(1)} collective-permute-done((f32[24,256]{1,0:T(8,128)S(1)}, f32[24,256]{1,0:T(8,128)S(1)}, u32[]{:S(2)}, u32[]{:S(2)}) %collective-permute-start.3) | collective-permute-done | bytes 24608 | tf_op jit(solution)/shard_map/ppermute | solution.py:478
  15.9 1.5 %shard_map.98 = (f32[256,256]{1,0:T(8,128)}, f32[256,256]{1,0:T(8,128)}, f32[256,256]{1,0:T(8,128)}) custom-call(f32[24,256]{1,0:T(8,128)S(1)} %collective-permute-done.2.xa_ref, f32[24,256]{1,0:T(8,128)S(1)} %collective-permute-done.3.xb_ref, f32[24,256]{1,0:T(8,128)S(1)} %get-tuple-element.28.xw_ref, f32[9,8,256]{2,1,0:T(8,128)S(1)} %get-tuple-element.25.tl_ref, ...), custom_call_target="tpu_custom_call" | custom-call | tf_op jit(solution)/shard_map/pallas_call | solution.py:545
Async XLA Ops:
  0.6 4.9 %copy-start.2 = (f32[256,256]{1,0:T(8,128)S(1)}, f32[256,256]{1,0:T(8,128)}, u32[]{:S(2)}) copy-start(f32[256,256]{1,0:T(8,128)} %lr_ref.3) | copy-start | bytes 786436
  0.6 4.9 %copy-start.1 = (f32[3,256,256]{2,1,0:T(8,128)S(1)}, f32[3,256,256]{2,1,0:T(8,128)}, u32[]{:S(2)}) copy-start(f32[3,256,256]{2,1,0:T(8,128)} %c_ref.1) | copy-start | bytes 2359300
  0.7 4.9 %copy-start.3 = (f32[256,256]{1,0:T(8,128)S(1)}, f32[256,256]{1,0:T(8,128)}, u32[]{:S(2)}) copy-start(f32[256,256]{1,0:T(8,128)} %z_ref.1) | copy-start | bytes 786436
  0.7 4.9 %copy-start = (f32[3,256,256]{2,1,0:T(8,128)S(1)}, f32[3,256,256]{2,1,0:T(8,128)}, u32[]{:S(2)}) copy-start(f32[3,256,256]{2,1,0:T(8,128)} %w_ref.1) | copy-start | bytes 2359300
  0.7 12.8 %copy-start.5 = (f32[256,256]{1,0:T(8,128)S(1)}, f32[256,256]{1,0:T(8,128)}, u32[]{:S(2)}) copy-start(f32[256,256]{1,0:T(8,128)} %v_ref.1) | copy-start | bytes 786436
  0.7 12.8 %copy-start.4 = (f32[256,256]{1,0:T(8,128)S(1)}, f32[256,256]{1,0:T(8,128)}, u32[]{:S(2)}) copy-start(f32[256,256]{1,0:T(8,128)} %m_ref.1) | copy-start | bytes 786436
  1.8 6.7 %collective-permute-start.1 = (f32[24,256]{1,0:T(8,128)S(1)}, f32[24,256]{1,0:T(8,128)S(1)}, u32[]{:S(2)}, u32[]{:S(2)}) collective-permute-start(f32[24,256]{1,0:T(8,128)S(1)} %get-tuple-element.23), channel_id=1, source_target_pairs={{0,1},{1,0},{2,3},{3,2},{4,5},{5,4},{6,7},{7,6},{8,9},{9,8},{10,11... | collective-permute-start | bytes 73736 | tf_op jit(solution)/shard_map/ppermute | solution.py:478
  3.1 6.3 %collective-permute-start = (f32[24,256]{1,0:T(8,128)S(1)}, f32[24,256]{1,0:T(8,128)S(1)}, u32[]{:S(2)}, u32[]{:S(2)}) collective-permute-start(f32[24,256]{1,0:T(8,128)S(1)} %get-tuple-element.22.yw_ref), channel_id=1, source_target_pairs={{0,8},{1,2},{2,1},{3,4},{4,3},{5,6},{6,5},{7,15},{8,0},{9,10},{10,... | collective-permute-start | bytes 73736 | tf_op jit(solution)/shard_map/ppermute | solution.py:478
  9.5 5.7 %collective-permute-start.2 = (f32[24,256]{1,0:T(8,128)S(1)}, f32[24,256]{1,0:T(8,128)S(1)}, u32[]{:S(2)}, u32[]{:S(2)}) collective-permute-start(f32[24,256]{1,0:T(8,128)S(1)} %get-tuple-element.27), channel_id=1, source_target_pairs={{0,8},{1,9},{2,10},{3,11},{4,12},{5,13},{6,14},{7,15},{8,0},{9,1},... | collective-permute-start | bytes 73736 | tf_op jit(solution)/shard_map/ppermute | solution.py:478
  11.6 4.3 %collective-permute-start.3 = (f32[24,256]{1,0:T(8,128)S(1)}, f32[24,256]{1,0:T(8,128)S(1)}, u32[]{:S(2)}, u32[]{:S(2)}) collective-permute-start(f32[24,256]{1,0:T(8,128)S(1)} %get-tuple-element.28.xw_ref), channel_id=1, source_target_pairs={{0,1},{1,0},{2,3},{3,2},{4,5},{5,4},{6,7},{7,6},{8,16},{9,17},{10,... | collective-permute-start | bytes 73736 | tf_op jit(solution)/shard_map/ppermute | solution.py:478

commit v7 on v6

--- a/solution.py
+++ b/solution.py
@@ -24,7 +24,7 @@
 TURNED = (H, QY, QX, Z, LR, CH, CY, CX, WET)
 BLK = 8
 UNROLL = 8
-VMEM_MB = 12
+VMEM_MB = 16
 
 
 def from_prev_col(x):
@@ -96,8 +96,8 @@
     lax.fori_loop(0, n, body, 0, unroll=UNROLL)
 
 
-UH, UX, UY, SX, SY, GA, GB = range(7)
-N_AHEAD, N_ACROSS, N_SHIFTED = 7, 5, 6
+SX, SY, GA, GB = range(4)
+N_AHEAD, N_ACROSS, N_SHIFTED = 4, 5, 6
 DOWN, UP = 0, 3
 PH, PX, PY = range(3)
 VU, VV = 3, 4
@@ -111,7 +111,7 @@
     ]
 
 
-def first_pass(get, wet, n, scr, shifted, across, adj):
+def first_pass(get, wet, n, scr, shifted, across, adj, then):
     zs = adj.at[0]
     looped(n, lambda j: give(zs, j, get(Z, j)))
 
@@ -136,9 +136,12 @@
         h, qx, qy = gathered(shifted, across, j)
         b, w, _ = drag_parts(h, qx, qy, get(LR, j))
         m = wet(j)
-        scr[UH, r, :] = jnp.where(m, h, get(H, j))
-        scr[UX, r, :] = jnp.where(m, qx * w, get(QX, j))
-        scr[UY, r, :] = jnp.where(m, qy * w, get(QY, j))
+        then(
+            j,
+            jnp.where(m, h, get(H, j)),
+            jnp.where(m, qx * w, get(QX, j)),
+            jnp.where(m, qy * w, get(QY, j)),
+        )
         t = jnp.where(m, -2.0 * b * w * w, 0.0)
         scr[GA, r, :] = t * qx
         scr[GB, r, :] = t * qy
@@ -146,10 +149,10 @@
     looped(n, finish)
 
 
-def second_pass(get, wet, n, scr, shifted, across, adj, pg):
-    def parts(j):
+def second_parts(scr, shifted, across):
+    def parts(j, h, qx, qy):
         r = rows(j)
-        cols, down, up, u, v = flux_parts(*(scr[f, r, :] for f in (UH, UX, UY, SX, SY)))
+        cols, down, up, u, v = flux_parts(h, qx, qy, scr[SX, r, :], scr[SY, r, :])
         across[VU, r, :] = u
         across[VV, r, :] = v
         for f in range(3):
@@ -157,8 +160,10 @@
             give(shifted.at[DOWN + f], j, down[f])
             give(shifted.at[UP + f], j, up[f])
 
-    looped(n, parts)
-
+    return parts
+
+
+def second_pass(get, wet, n, shifted, across, adj, pg):
     def finish(j):
         h, qx, qy = gathered(shifted, across, j)
         b, w, inv_s2 = drag_parts(h, qx, qy, get(LR, j))
@@ -275,7 +280,7 @@
     return wet_ref[rows(j // (n // 2)), :] > 0.5
 
 
-def forward_kernel(wet_ref, w_ref, z_ref, lr_ref, c_ref, scr, across, adj, pg, rs_ref, tl_ref, tr_ref, shifted):
+def forward_kernel(wet_ref, w_ref, z_ref, lr_ref, c_ref, scr, across, adj, pg, rs_ref, tl_ref, tr_ref, sh, across0, zs):
     height, lanes = z_ref.shape
     n = height // BLK
 
@@ -287,8 +292,11 @@
     def get(f, j):
         return field(f)[rows(j), :]
 
-    first_pass(get, lambda j: tile_wet(wet_ref, j, n), n, scr, shifted, across, adj)
-    second_pass(get, lambda j: tile_wet(wet_ref, j, n), n, scr, shifted, across, adj, pg)
+    def wet(j):
+        return tile_wet(wet_ref, j, n)
+
+    first_pass(get, wet, n, scr, sh.at[0], across0, zs, second_parts(scr, sh.at[1], across))
+    second_pass(get, wet, n, sh.at[1], across, adj, pg)
     lane = lax.broadcasted_iota(jnp.int32, (height, 128), 1)
     for f in range(WET):
         ref = field(f)
@@ -305,7 +313,7 @@
     tr_ref[WET] = jnp.concatenate([top[:, half:], bottom[:, half:]], 1)
 
 
-def strip_gradient(s_ref, scr, shifted, across, adj, pg, g_ref):
+def strip_gradient(s_ref, scr, sh, ac, adj, pg, g_ref):
     n = s_ref.shape[1] // BLK
 
     def get(f, j):
@@ -317,9 +325,9 @@
     def put_grad(j, value):
         g_ref[rows(j), :] = value
 
-    first_pass(get, wet, n, scr, shifted, across, adj)
-    second_pass(get, wet, n, scr, shifted, across, adj, pg)
-    third_pass((1, 2), scr, across, adj, pg, put_grad)
+    first_pass(get, wet, n, scr, sh.at[0], ac.at[0], adj, second_parts(scr, sh.at[1], ac.at[1]))
+    second_pass(get, wet, n, sh.at[1], ac.at[1], adj, pg)
+    third_pass((1, 2), scr, ac.at[1], adj, pg, put_grad)
 
 
 def arctan_ratio(y, x):
@@ -517,7 +525,11 @@
     scr, across, adj, pg, row_own, col_left, col_right = call(
         forward_kernel,
         [*kept, (NF, 16, lanes), (NF, 8, height), (NF, 8, height)],
-        scratch=[pltpu.VMEM((N_SHIFTED, lanes // 128, height + 16, 128), jnp.float32)],
+        scratch=[
+            pltpu.VMEM((2, N_SHIFTED, lanes // 128, height + 16, 128), jnp.float32),
+            pltpu.VMEM((N_ACROSS, height, lanes), jnp.float32),
+            pltpu.VMEM((1, lanes // 128, height + 16, 128), jnp.float32),
+        ],
         flops=20_000_000,
     )(wet, water, ground, rough, cot)
     x_b, x_a, corner_left, corner_right = call(
@@ -532,8 +544,8 @@
             pltpu.VMEM((height, lanes), jnp.float32),
             pltpu.VMEM((NF, 32, lanes), jnp.float32),
             pltpu.VMEM((N_AHEAD, 32, lanes), jnp.float32),
-            pltpu.VMEM((N_SHIFTED, lanes // 128, 48, 128), jnp.float32),
-            pltpu.VMEM((N_ACROSS, 32, lanes), jnp.float32),
+            pltpu.VMEM((2, N_SHIFTED, lanes // 128, 48, 128), jnp.float32),
+            pltpu.VMEM((2, N_ACROSS, 32, lanes), jnp.float32),
             pltpu.VMEM((3, lanes // 128, 48, 128), jnp.float32),
             pltpu.VMEM((32, lanes), jnp.float32),
             pltpu.VMEM((32, lanes), jnp.float32),
@@ -548,8 +560,8 @@
             scratch=[
                 pltpu.VMEM((NF, 32, height + 128), jnp.float32),
                 pltpu.VMEM((N_AHEAD, 32, height + 128), jnp.float32),
-                pltpu.VMEM((N_SHIFTED, height // 128 + 1, 48, 128), jnp.float32),
-                pltpu.VMEM((N_ACROSS, 32, height + 128), jnp.float32),
+                pltpu.VMEM((2, N_SHIFTED, height // 128 + 1, 48, 128), jnp.float32),
+                pltpu.VMEM((2, N_ACROSS, 32, height + 128), jnp.float32),
                 pltpu.VMEM((3, height // 128 + 1, 48, 128), jnp.float32),
                 pltpu.VMEM((32, height + 128), jnp.float32),
                 pltpu.VMEM((32, height + 128), jnp.float32),

time: 17.5 us -> 17.5 us (level)
  no operation moved by 1% of the time
where the time goes in v7:
time: 17.5 us; the launch traced here: 17.4 us
  starting transfers between devices  7.76 us (44%)
  Pallas kernels  7.17 us (41%)
  waiting for transfers between devices  1.72 us (10%)
  between operations  0.74 us (4%)
    ppermute x4, starting transfers between devices, swapped(): return lax.ppermute(value, ('gx', 'gy'), pairs)  7.76 us
    pallas_call x1, Pallas kernels, on_device(): call(forward_kernel, [*kept, (NF, 16, lanes), (NF, 8, height), (NF, 8, he...  2.82 us
    ppermute x4, waiting for transfers between devices, swapped(): return lax.ppermute(value, ('gx', 'gy'), pairs)  1.72 us
    pallas_call x1, Pallas kernels, on_device(): call(backward_kernel, [(height, lanes)] * 3 + [(2, 8, height)] * 2, scrat...  1.72 us
    pallas_call x1, Pallas kernels, on_device(): call(rim_kernel, [(height, lanes)] * 3, scratch=[pltpu.VMEM((NF, 32, heig...  1.45 us
    pallas_call x1, Pallas kernels, on_device(): call(pack_rows_kernel, [(24, lanes), (24, lanes), (16, lanes)], scratch=[...  1.08 us
  transfers between devices with their start and end apart: 4, of which 2 were waited for; matrix products, arithmetic and copies ran while one was open for 0% of the time, Pallas kernels for 26%

profile of v7, /device:TPU:57, one launch (start us, length us, event | category | flops | bytes accessed | tf_op | source)
XLA Modules:
  0.0 17.4 jit_solution(16971572367982494887)
XLA Ops:
  0.6 0.0 copy-start.2
  0.6 0.0 copy-start.1
  0.7 0.0 copy-start.3
  0.7 0.0 copy-start
  0.7 1.1 %shard_map.94 = (f32[24,256]{1,0:T(8,128)S(1)}, f32[24,256]{1,0:T(8,128)S(1)}, f32[16,256]{1,0:T(8,128)S(1)}) custom-call(s32[2,2]{1,0:T(2,128)} %wet_hbm.1, f32[3,256,256]{2,1,0:T(8,128)} %w_ref.1, f32[256,256]{1,0:T(8,128)} %z_ref.1, f32[256,256]{1,0:T(8,128)} %lr_ref.3, f32[3,256,256]{2,1,0:T(8,128)} %c_ref.1), custom_call_target="tpu_custom_call" | custom-call | tf_op jit(solution)/shard_map/pallas_call | solution.py:506
  1.8 0.0 copy-start.4
  1.8 0.0 copy-start.5
  1.8 1.3 %collective-permute-start.1 = (f32[24,256]{1,0:T(8,128)S(1)}, f32[24,256]{1,0:T(8,128)S(1)}, u32[]{:S(2)}, u32[]{:S(2)}) collective-permute-start(f32[24,256]{1,0:T(8,128)S(1)} %get-tuple-element.23), channel_id=1, source_target_pairs={{0,1},{1,0},{2,3},{3,2},{4,5},{5,4},{6,7},{7,6},{8,9},{9,8},{10,11... | collective-permute-start | bytes 73736 | tf_op jit(solution)/shard_map/ppermute | solution.py:486
  3.1 2.5 %collective-permute-start = (f32[24,256]{1,0:T(8,128)S(1)}, f32[24,256]{1,0:T(8,128)S(1)}, u32[]{:S(2)}, u32[]{:S(2)}) collective-permute-start(f32[24,256]{1,0:T(8,128)S(1)} %get-tuple-element.22.yw_ref), channel_id=1, source_target_pairs={{0,8},{1,2},{2,1},{3,4},{4,3},{5,6},{6,5},{7,15},{8,0},{9,10},{10,... | collective-permute-start | bytes 73736 | tf_op jit(solution)/shard_map/ppermute | solution.py:486
  5.6 0.0 copy-done.2
  5.6 0.0 copy-done.1
  5.6 0.0 copy-done.3
  5.6 0.0 copy-done
  5.6 2.8 %shard_map.95 = (f32[4,256,256]{2,1,0:T(8,128)S(1)}, f32[5,256,256]{2,1,0:T(8,128)S(1)}, f32[3,2,272,128]{3,2,1,0:T(8,128)S(1)}, f32[256,256]{1,0:T(8,128)S(1)},...) custom-call(f32[16,256]{1,0:T(8,128)S(1)} %get-tuple-element.24.wet_ref, ...), custom_call_target="tpu_custom_call" | custom-call | flops 20000000 | bytes 2500000 | tf_op jit(solution)/shard_map/pallas_call | solution.py:525
  8.4 0.0 collective-permute-done.1.ya_ref
  8.4 1.0 %collective-permute-done.yb_ref = f32[24,256]{1,0:T(8,128)S(1)} collective-permute-done((f32[24,256]{1,0:T(8,128)S(1)}, f32[24,256]{1,0:T(8,128)S(1)}, u32[]{:S(2)}, u32[]{:S(2)}) %collective-permute-start) | collective-permute-done | bytes 24608 | tf_op jit(solution)/shard_map/ppermute | solution.py:486
  9.4 0.1 shard_map.96
  9.5 2.2 %collective-permute-start.2 = (f32[24,256]{1,0:T(8,128)S(1)}, f32[24,256]{1,0:T(8,128)S(1)}, u32[]{:S(2)}, u32[]{:S(2)}) collective-permute-start(f32[24,256]{1,0:T(8,128)S(1)} %get-tuple-element.27), channel_id=1, source_target_pairs={{0,8},{1,9},{2,10},{3,11},{4,12},{5,13},{6,14},{7,15},{8,0},{9,1},... | collective-permute-start | bytes 73736 | tf_op jit(solution)/shard_map/ppermute | solution.py:486
  11.7 1.8 %collective-permute-start.3 = (f32[24,256]{1,0:T(8,128)S(1)}, f32[24,256]{1,0:T(8,128)S(1)}, u32[]{:S(2)}, u32[]{:S(2)}) collective-permute-start(f32[24,256]{1,0:T(8,128)S(1)} %get-tuple-element.28.xw_ref), channel_id=1, source_target_pairs={{0,1},{1,0},{2,3},{3,2},{4,5},{5,4},{6,7},{7,6},{8,16},{9,17},{10,... | collective-permute-start | bytes 73736 | tf_op jit(solution)/shard_map/ppermute | solution.py:486
  13.5 0.0 copy-done.4
  13.5 0.0 copy-done.5
  13.5 1.7 %shard_map.97 = (f32[256,256]{1,0:T(8,128)S(1)}, f32[256,256]{1,0:T(8,128)S(1)}, f32[256,256]{1,0:T(8,128)S(1)}, f32[2,8,256]{2,1,0:T(8,128)S(1)}, f32[2,8,256]{2,1,0:T(8,128)S(1)}) custom-call(f32[8,128]{1,0:T(8,128)S(1)} %get-tuple-element.29.after_ref.pl_ref, f32[24,256]{1,0:T(8,128)S(1)} %collective-permute-done.1.ya_ref, ...), custom_call_target="tpu_custom_call" | custom-call | flops 20000000 | bytes 2500000 | tf_op jit(solution)/shard_map/pallas_call | solution.py:540
  15.2 0.0 collective-permute-done.2.xa_ref
  15.2 0.8 %collective-permute-done.3.xb_ref = f32[24,256]{1,0:T(8,128)S(1)} collective-permute-done((f32[24,256]{1,0:T(8,128)S(1)}, f32[24,256]{1,0:T(8,128)S(1)}, u32[]{:S(2)}, u32[]{:S(2)}) %collective-permute-start.3) | collective-permute-done | bytes 24608 | tf_op jit(solution)/shard_map/ppermute | solution.py:486
  16.0 1.5 %shard_map.98 = (f32[256,256]{1,0:T(8,128)}, f32[256,256]{1,0:T(8,128)}, f32[256,256]{1,0:T(8,128)}) custom-call(f32[24,256]{1,0:T(8,128)S(1)} %collective-permute-done.2.xa_ref, f32[24,256]{1,0:T(8,128)S(1)} %collective-permute-done.3.xb_ref, f32[24,256]{1,0:T(8,128)S(1)} %get-tuple-element.28.xw_ref, f32[9,8,256]{2,1,0:T(8,128)S(1)} %get-tuple-element.25.tl_ref, ...), custom_call_target="tpu_custom_call" | custom-call | tf_op jit(solution)/shard_map/pallas_call | solution.py:557
Async XLA Ops:
  0.6 4.9 %copy-start.2 = (f32[256,256]{1,0:T(8,128)S(1)}, f32[256,256]{1,0:T(8,128)}, u32[]{:S(2)}) copy-start(f32[256,256]{1,0:T(8,128)} %lr_ref.3) | copy-start | bytes 786436
  0.6 4.9 %copy-start.1 = (f32[3,256,256]{2,1,0:T(8,128)S(1)}, f32[3,256,256]{2,1,0:T(8,128)}, u32[]{:S(2)}) copy-start(f32[3,256,256]{2,1,0:T(8,128)} %c_ref.1) | copy-start | bytes 2359300
  0.7 4.9 %copy-start.3 = (f32[256,256]{1,0:T(8,128)S(1)}, f32[256,256]{1,0:T(8,128)}, u32[]{:S(2)}) copy-start(f32[256,256]{1,0:T(8,128)} %z_ref.1) | copy-start | bytes 786436
  0.7 4.9 %copy-start = (f32[3,256,256]{2,1,0:T(8,128)S(1)}, f32[3,256,256]{2,1,0:T(8,128)}, u32[]{:S(2)}) copy-start(f32[3,256,256]{2,1,0:T(8,128)} %w_ref.1) | copy-start | bytes 2359300
  1.8 11.7 %copy-start.4 = (f32[256,256]{1,0:T(8,128)S(1)}, f32[256,256]{1,0:T(8,128)}, u32[]{:S(2)}) copy-start(f32[256,256]{1,0:T(8,128)} %m_ref.1) | copy-start | bytes 786436
  1.8 11.7 %copy-start.5 = (f32[256,256]{1,0:T(8,128)S(1)}, f32[256,256]{1,0:T(8,128)}, u32[]{:S(2)}) copy-start(f32[256,256]{1,0:T(8,128)} %v_ref.1) | copy-start | bytes 786436
  1.8 6.6 %collective-permute-start.1 = (f32[24,256]{1,0:T(8,128)S(1)}, f32[24,256]{1,0:T(8,128)S(1)}, u32[]{:S(2)}, u32[]{:S(2)}) collective-permute-start(f32[24,256]{1,0:T(8,128)S(1)} %get-tuple-element.23), channel_id=1, source_target_pairs={{0,1},{1,0},{2,3},{3,2},{4,5},{5,4},{6,7},{7,6},{8,9},{9,8},{10,11... | collective-permute-start | bytes 73736 | tf_op jit(solution)/shard_map/ppermute | solution.py:486
  3.1 6.3 %collective-permute-start = (f32[24,256]{1,0:T(8,128)S(1)}, f32[24,256]{1,0:T(8,128)S(1)}, u32[]{:S(2)}, u32[]{:S(2)}) collective-permute-start(f32[24,256]{1,0:T(8,128)S(1)} %get-tuple-element.22.yw_ref), channel_id=1, source_target_pairs={{0,8},{1,2},{2,1},{3,4},{4,3},{5,6},{6,5},{7,15},{8,0},{9,10},{10,... | collective-permute-start | bytes 73736 | tf_op jit(solution)/shard_map/ppermute | solution.py:486
  9.5 5.7 %collective-permute-start.2 = (f32[24,256]{1,0:T(8,128)S(1)}, f32[24,256]{1,0:T(8,128)S(1)}, u32[]{:S(2)}, u32[]{:S(2)}) collective-permute-start(f32[24,256]{1,0:T(8,128)S(1)} %get-tuple-element.27), channel_id=1, source_target_pairs={{0,8},{1,9},{2,10},{3,11},{4,12},{5,13},{6,14},{7,15},{8,0},{9,1},... | collective-permute-start | bytes 73736 | tf_op jit(solution)/shard_map/ppermute | solution.py:486
  11.7 4.3 %collective-permute-start.3 = (f32[24,256]{1,0:T(8,128)S(1)}, f32[24,256]{1,0:T(8,128)S(1)}, u32[]{:S(2)}, u32[]{:S(2)}) collective-permute-start(f32[24,256]{1,0:T(8,128)S(1)} %get-tuple-element.28.xw_ref), channel_id=1, source_target_pairs={{0,1},{1,0},{2,3},{3,2},{4,5},{5,4},{6,7},{7,6},{8,16},{9,17},{10,... | collective-permute-start | bytes 73736 | tf_op jit(solution)/shard_map/ppermute | solution.py:486
